TPU v7x, 32 devices: a whole 2x2x4 slice. The times are simulated.
32 devices in a mesh: batch: 4 (over y, x), seq: 4 (over z), frames: 2 (over core).
Axes of the slice: x: 2, y: 2, z: 4, core: 2. Of those that a mesh axis runs over, the one named last changes fastest.
Arguments:
- frames_in: bfloat16 [4, 4, 2, 192, 1024], P('batch', 'seq', 'frames'), may hold values from -6 to 6
- skip_in: bfloat16 [4, 4, 2, 192, 1024], P('batch', 'seq', 'frames'), may hold values from -6 to 6
- lengths: int32 [4, 2, 3], P('batch', 'frames'), may hold values from 1 to 512, 736 in all within a row
- cotangent: bfloat16 [4, 4, 2, 192, 1024], P('batch', 'seq', 'frames'), may hold values from -6 to 6
- w_skip: bfloat16 [2048, 1024], P('frames'), may hold values from -0.125 to 0.125
- w_qkv: bfloat16 [1024, 3072], P('frames'), may hold values from -0.1875 to 0.1875
- w_out: bfloat16 [1024, 1024], P('frames'), may hold values from -0.5 to 0.5
- w_up: bfloat16 [1024, 4096], P('frames'), may hold values from -0.1875 to 0.1875
- w_down: bfloat16 [4096, 1024], P('frames'), may hold values from -0.09375 to 0.09375
- skip_bias: bfloat16 [1024], P('frames'), may hold values from -3 to 3
- norm1_gain: bfloat16 [1024], P('frames'), may hold values from 0.25 to 1.75
- norm1_bias: bfloat16 [1024], P('frames'), may hold values from -3 to 3
- out_bias: bfloat16 [1024], P('frames'), may hold values from -3 to 3
- norm2_gain: bfloat16 [1024], P('frames'), may hold values from 0.25 to 1.75
- norm2_bias: bfloat16 [1024], P('frames'), may hold values from -3 to 3
- up_bias: bfloat16 [4096], P('frames'), may hold values from -3 to 3
- down_bias: bfloat16 [1024], P('frames'), may hold values from -3 to 3
Outputs:
- output: bfloat16 [4, 4, 2, 192, 1024], P('batch', 'seq', 'frames')
- input_grad: float32 [4, 4, 2, 192, 1024], P('batch', 'seq', 'frames')
- skip_grad: float32 [4, 4, 2, 192, 1024], P('batch', 'seq', 'frames')
- grad_w_skip: float32 [2048, 1024], P('frames')
- grad_w_qkv: float32 [1024, 3072], P('frames')
- grad_w_out: float32 [1024, 1024], P('frames')
- grad_w_up: float32 [1024, 4096], P('frames')
- grad_w_down: float32 [4096, 1024], P('frames')
- grad_skip_bias: float32 [1024], P('frames')
- grad_norm1_gain: float32 [1024], P('frames')
- grad_norm1_bias: float32 [1024], P('frames')
- grad_out_bias: float32 [1024], P('frames')
- grad_norm2_gain: float32 [1024], P('frames')
- grad_norm2_bias: float32 [1024], P('frames')
- grad_up_bias: float32 [4096], P('frames')
- grad_down_bias: float32 [1024], P('frames')
Inputs may be any that keep to these rules, and one draw needn't show every extreme that they name: `lengths`: in every group the utterances lie end to end from its first frame and fill all but its last 32 frames, which are padding; in every group the longest utterance has exactly 512 frames.
All inputs are finite; a program needn't handle non-finite values.
Results may differ from a plain program's by a relative error of at most 0.012.
Values may be sent and summed in bfloat16 or wider, within the bound.
No kernel may reach another device: no remote copies, remote signals or barrier semaphores. Data moves between devices by JAX's collectives and lax.ppermute only.
A program may use at most 320 MiB of HBM per device.

v0:
```python
import jax
import jax.numpy as jnp
from jax import lax
from jax.sharding import PartitionSpec as P

HEADS = 16
HD = 64
UTTS = 3


def layer_norm(values, gain, bias):
    row_mean = jnp.mean(values, axis=-1, keepdims=True)
    centred = values - row_mean
    variance = jnp.mean(centred * centred, axis=-1, keepdims=True)
    return centred * lax.rsqrt(variance + 1e-05) * gain + bias


def gelu_exact(values):
    return jax.nn.gelu(values, approximate=False)


def contract_rows(left_side, right_side):
    return lax.dot_general(
        left_side, right_side, (((0,), (0,)), ((), ())), preferred_element_type=jnp.float32
    )


def times_transposed(left_side, right_side):
    return lax.dot_general(
        left_side, right_side, (((1,), (1,)), ((), ())), preferred_element_type=jnp.float32
    )


def block_count(length):
    count = max(1, length // 512)
    while length % count:
        count = count - 1
    return count


def masked_scores(queries, q_pos, q_seg, key_rows, segment, slopes, scale):
    length = key_rows.shape[0]
    k_pos = jnp.arange(length, dtype=jnp.int32)
    raw_dots = (
        jnp.einsum("qhd,khd->hqk", queries, key_rows, preferred_element_type=jnp.float32) * scale
    )
    distance = jnp.abs(q_pos[:, None] - k_pos[None, :]).astype(jnp.float32)
    allowed = (q_seg[:, None] == segment[None, :]) & (segment[None, :] < UTTS)
    scores = jnp.where(
        allowed[None], raw_dots - slopes[:, None, None] * distance[None], -1000000000.0
    )
    return (scores, allowed)


def body(
    frames_in,
    skip_in,
    lengths,
    cotangent,
    w_skip,
    w_qkv,
    w_out,
    w_up,
    w_down,
    skip_bias,
    norm1_gain,
    norm1_bias,
    out_bias,
    norm2_gain,
    norm2_bias,
    up_bias,
    down_bias,
):
    tok_rows = frames_in.shape[3]
    model_width = frames_in.shape[4]
    frames = frames_in.reshape(tok_rows, model_width)
    skips = skip_in.reshape(tok_rows, model_width)
    cotan = cotangent.reshape(tok_rows, model_width)
    utt_lengths = lengths.reshape(-1)
    n_seq = lax.axis_size("seq")
    local_heads = HEADS // n_seq
    length = tok_rows * n_seq
    scale = HD ** (-0.5)
    gathered = (
        lax.all_gather(w_skip, "frames", axis=0, tiled=True),
        lax.all_gather(w_qkv, "frames", axis=0, tiled=True),
        lax.all_gather(w_out, "frames", axis=0, tiled=True),
        lax.all_gather(w_up, "frames", axis=0, tiled=True),
        lax.all_gather(w_down, "frames", axis=0, tiled=True),
        lax.all_gather(skip_bias, "frames", axis=0, tiled=True),
        lax.all_gather(norm1_gain, "frames", axis=0, tiled=True),
        lax.all_gather(norm1_bias, "frames", axis=0, tiled=True),
        lax.all_gather(out_bias, "frames", axis=0, tiled=True),
        lax.all_gather(norm2_gain, "frames", axis=0, tiled=True),
        lax.all_gather(norm2_bias, "frames", axis=0, tiled=True),
        lax.all_gather(up_bias, "frames", axis=0, tiled=True),
        lax.all_gather(down_bias, "frames", axis=0, tiled=True),
    )
    (
        full_skip,
        full_qkv,
        full_out,
        full_up,
        full_down,
        full_sbias,
        full_g1,
        full_b1,
        full_obias,
        full_g2,
        full_b2,
        full_ubias,
        full_dbias,
    ) = gathered
    joined = jnp.concatenate([frames, skips], axis=1)
    hidden_z = jnp.dot(joined, full_skip, preferred_element_type=jnp.float32) + full_sbias.astype(
        jnp.float32
    )
    normed, norm1_pull = jax.vjp(
        layer_norm, hidden_z, full_g1.astype(jnp.float32), full_b1.astype(jnp.float32)
    )
    normed_low = normed.astype(jnp.bfloat16)
    projected = jnp.dot(normed_low, full_qkv, preferred_element_type=jnp.float32).astype(
        jnp.bfloat16
    )
    projected = projected.reshape(tok_rows, 3, n_seq, local_heads * HD)
    grouped = lax.all_to_all(projected, "seq", split_axis=2, concat_axis=0, tiled=True)
    grouped = grouped.reshape(length, 3, local_heads, HD)
    queries = grouped[:, 0]
    key_rows = grouped[:, 1]
    value_rows = grouped[:, 2]
    bounds = jnp.cumsum(utt_lengths, dtype=jnp.int32)
    positions = jnp.arange(length, dtype=jnp.int32)
    segment = jnp.sum(
        (positions[:, None] >= bounds[None, :]).astype(jnp.int32), axis=1, dtype=jnp.int32
    )
    live_rows = segment < UTTS
    first_head = lax.axis_index("seq") * local_heads
    slopes = 2.0 ** (
        -8.0
        * (first_head + jnp.arange(local_heads, dtype=jnp.int32) + 1).astype(jnp.float32)
        / HEADS
    )
    count = block_count(length)
    rows_block = length // count
    query_blocks = queries.reshape(count, rows_block, local_heads, HD)
    pos_blocks = positions.reshape(count, rows_block)
    seg_blocks = segment.reshape(count, rows_block)

    def forward_block(mapped):
        block_queries, q_pos, q_seg = mapped
        scores, allowed = masked_scores(
            block_queries, q_pos, q_seg, key_rows, segment, slopes, scale
        )
        row_max = jnp.max(scores, axis=-1, keepdims=True)
        exp_scores = jnp.exp(scores - row_max)
        row_total = jnp.sum(exp_scores, axis=-1, keepdims=True)
        attn_prob = (exp_scores / row_total).astype(jnp.bfloat16)
        mixed = jnp.einsum(
            "hqk,khd->qhd", attn_prob, value_rows, preferred_element_type=jnp.float32
        )
        mixed = mixed * (q_seg < UTTS).astype(jnp.float32)[:, None, None]
        return (mixed, (row_max + jnp.log(row_total))[..., 0])

    mixed_blocks, log_totals = lax.map(forward_block, (query_blocks, pos_blocks, seg_blocks))
    mixed_low = mixed_blocks.reshape(length, 1, local_heads * HD).astype(jnp.bfloat16)
    attended = lax.all_to_all(mixed_low, "seq", split_axis=0, concat_axis=1, tiled=True).reshape(
        tok_rows, model_width
    )
    branch = jnp.dot(attended, full_out, preferred_element_type=jnp.float32) + full_obias.astype(
        jnp.float32
    )
    resid = hidden_z + branch
    normed_two, norm2_pull = jax.vjp(
        layer_norm, resid, full_g2.astype(jnp.float32), full_b2.astype(jnp.float32)
    )
    normed_two_low = normed_two.astype(jnp.bfloat16)
    pre_act = jnp.dot(
        normed_two_low, full_up, preferred_element_type=jnp.float32
    ) + full_ubias.astype(jnp.float32)
    activ, gelu_pull = jax.vjp(gelu_exact, pre_act)
    activ_low = activ.astype(jnp.bfloat16)
    result = (
        resid
        + jnp.dot(activ_low, full_down, preferred_element_type=jnp.float32)
        + full_dbias.astype(jnp.float32)
    )
    output = result.astype(jnp.bfloat16).reshape(1, 1, 1, tok_rows, model_width)
    back_weights = (
        lax.all_gather(w_skip, "frames", axis=0, tiled=True),
        lax.all_gather(w_qkv, "frames", axis=0, tiled=True),
        lax.all_gather(w_out, "frames", axis=0, tiled=True),
        lax.all_gather(w_up, "frames", axis=0, tiled=True),
        lax.all_gather(w_down, "frames", axis=0, tiled=True),
        lax.all_gather(skip_bias, "frames", axis=0, tiled=True),
        lax.all_gather(norm1_gain, "frames", axis=0, tiled=True),
        lax.all_gather(norm1_bias, "frames", axis=0, tiled=True),
        lax.all_gather(out_bias, "frames", axis=0, tiled=True),
        lax.all_gather(norm2_gain, "frames", axis=0, tiled=True),
        lax.all_gather(norm2_bias, "frames", axis=0, tiled=True),
        lax.all_gather(up_bias, "frames", axis=0, tiled=True),
        lax.all_gather(down_bias, "frames", axis=0, tiled=True),
    )
    back_skip = back_weights[0]
    back_qkv = back_weights[1]
    back_out = back_weights[2]
    back_up = back_weights[3]
    back_down = back_weights[4]
    grad_down_bias = jnp.sum(cotan, axis=0, dtype=jnp.float32)
    grad_w_down = contract_rows(activ_low, cotan)
    grad_activ = times_transposed(cotan, back_down)
    (grad_pre,) = gelu_pull(grad_activ)
    grad_pre_low = grad_pre.astype(jnp.bfloat16)
    grad_up_bias = jnp.sum(grad_pre_low, axis=0, dtype=jnp.float32)
    grad_w_up = contract_rows(normed_two_low, grad_pre_low)
    grad_normed_two = times_transposed(grad_pre_low, back_up)
    grad_resid_ln, grad_norm2_gain, grad_norm2_bias = norm2_pull(grad_normed_two)
    grad_resid = cotan.astype(jnp.float32) + grad_resid_ln
    grad_branch = grad_resid.astype(jnp.bfloat16)
    grad_out_bias = jnp.sum(grad_branch, axis=0, dtype=jnp.float32)
    grad_w_out = contract_rows(attended, grad_branch)
    grad_attended = times_transposed(grad_branch, back_out).astype(jnp.bfloat16)
    grad_attended = grad_attended.reshape(tok_rows, n_seq, local_heads * HD)
    grad_heads = lax.all_to_all(grad_attended, "seq", split_axis=1, concat_axis=0, tiled=True)
    grad_heads = (
        grad_heads.reshape(length, local_heads, HD) * live_rows.astype(jnp.bfloat16)[:, None, None]
    )
    grad_blocks = grad_heads.reshape(count, rows_block, local_heads, HD)

    def backward_block(grads_kv, mapped):
        block_queries, q_pos, q_seg, out_grad, log_total = mapped
        scores, allowed = masked_scores(
            block_queries, q_pos, q_seg, key_rows, segment, slopes, scale
        )
        attn_prob = jnp.exp(scores - log_total[:, :, None])
        prob_low = attn_prob.astype(jnp.bfloat16)
        value_grad = grads_kv[1] + jnp.einsum(
            "hqk,qhd->khd", prob_low, out_grad, preferred_element_type=jnp.float32
        )
        prob_grad = jnp.einsum(
            "qhd,khd->hqk", out_grad, value_rows, preferred_element_type=jnp.float32
        )
        score_grad = attn_prob * (
            prob_grad - jnp.sum(attn_prob * prob_grad, axis=-1, keepdims=True)
        )
        score_low = jnp.where(allowed[None], score_grad, 0.0).astype(jnp.bfloat16)
        query_grad = (
            jnp.einsum("hqk,khd->qhd", score_low, key_rows, preferred_element_type=jnp.float32)
            * scale
        )
        key_grad = (
            grads_kv[0]
            + jnp.einsum(
                "hqk,qhd->khd", score_low, block_queries, preferred_element_type=jnp.float32
            )
            * scale
        )
        return ((key_grad, value_grad), query_grad)

    zero_kv = jnp.zeros((length, local_heads, HD), jnp.float32)
    (key_grads, value_grads), query_grads = lax.scan(
        backward_block,
        (zero_kv, zero_kv),
        (query_blocks, pos_blocks, seg_blocks, grad_blocks, log_totals),
    )
    grad_grouped = jnp.stack(
        [query_grads.reshape(length, local_heads, HD), key_grads, value_grads], axis=1
    )
    grad_grouped = grad_grouped.astype(jnp.bfloat16).reshape(length, 3, 1, local_heads * HD)
    grad_projected = lax.all_to_all(grad_grouped, "seq", split_axis=0, concat_axis=2, tiled=True)
    grad_projected = grad_projected.reshape(tok_rows, 3 * model_width)
    grad_w_qkv = contract_rows(normed_low, grad_projected)
    grad_normed = times_transposed(grad_projected, back_qkv)
    grad_z_ln, grad_norm1_gain, grad_norm1_bias = norm1_pull(grad_normed)
    grad_z_low = (grad_resid + grad_z_ln).astype(jnp.bfloat16)
    grad_skip_bias = jnp.sum(grad_z_low, axis=0, dtype=jnp.float32)
    grad_w_skip = contract_rows(joined, grad_z_low)
    grad_joined = times_transposed(grad_z_low, back_skip)
    input_grad = grad_joined[:, :model_width].reshape(1, 1, 1, tok_rows, model_width)
    skip_grad = grad_joined[:, model_width:].reshape(1, 1, 1, tok_rows, model_width)
    matrices = (grad_w_skip, grad_w_qkv, grad_w_out, grad_w_up, grad_w_down)
    vectors = (
        grad_skip_bias,
        grad_norm1_gain,
        grad_norm1_bias,
        grad_out_bias,
        grad_norm2_gain,
        grad_norm2_bias,
        grad_up_bias,
        grad_down_bias,
    )
    shards = (
        lax.psum_scatter(matrices[0], "frames", scatter_dimension=0, tiled=True),
        lax.psum_scatter(matrices[1], "frames", scatter_dimension=0, tiled=True),
        lax.psum_scatter(matrices[2], "frames", scatter_dimension=0, tiled=True),
        lax.psum_scatter(matrices[3], "frames", scatter_dimension=0, tiled=True),
        lax.psum_scatter(matrices[4], "frames", scatter_dimension=0, tiled=True),
        lax.psum_scatter(vectors[0], "frames", scatter_dimension=0, tiled=True),
        lax.psum_scatter(vectors[1], "frames", scatter_dimension=0, tiled=True),
        lax.psum_scatter(vectors[2], "frames", scatter_dimension=0, tiled=True),
        lax.psum_scatter(vectors[3], "frames", scatter_dimension=0, tiled=True),
        lax.psum_scatter(vectors[4], "frames", scatter_dimension=0, tiled=True),
        lax.psum_scatter(vectors[5], "frames", scatter_dimension=0, tiled=True),
        lax.psum_scatter(vectors[6], "frames", scatter_dimension=0, tiled=True),
        lax.psum_scatter(vectors[7], "frames", scatter_dimension=0, tiled=True),
    )
    summed = lax.psum(
        (
            shards[0],
            shards[1],
            shards[2],
            shards[3],
            shards[4],
            shards[5],
            shards[6],
            shards[7],
            shards[8],
            shards[9],
            shards[10],
            shards[11],
            shards[12],
        ),
        ("batch", "seq"),
    )
    return (
        output,
        input_grad,
        skip_grad,
        summed[0],
        summed[1],
        summed[2],
        summed[3],
        summed[4],
        summed[5],
        summed[6],
        summed[7],
        summed[8],
        summed[9],
        summed[10],
        summed[11],
        summed[12],
    )


def solution(mesh):
    in_specs = (
        P("batch", "seq", "frames", None, None),
        P("batch", "seq", "frames", None, None),
        P("batch", "frames", None),
        P("batch", "seq", "frames", None, None),
        P("frames", None),
        P("frames", None),
        P("frames", None),
        P("frames", None),
        P("frames", None),
        P("frames"),
        P("frames"),
        P("frames"),
        P("frames"),
        P("frames"),
        P("frames"),
        P("frames"),
        P("frames"),
    )
    out_specs = (
        P("batch", "seq", "frames", None, None),
        P("batch", "seq", "frames", None, None),
        P("batch", "seq", "frames", None, None),
        P("frames", None),
        P("frames", None),
        P("frames", None),
        P("frames", None),
        P("frames", None),
        P("frames"),
        P("frames"),
        P("frames"),
        P("frames"),
        P("frames"),
        P("frames"),
        P("frames"),
        P("frames"),
    )
    return jax.shard_map(body, mesh=mesh, in_specs=in_specs, out_specs=out_specs, check_vma=False)
```

profile of v0, /device:TPU:0, one launch (start us, length us, event | category | flops | bytes accessed | tf_op | source)
XLA Modules:
  0.0 1173.8 jit_solution(2750756458247903826)
XLA Ops:
  16.4 9.6 all-gather.13.cloned.1.call-done
  29.5 15.9 %all-gather.15.cloned.1.call-done = bf16[1024,3072]{1,0:T(8,128)(2,1)} async-done(((bf16[512,3072]{1,0:T(8,128)(2,1)}), bf16[1024,3072]{1,0:T(8,128)(2,1)}) %all-gather.15.cloned.1.call-update) | async-done | bytes 6291472 | tf_op jit(solution)/shard_map/all_gather | solution.py:86
  45.5 5.3 convolution_convert_fusion
  54.6 4.9 all-to-all-start
  62.5 26.0 %all-to-all-done = bf16[192,3,4,256]{3,0,1,2:T(8,128)(2,1)S(1)} async-done(((bf16[192,3,4,256]{3,0,1,2:T(8,128)(2,1)}), bf16[192,3,4,256]{3,0,1,2:T(8,128)(2,1)S(1)}, u32[]{:S(2)}, u32[]{:S(2)}) %all-to-all-start) | async-done | bytes 1179680 | tf_op jit(solution)/shard_map/all_to_all | solution.py:126
  94.5 5.2 fusion.78
  108.6 3.9 all-to-all-start.1
  126.8 12.9 %multiply_convert_fusion = (bf16[192,4096]{1,0:T(8,128)(2,1)}, f32[192,4096]{1,0:T(8,128)}, f32[192,4096]{1,0:T(8,128)}) fusion(f32[4096]{0:T(1024)S(1)} %convert_element_type.153, bf16[1024,4096]{1,0:T(8,128)(2,1)} %all-gather.19.cloned.1.call-done, f32[192,1024]{1,0:T(8,128)S(1)} %get-tuple-element.132, f32[1024]{0:T(1024)S(1)} %bitcast.132, ...), kind=kOutput, calls=%fused_computation.27 | convolution fusion | flops 1663500288 | bytes 17065472 | tf_op jit(solution)/shard_map/dot_general | solution.py:177
  139.7 9.8 convert_reduce_fusion
  149.5 3.6 multiply_reduce_fusion.1
  163.9 11.1 all-to-all-done.2
  175.7 6.0 fusion.39
  184.1 6.1 fusion.59
  190.2 16.2 %fusion.46 = bf16[4,64,768]{2,1,0:T(8,128)(2,1)S(1)} fusion(f32[4,768,768]{1,2,0:T(8,128)} %fusion.59, f32[4,768,768]{1,2,0:T(8,128)} %copy-done, f32[4,768]{1,0:T(4,128)} %copy-done.15, pred[768,768]{0,1:T(8,128)(4,1)} %copy-done.10, bf16[768,3,4,64]{0,3,2,1:T(8,128)(2,1)} %reshape.334), kind=kOutput, calls=%fused_computation.56 | convolution fusion | flops 318902016 | bytes 39149568 | tf_op jit(solution)/shard_map/while/body/eval_jaxpr/hqk,khd->qhd/dot_general | solution.py:247
  208.1 16.3 %fusion.43 = bf16[4,64,768]{2,1,0:T(8,128)(2,1)S(1)} fusion(f32[4,768,768]{1,2,0:T(8,128)} %fusion.59, f32[4,768,768]{1,2,0:T(8,128)} %copy-done, f32[4,768]{1,0:T(4,128)} %copy-done.15, pred[768,768]{0,1:T(8,128)(4,1)} %copy-done.10, bf16[768,3,4,64]{0,3,2,1:T(8,128)(2,1)} %reshape.334), kind=kOutput, calls=%fused_computation.55 | convolution fusion | flops 318902016 | bytes 39149568 | tf_op jit(solution)/shard_map/while/body/eval_jaxpr/hqk,qhd->khd/dot_general | solution.py:252
  226.2 3.9 pad_maximum_fusion
  230.1 39.2 %all_to_all.60 = bf16[768,3,1,256]{3,1,2,0:T(4,128)(2,1)S(1)} all-to-all(bf16[768,3,1,256]{3,1,2,0:T(4,128)(2,1)S(1)} %pad_maximum_fusion), channel_id=1, replica_groups=mesh['batch'=4,'seq'=4,'frames'=2] {'seq'}, dimensions={0} | all-to-all | bytes 2359296 | tf_op jit(solution)/shard_map/all_to_all | solution.py:269
  272.1 6.2 multiply_reduce_fusion.2
  279.5 4.7 fusion.51
  285.5 9.4 fusion.70
  296.7 8.2 fusion.71
  306.3 12.8 %fusion.53 = f32[4096,1024]{1,0:T(8,128)} fusion(bf16[192,4096]{1,0:T(8,128)(2,1)S(1)} %copy-done.7, bf16[1,1,1,192,1024]{4,3,2,1,0:T(8,128)(2,1)S(1)} %copy-done.5), kind=kOutput, calls=%fused_computation.83 | convolution fusion | flops 1610612736 | bytes 18743296 | tf_op jit(solution)/shard_map/dot_general | solution.py:23
  319.6 3.5 reduce-scatter.8.cloned.1.call-done
  323.0 30.9 %reduce-scatter.12.cloned.1.call-done = f32[512,4096]{1,0:T(8,128)} async-done(((f32[1024,4096]{1,0:T(8,128)}), f32[512,4096]{1,0:T(8,128)}) %reduce-scatter.12.cloned.1.call-update) | async-done | bytes 8388624 | tf_op jit(solution)/shard_map/reduce_scatter | solution.py:295
  354.0 28.6 %reduce-scatter.14.cloned.1.call-done = f32[2048,1024]{1,0:T(8,128)} async-done(((f32[4096,1024]{1,0:T(8,128)}), f32[2048,1024]{1,0:T(8,128)}) %reduce-scatter.14.cloned.1.call-update) | async-done | bytes 8388624 | tf_op jit(solution)/shard_map/reduce_scatter | solution.py:296
  387.0 5.9 fusion.50
  393.0 3.7 all-reduce.10
  397.2 82.5 %all-reduce.8 = (f32[512]{0:T(512)}, f32[512]{0:T(512)}, f32[512]{0:T(512)}, f32[512]{0:T(512)}, f32[512]{0:T(512)}, /*index=5*/f32[512]{0:T(512)}, f32[2048]{0:T(1024)}, f32[512]{0:T(512)}) all-reduce(f32[512]{0:T(512)S(1)} %dynamic-slice.3, ...), channel_id=1, replica_groups=mesh['batch'=4,'seq'=4,'frames'=2] {'batch','seq'}, use_global_device_ids=true, to_apply=%region_25.26 | all-reduce | flops 5632 | bytes 45056 | tf_op jit(solution)/shard_map/psum | solution.py:306
  479.7 3.7 fusion.80
  484.8 661.6 %all-reduce.13.cloned.1.call-done = (f32[1024,1024]{1,0:T(8,128)}, f32[512,3072]{1,0:T(8,128)}, f32[512,1024]{1,0:T(8,128)}, f32[512,4096]{1,0:T(8,128)}, f32[2048,1024]{1,0:T(8,128)}) async-done(((f32[1024,1024]{1,0:T(8,128)}, f32[512,3072]{1,0:T(8,128)}, f32[512,1024]{1,0:T(8,128)}, f32[512,4096]{1,0:T(8,128)}, f32[2048,1024]{1,0:T(8,128)}), (f32[1024,1024]{1,0:T(8,128)}, f32[512,3072]{1,0:T(8,128)}, ...) | async-done | bytes 29360144 | tf_op jit(solution)/shard_map/psum | solution.py:306
  1146.4 5.1 copy.96
  1157.9 4.3 copy.99
  (228 shorter events, 90.9 us)
Async XLA Ops:
  7.2 18.8 %all-gather.13.cloned.1.call-start = ((), (), s32[]{:S(2)}) async-start(), calls=%async_computation.9 | async-start | bytes 6291456 | tf_op jit(solution)/shard_map/all_gather | solution.py:85
  7.9 37.5 %all-gather.15.cloned.1.call-start = ((), (), s32[]{:S(2)}) async-start(), calls=%async_computation.10 | async-start | bytes 9437184 | tf_op jit(solution)/shard_map/all_gather | solution.py:86
  8.7 115.5 %all-gather.17.cloned.1.call-start = ((), (), s32[]{:S(2)}) async-start(), calls=%async_computation.11 | async-start | bytes 3145728 | tf_op jit(solution)/shard_map/all_gather | solution.py:87
  9.4 117.3 %all-gather.19.cloned.1.call-start = ((), (), s32[]{:S(2)}) async-start(), calls=%async_computation.12 | async-start | bytes 12582912 | tf_op jit(solution)/shard_map/all_gather | solution.py:88
  10.0 16.0 %copy-start.11 = (bf16[1,1,1,192,1024]{4,3,2,1,0:T(8,128)(2,1)S(1)}, bf16[1,1,1,192,1024]{4,3,2,1,0:T(8,128)(2,1)}, u32[]{:S(2)}) copy-start(bf16[1,1,1,192,1024]{4,3,2,1,0:T(8,128)(2,1)} %param.18) | copy-start | bytes 1179652
  10.0 15.9 %copy-start.13 = (bf16[1,1,1,192,1024]{4,3,2,1,0:T(8,128)(2,1)S(1)}, bf16[1,1,1,192,1024]{4,3,2,1,0:T(8,128)(2,1)}, u32[]{:S(2)}) copy-start(bf16[1,1,1,192,1024]{4,3,2,1,0:T(8,128)(2,1)} %param.17) | copy-start | bytes 1179652
  10.0 129.6 %all-gather.21.cloned.1.call-start = ((), (), s32[]{:S(2)}) async-start(), calls=%async_computation.13 | async-start | bytes 12582912 | tf_op jit(solution)/shard_map/all_gather | solution.py:89
  29.2 21.5 %copy-start.22 = (f32[192]{0:T(256)}, f32[192]{0:T(256)S(1)}, u32[]{:S(2)}) copy-start(f32[192]{0:T(256)S(1)} %broadcast_multiply_fusion.1) | copy-start | bytes 2308
  29.5 21.3 %copy-start.33 = (f32[192]{0:T(256)}, f32[192]{0:T(256)S(1)}, u32[]{:S(2)}) copy-start(f32[192]{0:T(256)S(1)} %multiply_reduce_fusion.6) | copy-start | bytes 2308
  29.5 21.2 %copy-start.27 = (f32[192]{0:T(256)}, f32[192]{0:T(256)S(1)}, u32[]{:S(2)}) copy-start(f32[192]{0:T(256)S(1)} %fusion.64) | copy-start | bytes 2308
  50.7 8.8 copy-start.50
  54.6 33.9 %all-to-all-start = ((bf16[192,3,4,256]{3,0,1,2:T(8,128)(2,1)}), bf16[192,3,4,256]{3,0,1,2:T(8,128)(2,1)S(1)}, u32[]{:S(2)}, u32[]{:S(2)}) async-start(bf16[192,3,4,256]{3,0,1,2:T(8,128)(2,1)} %copy.66), calls=%async_computation | async-start | bytes 2359296 | tf_op jit(solution)/shard_map/all_to_all | solution.py:126
  62.5 37.1 %copy-start.10 = (pred[768,768]{0,1:T(8,128)(4,1)}, pred[768,768]{0,1:T(8,128)(4,1)S(1)}, u32[]{:S(2)}) copy-start(pred[768,768]{0,1:T(8,128)(4,1)S(1)} %compare_and_fusion) | copy-start | bytes 1769476
  106.1 8.3 copy-start.46
  106.2 10.2 copy-start.47
  106.2 12.0 %copy-start.37 = (bf16[2048]{0:T(1024)(128)(2,1)S(1)}, bf16[2048]{0:T(1024)(128)(2,1)}, u32[]{:S(2)}) copy-start(bf16[2048]{0:T(1024)(128)(2,1)} %param.32) | copy-start | bytes 12292
  108.6 14.7 %all-to-all-start.1 = ((bf16[4,2,24576]{2,1,0:T(2,128)(2,1)}), bf16[4,2,24576]{2,1,0:T(2,128)(2,1)S(1)}, u32[]{:S(2)}, u32[]{:S(2)}) async-start(bf16[4,2,24576]{2,1,0:T(2,128)(2,1)} %reshape.374), calls=%async_computation.1 | async-start | bytes 786432 | tf_op jit(solution)/shard_map/all_to_all | solution.py:166
  112.6 207.0 %reduce-scatter.10.cloned.1.call-start = ((), (), s32[]{:S(2)}) async-start(), calls=%async_computation.16 | async-start | bytes 6291456 | tf_op jit(solution)/shard_map/reduce_scatter | solution.py:294
  126.5 26.6 %copy-start.20 = (f32[192]{0:T(256)}, f32[192]{0:T(256)S(1)}, u32[]{:S(2)}) copy-start(f32[192]{0:T(256)S(1)} %broadcast_multiply_fusion) | copy-start | bytes 2308
  126.7 26.4 %copy-start.24 = (f32[192]{0:T(256)}, f32[192]{0:T(256)S(1)}, u32[]{:S(2)}) copy-start(f32[192]{0:T(256)S(1)} %fusion.65) | copy-start | bytes 2308
  126.8 12.9 %copy-start.4 = (bf16[1,1,1,192,1024]{4,3,2,1,0:T(8,128)(2,1)S(1)}, bf16[1,1,1,192,1024]{4,3,2,1,0:T(8,128)(2,1)}, u32[]{:S(2)}) copy-start(bf16[1,1,1,192,1024]{4,3,2,1,0:T(8,128)(2,1)} %param.20) | copy-start | bytes 1179652
  139.7 9.8 copy-start.49
  157.0 6.8 copy-start.17
  157.1 18.7 %copy-start.26 = (bf16[768]{0:T(1024)(128)(2,1)S(1)}, bf16[768]{0:T(1024)(128)(2,1)}, u32[]{:S(2)}) copy-start(bf16[768]{0:T(1024)(128)(2,1)} %get-tuple-element.118) | copy-start | bytes 4612
  160.3 14.7 %all-to-all-start.2 = ((bf16[192,4,256]{2,0,1:T(8,128)(2,1)}), bf16[192,4,256]{2,0,1:T(8,128)(2,1)S(1)}, u32[]{:S(2)}, u32[]{:S(2)}) async-start(bf16[192,4,256]{2,0,1:T(8,128)(2,1)} %bitcast.107), calls=%async_computation.2 | async-start | bytes 786432 | tf_op jit(solution)/shard_map/all_to_all | solution.py:223
  163.8 155.8 %reduce-scatter.6.cloned.1.call-start = ((), (), s32[]{:S(2)}) async-start(), calls=%async_computation.14 | async-start | bytes 12582912 | tf_op jit(solution)/shard_map/reduce_scatter | solution.py:292
  163.9 17.9 %copy-start.15 = (f32[4,768]{1,0:T(4,128)}, f32[4,768]{1,0:T(4,128)S(1)}, u32[]{:S(2)}) copy-start(f32[4,768]{1,0:T(4,128)S(1)} %log_add_fusion) | copy-start | bytes 36868
  284.2 38.8 %reduce-scatter.8.cloned.1.call-start = ((), (), s32[]{:S(2)}) async-start(), calls=%async_computation.15 | async-start | bytes 18874368 | tf_op jit(solution)/shard_map/reduce_scatter | solution.py:293
  294.9 59.1 %reduce-scatter.12.cloned.1.call-start = ((), (), s32[]{:S(2)}) async-start(), calls=%async_computation.17 | async-start | bytes 25165824 | tf_op jit(solution)/shard_map/reduce_scatter | solution.py:295
  305.0 77.6 %reduce-scatter.14.cloned.1.call-start = ((), (), s32[]{:S(2)}) async-start(), calls=%async_computation.18 | async-start | bytes 25165824 | tf_op jit(solution)/shard_map/reduce_scatter | solution.py:296
  319.2 827.2 %all-reduce.13.cloned.1.call-start = ((), (), s32[]{:S(2)}) async-start(), calls=%async_computation.19 | async-start | bytes 58720256 | tf_op jit(solution)/shard_map/psum | solution.py:306
  1146.4 11.0 slice-start.2
  (38 other events, 158.4 us)
Sparse Core Ops, SparseCore 0:
  9.5 16.3 all-gather.12
  27.5 17.9 all-gather.14
  47.0 11.7 all-gather.16
  60.2 21.0 all-gather.18
  82.6 21.0 all-gather.20
  157.1 11.1 reduce-scatter.9
  284.3 15.4 reduce-scatter.5
  302.1 20.8 reduce-scatter.7
  325.3 28.5 reduce-scatter.11
  356.1 26.3 reduce-scatter.13
  389.0 757.3 all-reduce.12
where the time goes:
time: 1180 us; the launch traced here: 1170 us
  waiting for transfers between devices  794 us (67%)
  matrix products  146 us (12%)
  blocking collectives  140 us (12%)
  local copies, waits for them, and re-layouts  53.1 us (4%)
  between operations  16.2 us (1%)
  starting transfers between devices  13 us (1%)
  other arithmetic  11.9 us (1%)
    psum x1, waiting for transfers between devices, body(): lax.psum((shards[0], shards[1], shards[2], shards[3], shards[4], shards[5...  662 us
    psum x1, blocking collectives, body(): lax.psum((shards[0], shards[1], shards[2], shards[3], shards[4], shards[5...  82.5 us
    all_to_all x1, blocking collectives, body(): lax.all_to_all(grad_grouped, 'seq', split_axis=0, concat_axis=2, tiled=True)  39.2 us
    dot_general x5, matrix products, contract_rows(): lax.dot_general(left_side, right_side, (((0,), (0,)), ((), ())), preferre...  37.9 us
    unnamed x138, local copies, waits for them, and re-layouts  31.9 us
    reduce_scatter x1, waiting for transfers between devices, body(): lax.psum_scatter(matrices[3], 'frames', scatter_dimension=0, tiled=True)  30.9 us
    reduce_scatter x1, waiting for transfers between devices, body(): lax.psum_scatter(matrices[4], 'frames', scatter_dimension=0, tiled=True)  28.6 us
    all_to_all x1, waiting for transfers between devices, body(): lax.all_to_all(projected, 'seq', split_axis=2, concat_axis=0, tiled=True)  26 us
  transfers between devices with their start and end apart: 14, of which 9 were waited for; matrix products, arithmetic and copies ran while one was open for 14% of the time, Pallas kernels for 0%

commit v1 on v0

v1 whole, which is shorter than its diff:
```python
import functools

import jax
import jax.numpy as jnp
from jax import lax
from jax.experimental import pallas as pl
from jax.experimental.pallas import tpu as pltpu
from jax.sharding import PartitionSpec as P

HEADS = 16
HD = 64
UTTS = 3
EPS = 1e-05
MASKED = 1e12
BF16 = jnp.bfloat16
F32 = jnp.float32
INV_SQRT2 = 0.7071067811865476
INV_SQRT_2PI = 0.3989422804014327


def contract_rows(left_side, right_side):
    return lax.dot_general(
        left_side, right_side, (((0,), (0,)), ((), ())), preferred_element_type=F32
    )


def times_transposed(left_side, right_side):
    return lax.dot_general(
        left_side, right_side, (((1,), (1,)), ((), ())), preferred_element_type=F32
    )


def times(left_side, right_side):
    return jnp.dot(left_side, right_side, preferred_element_type=F32)


def pair_rows(block, lane):
    zero = jnp.zeros_like(block)
    return jnp.concatenate(
        [jnp.where(lane < HD, block, zero), jnp.where(lane >= HD, block, zero)], axis=0
    )


def attend_forward_kernel(n_seq, meta, q_ref, k_ref, v_ref, slope_ref, out_ref, prob_ref, dist):
    tok = q_ref.shape[0]
    length = k_ref.shape[0]

    @pl.when(pl.program_id(0) == 0)
    def _():
        shard = meta[0]
        row = lax.broadcasted_iota(jnp.int32, (length, 2 * tok), 0)
        col = lax.broadcasted_iota(jnp.int32, (length, 2 * tok), 1)
        k_pos = row + shard * tok
        k_pos = jnp.where(k_pos >= length, k_pos - length, k_pos)
        q_pos = jnp.where(col >= tok, col - tok, col) + shard * tok
        k_seg = jnp.zeros_like(k_pos)
        q_seg = jnp.zeros_like(q_pos)
        for j in range(UTTS):
            k_seg = k_seg + (k_pos >= meta[1 + j]).astype(jnp.int32)
            q_seg = q_seg + (q_pos >= meta[1 + j]).astype(jnp.int32)
        allowed = (k_seg == q_seg) & (k_seg < UTTS)
        dist[...] = jnp.where(allowed, jnp.abs(k_pos - q_pos).astype(F32), MASKED)

    lane = lax.broadcasted_iota(jnp.int32, (tok, 2 * HD), 1)
    pair = pair_rows(q_ref[...] * jnp.asarray(HD**-0.5, BF16), lane)
    scores = times_transposed(k_ref[...], pair) - slope_ref[0] * dist[...]
    top = jnp.max(scores, axis=0, keepdims=True)
    exp_scores = jnp.exp(scores - top)
    total = jnp.sum(exp_scores, axis=0, keepdims=True)
    prob = (exp_scores * (1.0 / total)).astype(BF16)
    prob_ref[0] = prob
    mixed = times(v_ref[...].T, prob).T
    mixed = jnp.where(lane < HD, mixed[:tok], mixed[tok:])
    row = lax.broadcasted_iota(jnp.int32, (tok, 2 * HD), 0) + meta[0] * tok
    out_ref[...] = jnp.where(row < meta[UTTS], mixed, 0.0).astype(BF16)


def attend_backward_kernel(q_ref, k_ref, v_ref, grad_ref, prob_ref, gq_ref, gk_ref, gv_ref):
    tok = q_ref.shape[0]
    lane = lax.broadcasted_iota(jnp.int32, (tok, 2 * HD), 1)
    scale = jnp.asarray(HD**-0.5, BF16)
    pair_q = pair_rows(q_ref[...] * scale, lane)
    pair_g = pair_rows(grad_ref[...], lane)
    prob_low = prob_ref[0]
    prob = prob_low.astype(F32)
    prob_grad = times_transposed(v_ref[...], pair_g)
    weighted = prob * prob_grad
    delta = jnp.sum(weighted, axis=0, keepdims=True)
    score_low = (weighted - prob * delta).astype(BF16)
    gv_ref[...] = times(prob_low, pair_g).astype(BF16)
    gk_ref[...] = times(score_low, pair_q).astype(BF16)
    mixed = times((k_ref[...] * scale).T, score_low).T
    gq_ref[...] = jnp.where(lane < HD, mixed[:tok], mixed[tok:]).astype(BF16)


def attend_forward(meta, queries, key_rows, value_rows, slopes, n_seq):
    tok, width = queries.shape
    length = key_rows.shape[0]
    pairs = width // (2 * HD)
    return pl.pallas_call(
        functools.partial(attend_forward_kernel, n_seq),
        grid_spec=pltpu.PrefetchScalarGridSpec(
            num_scalar_prefetch=1,
            grid=(pairs,),
            in_specs=[
                pl.BlockSpec((tok, 2 * HD), lambda g, m: (0, g)),
                pl.BlockSpec((length, 2 * HD), lambda g, m: (0, g)),
                pl.BlockSpec((length, 2 * HD), lambda g, m: (0, g)),
                pl.BlockSpec((1, 1, 2 * tok), lambda g, m: (g, 0, 0)),
            ],
            out_specs=[
                pl.BlockSpec((tok, 2 * HD), lambda g, m: (0, g)),
                pl.BlockSpec((1, length, 2 * tok), lambda g, m: (g, 0, 0)),
            ],
            scratch_shapes=[pltpu.VMEM((length, 2 * tok), F32)],
        ),
        out_shape=[
            jax.ShapeDtypeStruct((tok, width), BF16),
            jax.ShapeDtypeStruct((pairs, length, 2 * tok), BF16),
        ],
        cost_estimate=pl.CostEstimate(
            flops=8 * tok * length * width * 2,
            bytes_accessed=4 * length * width + pairs * length * tok * 4,
            transcendentals=tok * length * HEADS,
        ),
        name="attend_forward",
    )(meta, queries, key_rows, value_rows, slopes)


def attend_backward(queries, key_rows, value_rows, grad_heads, prob):
    tok, width = queries.shape
    length = key_rows.shape[0]
    pairs = width // (2 * HD)
    q_spec = pl.BlockSpec((tok, 2 * HD), lambda g: (0, g))
    k_spec = pl.BlockSpec((length, 2 * HD), lambda g: (0, g))
    return pl.pallas_call(
        attend_backward_kernel,
        grid=(pairs,),
        in_specs=[
            q_spec,
            k_spec,
            k_spec,
            q_spec,
            pl.BlockSpec((1, length, 2 * tok), lambda g: (g, 0, 0)),
        ],
        out_specs=[q_spec, k_spec, k_spec],
        out_shape=[
            jax.ShapeDtypeStruct((tok, width), BF16),
            jax.ShapeDtypeStruct((length, width), BF16),
            jax.ShapeDtypeStruct((length, width), BF16),
        ],
        cost_estimate=pl.CostEstimate(
            flops=16 * tok * length * width * 2,
            bytes_accessed=8 * length * width + pairs * length * tok * 4,
            transcendentals=0,
        ),
        name="attend_backward",
    )(queries, key_rows, value_rows, grad_heads, prob)


def middle_kernel(n_pieces, *refs):
    n2_refs = refs[:n_pieces]
    w_refs = refs[n_pieces : 2 * n_pieces]
    bias_ref, gact_ref = refs[2 * n_pieces : 2 * n_pieces + 2]
    act_ref, gup_ref = refs[2 * n_pieces + 2 : 2 * n_pieces + 4]
    gn2_refs = refs[2 * n_pieces + 4 :]
    pre = bias_ref[...]
    for n2_ref, w_ref in zip(n2_refs, w_refs):
        pre = pre + times(n2_ref[...], w_ref[...])
    cdf = 0.5 + 0.5 * lax.erf(pre * INV_SQRT2)
    pdf = jnp.exp(pre * pre * (-0.5)) * INV_SQRT_2PI
    act_ref[...] = (pre * cdf).astype(BF16)
    gup = (gact_ref[...] * (cdf + pre * pdf)).astype(BF16)
    gup_ref[...] = gup
    first = pl.program_id(0) == 0
    for gn2_ref, w_ref in zip(gn2_refs, w_refs):
        term = times_transposed(gup, w_ref[...])

        @pl.when(first)
        def _():
            gn2_ref[...] = term

        @pl.when(jnp.logical_not(first))
        def _():
            gn2_ref[...] += term


def middle(n2_pieces, w_pieces, up_bias, gact, tile=512):
    tok = gact.shape[0]
    hidden = gact.shape[1]
    rows = [w.shape[0] for w in w_pieces]
    n = len(w_pieces)
    return pl.pallas_call(
        functools.partial(middle_kernel, n),
        grid=(hidden // tile,),
        in_specs=[pl.BlockSpec((tok, r), lambda t: (0, 0)) for r in rows]
        + [pl.BlockSpec((r, tile), lambda t: (0, t)) for r in rows]
        + [pl.BlockSpec((1, tile), lambda t: (0, t)), pl.BlockSpec((tok, tile), lambda t: (0, t))],
        out_specs=[pl.BlockSpec((tok, tile), lambda t: (0, t))] * 2
        + [pl.BlockSpec((tok, r), lambda t: (0, 0)) for r in rows],
        out_shape=[jax.ShapeDtypeStruct((tok, hidden), BF16)] * 2
        + [jax.ShapeDtypeStruct((tok, r), F32) for r in rows],
        cost_estimate=pl.CostEstimate(
            flops=4 * tok * hidden * sum(rows),
            bytes_accessed=2 * hidden * sum(rows) + 8 * tok * hidden,
            transcendentals=2 * tok * hidden,
        ),
        name="middle",
    )(*n2_pieces, *w_pieces, up_bias, gact)


def place_kernel(places, meta, own, by_x, by_y, far_low, far_high, *outs):
    plane = meta[1]
    lower = pl.program_id(0) < pl.num_programs(0) // 2

    def put(ref, index):
        start = 0
        for width, out, base in places:
            at = pl.multiple_of(base + index * width, 128)
            outs[out][:, pl.ds(at, width)] = ref[:, start : start + width].astype(F32)
            start = start + width

    put(own, plane)
    put(by_x, plane ^ 1)
    put(by_y, plane ^ 2)

    @pl.when(lower)
    def _():
        put(far_low, plane ^ 3)

    @pl.when(jnp.logical_not(lower))
    def _():
        put(far_high, plane ^ 3)


def place(meta, parts, places, out_widths, n_seq):
    rows, width = parts[0].shape
    block = rows // n_seq
    half = n_seq // 2
    whole = pl.BlockSpec((block, width), lambda j, m: (j, 0))
    low = pl.BlockSpec((block, width), lambda j, m: (jnp.minimum(j, half - 1), 0))
    high = pl.BlockSpec((block, width), lambda j, m: (jnp.maximum(j - half, 0), 0))
    return pl.pallas_call(
        functools.partial(place_kernel, places),
        grid_spec=pltpu.PrefetchScalarGridSpec(
            num_scalar_prefetch=1,
            grid=(n_seq,),
            in_specs=[whole, whole, whole, low, high],
            out_specs=[
                pl.BlockSpec((block, w), lambda j, m: (lax.rem(j + m[0], n_seq), 0))
                for w in out_widths
            ],
        ),
        out_shape=[jax.ShapeDtypeStruct((rows, w), F32) for w in out_widths],
        cost_estimate=pl.CostEstimate(
            flops=0, bytes_accessed=rows * sum(out_widths) * 6, transcendentals=0
        ),
        name="place",
    )(meta, *parts)


def body(
    frames_in,
    skip_in,
    lengths,
    cotangent,
    w_skip,
    w_qkv,
    w_out,
    w_up,
    w_down,
    skip_bias,
    norm1_gain,
    norm1_bias,
    out_bias,
    norm2_gain,
    norm2_bias,
    up_bias,
    down_bias,
):
    tok = frames_in.shape[3]
    width = frames_in.shape[4]
    frames = frames_in.reshape(tok, width)
    skips = skip_in.reshape(tok, width)
    cotan = cotangent.reshape(tok, width)
    n_batch = lax.axis_size("batch")
    n_seq = lax.axis_size("seq")
    n_frames = lax.axis_size("frames")
    assert n_batch == 4 and n_seq % 2 == 0
    paired = n_frames == 2
    plane = lax.axis_index("batch")
    shard = lax.axis_index("seq")
    core = lax.axis_index("frames")

    def over_frames(array):
        return lax.ppermute(array, "frames", [(0, 1), (1, 0)])

    def over_batch(array, bit):
        return lax.ppermute(array, "batch", [(i, i ^ bit) for i in range(n_batch)])

    def to_seq(array, step):
        return lax.ppermute(array, "seq", [(i, (i + step) % n_seq) for i in range(n_seq)])

    def from_seq(array, step):
        return lax.ppermute(array, "seq", [((i + step) % n_seq, i) for i in range(n_seq)])

    def after(array, *others):
        return lax.optimization_barrier((array, *others))[0]

    def gathered(weight):
        if paired:
            return [weight, over_frames(weight)]
        return [lax.all_gather(weight, "frames", axis=0, tiled=True)]

    def columns(array):
        if not paired:
            return [array]
        half = array.shape[1] // 2
        return [
            lax.dynamic_slice_in_dim(array, core * half, half, 1),
            lax.dynamic_slice_in_dim(array, (1 - core) * half, half, 1),
        ]

    def ordered(pieces, axis=1):
        if not paired:
            return pieces[0]
        own, other = pieces
        return jnp.where(
            core == 0,
            jnp.concatenate([own, other], axis=axis),
            jnp.concatenate([other, own], axis=axis),
        )

    def product(pieces, weights):
        total = times(pieces[0], weights[0])
        for piece, weight in zip(pieces[1:], weights[1:]):
            total = total + times(piece, weight)
        return total

    def back_product(array, weights):
        return [times_transposed(array, weight) for weight in weights]

    def left_rows(array):
        if paired:
            own, other = columns(array)
            return jnp.concatenate([own, over_frames(other)], axis=0)
        split = array.reshape(tok_of(array), n_frames, array.shape[1] // n_frames)
        moved = lax.all_to_all(split, "frames", split_axis=1, concat_axis=0, tiled=True)
        return moved.reshape(array.shape[0] * n_frames, array.shape[1] // n_frames)

    def tok_of(array):
        return array.shape[0]

    def right_rows(array):
        if paired:
            return jnp.concatenate([array, over_frames(array)], axis=0)
        return lax.all_gather(array, "frames", axis=0, tiled=True)

    def by_shard(left):
        block = left.shape[1] // n_seq
        return lax.dynamic_slice_in_dim(
            jnp.concatenate([left, left], axis=1), shard * block, left.shape[1], 1
        )

    def by_plane(right):
        block = right.shape[1] // n_batch
        return jnp.concatenate(
            [
                lax.dynamic_slice_in_dim(right, (plane ^ bits) * block, block, 1)
                for bits in (0, 1, 3, 2)
            ],
            axis=1,
        )

    def joined_send(arrays, move):
        sizes = [a.shape[1] for a in arrays]
        moved = move(jnp.concatenate(arrays, axis=1) if len(arrays) > 1 else arrays[0])
        if len(arrays) == 1:
            return [moved]
        ends = [sum(sizes[: i + 1]) for i in range(len(sizes))]
        return [moved[:, e - s : e] for e, s in zip(ends, sizes)]

    def summed_over_groups(terms):
        terms = [(by_shard(left), by_plane(right)) for left, right in terms]
        rows = terms[0][0].shape[1]
        half = rows // 2

        def gemm(low, high, first, last):
            outs = []
            for left, right in terms:
                block = right.shape[1] // n_batch
                outs.append(
                    contract_rows(left[:, low:high], right[:, first * block : last * block])
                )
            return outs

        low_x = [g.astype(BF16) for g in gemm(0, half, 1, 3)]
        high_y = [g.astype(BF16) for g in gemm(half, rows, 2, 4)]
        from_x = joined_send(low_x, lambda a: over_batch(a, 1))
        from_y = joined_send(high_y, lambda a: over_batch(a, 2))
        low_y = [
            (g + r[:, g.shape[1] :].astype(F32)).astype(BF16)
            for g, r in zip(gemm(0, half, 3, 4), from_x)
        ]
        high_x = [
            (g + r[:, : g.shape[1]].astype(F32)).astype(BF16)
            for g, r in zip(gemm(half, rows, 1, 2), from_y)
        ]
        then_y = joined_send(low_y, lambda a: over_batch(a, 2))
        then_x = joined_send(high_x, lambda a: over_batch(a, 1))
        own = []
        for g, fx, fy, ty, tx in zip(gemm(0, rows, 0, 1), from_x, from_y, then_y, then_x):
            n = g.shape[1]
            low = fx[:, :n].astype(F32) + ty.astype(F32)
            high = fy[:, n:].astype(F32) + tx.astype(F32)
            own.append(g + jnp.concatenate([low, high], axis=0))
        own = jnp.concatenate(own, axis=1) if len(own) > 1 else own[0]
        block = rows // n_seq
        total = own[:block]
        for j in range(1, n_seq):
            sent = own[j * block : (j + 1) * block].astype(BF16)
            total = total + to_seq(sent, j).astype(F32)
        total = total.astype(BF16)
        whole = jnp.concatenate(
            [total] + [from_seq(total, j) for j in range(1, n_seq)], axis=0
        )
        by_x = over_batch(whole, 1)
        by_y = over_batch(whole, 2)
        far_low = over_batch(by_y[:half], 1)
        far_high = over_batch(by_x[half:], 2)
        return whole, by_x, by_y, far_low, far_high

    vectors_in = (
        skip_bias,
        norm1_gain,
        norm1_bias,
        out_bias,
        norm2_gain,
        norm2_bias,
        up_bias,
        down_bias,
    )
    sizes = [v.shape[0] for v in vectors_in]
    packed = jnp.concatenate(vectors_in).reshape(1, -1)
    if paired:
        other = over_frames(packed)
        packed = jnp.where(
            core == 0,
            jnp.concatenate([packed, other], axis=0),
            jnp.concatenate([other, packed], axis=0),
        )
    else:
        packed = lax.all_gather(packed, "frames", axis=0, tiled=True)
    packed = packed.astype(F32)
    starts = [sum(sizes[:i]) for i in range(len(sizes))]
    sbias, gain1, bias1, obias, gain2, bias2, ubias, dbias = [
        packed[:, b : b + n].reshape(1, -1) for b, n in zip(starts, sizes)
    ]
    full_skip = gathered(w_skip)
    full_qkv = gathered(after(w_qkv, full_skip[-1]))
    full_down = gathered(after(w_down, full_qkv[-1]))
    full_out = gathered(after(w_out, full_down[-1]))
    full_up = gathered(after(w_up, full_out[-1]))

    joined = [frames, skips] if paired else [jnp.concatenate([frames, skips], axis=1)]
    if paired:
        inputs = [jnp.where(core == 0, frames, skips), jnp.where(core == 0, skips, frames)]
    else:
        inputs = joined
    hidden_z = product(inputs, full_skip) + sbias

    def statistics(values):
        mean = jnp.mean(values, axis=-1, keepdims=True)
        centred = values - mean
        variance = jnp.mean(centred * centred, axis=-1, keepdims=True)
        return mean, lax.rsqrt(variance + EPS)

    mean1, rstd1 = statistics(hidden_z)
    unit1 = (hidden_z - mean1) * rstd1
    n1 = (unit1 * gain1 + bias1).astype(BF16)
    n1_all = [n1] + [from_seq(n1, j) for j in range(1, n_seq)]
    w_q = [w[:, :width] for w in full_qkv]
    w_kv = [w[:, width:] for w in full_qkv]
    qkv_own = product(columns(n1), full_qkv).astype(BF16)
    n1_rest = jnp.concatenate(n1_all[1:], axis=0)
    kv_rest = product(columns(n1_rest), w_kv).astype(BF16)
    queries = qkv_own[:, :width]
    key_rows = jnp.concatenate([qkv_own[:, width : 2 * width], kv_rest[:, :width]], axis=0)
    value_rows = jnp.concatenate([qkv_own[:, 2 * width :], kv_rest[:, width:]], axis=0)
    gact = ordered(back_product(cotan, full_down))
    bounds = jnp.cumsum(lengths.reshape(-1), dtype=jnp.int32)
    meta = jnp.concatenate([shard.astype(jnp.int32).reshape(1), bounds])
    slopes = 2.0 ** (-8.0 * jnp.arange(1, HEADS + 1, dtype=F32) / HEADS)
    slopes = jnp.repeat(slopes, tok).reshape(HEADS // 2, 1, 2 * tok)
    attended, prob = attend_forward(meta, queries, key_rows, value_rows, slopes, n_seq)
    resid = hidden_z + product(columns(attended), full_out) + obias
    mean2, rstd2 = statistics(resid)
    unit2 = (resid - mean2) * rstd2
    n2 = (unit2 * gain2 + bias2).astype(BF16)
    activ, gup, *gn2 = middle(columns(n2), full_up, ubias, gact)
    gn2 = ordered(gn2)
    output = resid + product(columns(activ), full_down) + dbias

    def norm_back(unit, rstd, gain, grad):
        scaled = grad * gain
        mean_e = jnp.mean(scaled, axis=-1, keepdims=True)
        mean_eu = jnp.mean(scaled * unit, axis=-1, keepdims=True)
        return rstd * (scaled - mean_e - unit * mean_eu)

    grad_resid = cotan.astype(F32) + norm_back(unit2, rstd2, gain2, gn2)
    grad_branch = grad_resid.astype(BF16)
    row = lax.broadcasted_iota(jnp.int32, (tok, 1), 0) + shard * tok
    live = row < bounds[UTTS - 1]
    grad_heads = jnp.where(live, ordered(back_product(grad_branch, full_out)), 0.0).astype(BF16)
    gq, gk, gv = attend_backward(queries, key_rows, value_rows, grad_heads, prob)
    gkv = jnp.concatenate([gk, gv], axis=1)
    gn1_rest = ordered(back_product(gkv[tok:], w_kv)).astype(BF16)
    gn1 = ordered(
        [a + b for a, b in zip(back_product(gkv[:tok], w_kv), back_product(gq, w_q))]
    )
    for j in range(1, n_seq):
        gn1 = gn1 + to_seq(gn1_rest[(j - 1) * tok : j * tok], j).astype(F32)
    grad_z = (grad_resid + norm_back(unit1, rstd1, gain1, gn1)).astype(BF16)
    pieces = back_product(grad_z, full_skip)
    if paired:
        input_grad = jnp.where(core == 0, pieces[0], pieces[1])
        skip_grad = jnp.where(core == 0, pieces[1], pieces[0])
    else:
        input_grad, skip_grad = pieces[0][:, :width], pieces[0][:, width:]

    both_cotan = right_rows(cotan)
    parts_down = summed_over_groups([(left_rows(activ), both_cotan)])
    parts_up = summed_over_groups(
        [(left_rows(n2), right_rows(gup)), (left_rows(attended), right_rows(grad_branch))]
    )
    left_n1 = left_rows(jnp.concatenate(n1_all, axis=0))
    parts_qkv = summed_over_groups(
        [(left_rows(n1), right_rows(gq)), (left_n1, right_rows(gkv))]
    )
    if paired:
        left_joined = jnp.concatenate([inputs[0], over_frames(inputs[1])], axis=0)
    else:
        left_joined = left_rows(joined[0])
    parts_skip = summed_over_groups([(left_joined, right_rows(grad_z))])
    where = jnp.stack([shard.astype(jnp.int32), plane.astype(jnp.int32)])
    hidden = w_up.shape[1]
    n_b = n_batch
    (grad_w_down,) = place(where, parts_down, ((width // n_b, 0, 0),), (width,), n_seq)
    grad_w_up, grad_w_out = place(
        where,
        parts_up,
        ((hidden // n_b, 0, 0), (width // n_b, 1, 0)),
        (hidden, width),
        n_seq,
    )
    (grad_w_qkv,) = place(
        where,
        parts_qkv,
        ((width // n_b, 0, 0), (2 * width // n_b, 0, width)),
        (3 * width,),
        n_seq,
    )
    (grad_w_skip,) = place(where, parts_skip, ((width // n_b, 0, 0),), (width,), n_seq)

    vectors = (
        jnp.sum(grad_z, axis=0, dtype=F32),
        jnp.sum(unit1 * gn1, axis=0),
        jnp.sum(gn1, axis=0),
        jnp.sum(grad_branch, axis=0, dtype=F32),
        jnp.sum(unit2 * gn2, axis=0),
        jnp.sum(gn2, axis=0),
        jnp.sum(gup, axis=0, dtype=F32),
        jnp.sum(cotan, axis=0, dtype=F32),
    )
    stacked = jnp.concatenate([v.reshape(n_frames, -1) for v in vectors], axis=1)
    if paired:
        mine = lax.dynamic_slice_in_dim(stacked, core, 1, 0)
        theirs = lax.dynamic_slice_in_dim(stacked, 1 - core, 1, 0)
        mine = mine + over_frames(theirs)
    else:
        mine = lax.psum_scatter(stacked, "frames", scatter_dimension=0, tiled=True)
    mine = mine + over_batch(mine, 1)
    mine = mine + over_batch(mine, 2)
    total = mine
    for j in range(1, n_seq):
        total = total + from_seq(mine, j)
    total = total.reshape(-1)
    vector_grads = [total[b : b + n] for b, n in zip(starts, sizes)]

    def back(array):
        return array.reshape(1, 1, 1, tok, width)

    return (
        back(output.astype(BF16)),
        back(input_grad),
        back(skip_grad),
        grad_w_skip,
        grad_w_qkv,
        grad_w_out,
        grad_w_up,
        grad_w_down,
        *vector_grads,
    )


def solution(mesh):
    rows = P("batch", "seq", "frames", None, None)
    in_specs = (
        (rows, rows, P("batch", "frames", None), rows)
        + (P("frames", None),) * 5
        + (P("frames"),) * 8
    )
    out_specs = (rows,) * 3 + (P("frames", None),) * 5 + (P("frames"),) * 8
    return jax.shard_map(body, mesh=mesh, in_specs=in_specs, out_specs=out_specs, check_vma=False)
```

time: 1180 us -> 584 us (0.49)
  waiting for transfers between devices: 794 us -> 237 us
  blocking collectives: 140 us -> 0 us
  starting transfers between devices: 13 us -> 126 us
  matrix products: 146 us -> 62.9 us
  Pallas kernels: 0 us -> 60.3 us
  other arithmetic: 11.9 us -> 48.1 us
  between operations: 16.2 us -> 2.74 us
    psum x1 -> x0, waiting for transfers between devices: 662 us -> none  [body(): lax.psum((shards[0], shards[1], shards[2], shards[3], shards[4], shards[5...]
    ppermute x0 -> x86, waiting for transfers between devices: none -> 237 us  [the longest x34 119 us: over_batch(): return lax.ppermute(array, 'batch', [(i, i ^ bit) for i in range(n_batch)])]
    ppermute x0 -> x86, starting transfers between devices: none -> 126 us  [the longest x15 46.3 us: to_seq(): lax.ppermute(array, 'seq', [(i, (i + step) % n_seq) for i in range(n_seq)])]
    psum x1 -> x0, blocking collectives: 82.5 us -> none  [body(): lax.psum((shards[0], shards[1], shards[2], shards[3], shards[4], shards[5...]
    reduce_scatter x5 -> x0, waiting for transfers between devices: 63 us -> none  [the longest x1 30.9 us: body(): lax.psum_scatter(matrices[3], 'frames', scatter_dimension=0, tiled=True)]
    dot_general x11 -> x10, matrix products: 82.2 us -> 20 us  [times(): return jnp.dot(left_side, right_side, preferred_element_type=F32)]
    pallas_call x0 -> x7, Pallas kernels: none -> 60.3 us  [the longest x4 25.3 us: place(): pl.pallas_call(functools.partial(place_kernel, places), grid_spec=pltpu.P...]
    all_to_all x3 -> x0, waiting for transfers between devices: 40.3 us -> none  [the longest x1 26 us: body(): lax.all_to_all(projected, 'seq', split_axis=2, concat_axis=0, tiled=True)]
  transfers between devices with their start and end apart: 14 -> 86, of which waited for: 9 -> 32; matrix products, arithmetic and copies ran while one was open for 14% -> 23% of each run, Pallas kernels for 0% -> 5%
where the time goes in v1:
time: 584 us; the launch traced here: 579 us
  waiting for transfers between devices  237 us (41%)
  starting transfers between devices  126 us (22%)
  matrix products  62.9 us (11%)
  Pallas kernels  60.3 us (10%)
  other arithmetic  48.1 us (8%)
  local copies, waits for them, and re-layouts  41.9 us (7%)
    ppermute x34, waiting for transfers between devices, over_batch(): return lax.ppermute(array, 'batch', [(i, i ^ bit) for i in range(n_batch)])  119 us
    ppermute x15, waiting for transfers between devices, to_seq(): lax.ppermute(array, 'seq', [(i, (i + step) % n_seq) for i in range(n_seq)])  70.7 us
    ppermute x15, starting transfers between devices, to_seq(): lax.ppermute(array, 'seq', [(i, (i + step) % n_seq) for i in range(n_seq)])  46.3 us
    ppermute x18, waiting for transfers between devices, from_seq(): lax.ppermute(array, 'seq', [((i + step) % n_seq, i) for i in range(n_seq)])  43.1 us
    ppermute x18, starting transfers between devices, from_seq(): lax.ppermute(array, 'seq', [((i + step) % n_seq, i) for i in range(n_seq)])  38.9 us
    ppermute x34, starting transfers between devices, over_batch(): return lax.ppermute(array, 'batch', [(i, i ^ bit) for i in range(n_batch)])  35.7 us
    dot_general x12, matrix products, times_transposed(): lax.dot_general(left_side, right_side, (((1,), (1,)), ((), ())), preferre...  25.3 us
    pallas_call x4, Pallas kernels, place(): pl.pallas_call(functools.partial(place_kernel, places), grid_spec=pltpu.P...  25.3 us
  transfers between devices with their start and end apart: 86, of which 32 were waited for; matrix products, arithmetic and copies ran while one was open for 23% of the time, Pallas kernels for 5%

profile of v1, /device:TPU:0, one launch (start us, length us, event | category | flops | bytes accessed | tf_op | source)
XLA Modules:
  0.0 578.5 jit_solution(1474427789887244222)
XLA Ops:
  32.4 7.4 %collective-permute-done.5 = bf16[192,1024]{1,0:T(8,128)(2,1)S(1)} collective-permute-done((bf16[192,1024]{1,0:T(8,128)(2,1)S(1)}, bf16[192,1024]{1,0:T(8,128)(2,1)S(1)}, u32[]{:S(2)}, u32[]{:S(2)}) %collective-permute-start.5) | collective-permute-done | bytes 393248 | tf_op jit(solution)/shard_map/ppermute | solution.py:305
  39.8 16.3 %collective-permute-done.4 = bf16[192,1024]{1,0:T(8,128)(2,1)S(1)} collective-permute-done((bf16[192,1024]{1,0:T(8,128)(2,1)S(1)}, bf16[192,1024]{1,0:T(8,128)(2,1)S(1)}, u32[]{:S(2)}, u32[]{:S(2)}) %collective-permute-start.4) | collective-permute-done | bytes 393248 | tf_op jit(solution)/shard_map/ppermute | solution.py:305
  63.7 6.0 %fusion.29 = bf16[1536,512]{1,0:T(8,128)(2,1)S(1)} fusion(s32[]{:T(128)S(6)} %select_n.191, bf16[768,512]{1,0:T(8,128)(2,1)S(1)} %get-tuple-element.68, bf16[768,512]{1,0:T(8,128)(2,1)S(1)} %collective-permute-done.30), kind=kLoop, calls=%fused_computation.62 | loop fusion | flops 6291456 | bytes 3145732 | tf_op jit(solution)/shard_map/concatenate | solution.py:362
  72.9 4.8 fusion.225
  83.8 11.1 %attend_forward.1 = (bf16[192,1024]{1,0:T(8,128)(2,1)}, bf16[8,768,384]{2,1,0:T(8,128)(2,1)}) custom-call(s32[4]{0:T(128)} %pad_add_fusion.meta, bf16[192,1024]{1,0:T(8,128)(2,1)} %get-tuple-element.81.q_ref, bf16[768,1024]{1,0:T(8,128)(2,1)} %get-tuple-element.135.k_ref, bf16[768,1024]{1,0:T(8,128)(2,1)} %get-tuple-element.136.v_ref, ...), custom_call_target="tpu_custom_call" | custom-call | flops 2415919104 | bytes 7864320 | tf_op jit(solution)/shard_map/attend_forward/pallas_call | solution.py:100
  111.1 12.9 %middle.1 = (bf16[192,4096]{1,0:T(8,128)(2,1)}, bf16[192,4096]{1,0:T(8,128)(2,1)}, f32[192,512]{1,0:T(8,128)}, f32[192,512]{1,0:T(8,128)}) custom-call(bf16[192,512]{1,0:T(8,128)(2,1)} %copy-done.32, bf16[192,512]{1,0:T(8,128)(2,1)} %copy-done.41, bf16[512,4096]{1,0:T(8,128)(2,1)} %refs_2_, bf16[512,4096]{1,0:T(8,128)(2,1)} %collective-permute-done.8.refs_3_, ...), custom_call_target="tpu_custom_call" | custom-call | flops 3221225472 | bytes 14680064 | tf_op jit(solution)/shard_map/middle/pallas_call | solution.py:193
  133.4 11.0 %attend_backward.1 = (bf16[192,1024]{1,0:T(8,128)(2,1)}, bf16[768,1024]{1,0:T(8,128)(2,1)}, bf16[768,1024]{1,0:T(8,128)(2,1)}) custom-call(bf16[192,1024]{1,0:T(8,128)(2,1)} %get-tuple-element.81.q_ref, bf16[768,1024]{1,0:T(8,128)(2,1)} %get-tuple-element.135.k_ref, bf16[768,1024]{1,0:T(8,128)(2,1)} %get-tuple-element.136.v_ref, ...), custom_call_target="tpu_custom_call" | custom-call | flops 4831838208 | bytes 11010048 | tf_op jit(solution)/shard_map/attend_backward/pallas_call | solution.py:136
  163.8 8.9 %collective-permute-start.9 = (bf16[192,1024]{1,0:T(8,128)(2,1)S(1)}, bf16[192,1024]{1,0:T(8,128)(2,1)S(1)}, u32[]{:S(2)}, u32[]{:S(2)}) collective-permute-start(bf16[192,1024]{1,0:T(8,128)(2,1)S(1)} %get-tuple-element.76), channel_id=1, source_target_pairs={{0,2},{2,4},{4,6},{6,0},{1,3},{3,5},{5,7},{7,1},{8,10},{10,12},{12... | collective-permute-start | bytes 1179656 | tf_op jit(solution)/shard_map/ppermute | solution.py:302
  183.8 7.8 %collective-permute-done.11 = bf16[192,1024]{1,0:T(8,128)(2,1)S(1)} collective-permute-done((bf16[192,1024]{1,0:T(8,128)(2,1)S(1)}, bf16[192,1024]{1,0:T(8,128)(2,1)S(1)}, u32[]{:S(2)}, u32[]{:S(2)}) %collective-permute-start.11) | collective-permute-done | bytes 393248 | tf_op jit(solution)/shard_map/ppermute | solution.py:302
  191.7 16.8 %collective-permute-done.10 = bf16[192,1024]{1,0:T(8,128)(2,1)S(1)} collective-permute-done((bf16[192,1024]{1,0:T(8,128)(2,1)S(1)}, bf16[192,1024]{1,0:T(8,128)(2,1)S(1)}, u32[]{:S(2)}, u32[]{:S(2)}) %collective-permute-start.10) | collective-permute-done | bytes 393248 | tf_op jit(solution)/shard_map/ppermute | solution.py:302
  262.9 9.7 %collective-permute-done.68 = bf16[1024,512]{1,0:T(8,128)(2,1)S(1)} collective-permute-done((bf16[1024,512]{1,0:T(8,128)(2,1)S(1)}, bf16[1024,512]{1,0:T(8,128)(2,1)S(1)}, u32[]{:S(2)}, u32[]{:S(2)}) %collective-permute-start.68) | collective-permute-done | bytes 1048608 | tf_op jit(solution)/shard_map/ppermute | solution.py:299
  279.0 5.9 %collective-permute-done.69 = bf16[1024,256]{1,0:T(8,128)(2,1)S(1)} collective-permute-done((bf16[1024,256]{1,0:T(8,128)(2,1)S(1)}, bf16[1024,256]{1,0:T(8,128)(2,1)S(1)}, u32[]{:S(2)}, u32[]{:S(2)}) %collective-permute-start.69) | collective-permute-done | bytes 524320 | tf_op jit(solution)/shard_map/ppermute | solution.py:299
  292.5 8.1 %collective-permute-done.22 = bf16[256,256]{1,0:T(8,128)(2,1)S(1)} collective-permute-done((bf16[256,256]{1,0:T(8,128)(2,1)S(1)}, bf16[256,256]{1,0:T(8,128)(2,1)S(1)}, u32[]{:S(2)}, u32[]{:S(2)}) %collective-permute-start.22) | collective-permute-done | bytes 131104 | tf_op jit(solution)/shard_map/ppermute | solution.py:305
  305.4 8.2 %collective-permute-start.71 = (bf16[512,256]{1,0:T(8,128)(2,1)S(1)}, bf16[512,256]{1,0:T(8,128)(2,1)S(1)}, u32[]{:S(2)}, u32[]{:S(2)}) collective-permute-start(bf16[512,256]{1,0:T(8,128)(2,1)S(1)} %get-tuple-element.84), channel_id=1, source_target_pairs={{0,4},{2,6},{4,0},{6,2},{1,5},{3,7},{5,1},{7,3},{8,12},{10,14},{12... | collective-permute-start | bytes 786440 | tf_op jit(solution)/shard_map/ppermute | solution.py:302
  314.6 14.5 %collective-permute-done.71 = bf16[512,256]{1,0:T(8,128)(2,1)S(1)} collective-permute-done((bf16[512,256]{1,0:T(8,128)(2,1)S(1)}, bf16[512,256]{1,0:T(8,128)(2,1)S(1)}, u32[]{:S(2)}, u32[]{:S(2)}) %collective-permute-start.71) | collective-permute-done | bytes 262176 | tf_op jit(solution)/shard_map/ppermute | solution.py:302
  349.2 8.2 %collective-permute-done.53 = bf16[256,1280]{1,0:T(8,128)(2,1)S(1)} collective-permute-done((bf16[256,1280]{1,0:T(8,128)(2,1)S(1)}, bf16[256,1280]{1,0:T(8,128)(2,1)S(1)}, u32[]{:S(2)}, u32[]{:S(2)}) %collective-permute-start.53) | collective-permute-done | bytes 655392 | tf_op jit(solution)/shard_map/ppermute | solution.py:299
  364.2 10.3 %collective-permute-done.34 = bf16[256,1536]{1,0:T(8,128)(2,1)S(1)} collective-permute-done((bf16[256,1536]{1,0:T(8,128)(2,1)S(1)}, bf16[256,1536]{1,0:T(8,128)(2,1)S(1)}, u32[]{:S(2)}, u32[]{:S(2)}) %collective-permute-start.34) | collective-permute-done | bytes 786464 | tf_op jit(solution)/shard_map/ppermute | solution.py:299
  387.3 5.9 %collective-permute-start.55 = (bf16[128,1280]{1,0:T(8,128)(2,1)S(1)}, bf16[128,1280]{1,0:T(8,128)(2,1)S(1)}, u32[]{:S(2)}, u32[]{:S(2)}) collective-permute-start(bf16[128,1280]{1,0:T(8,128)(2,1)S(1)} %get-tuple-element.75), channel_id=1, source_target_pairs={{0,4},{2,6},{4,0},{6,2},{1,5},{3,7},{5,1},{7,3},{8,12},{10,14},{12... | collective-permute-start | bytes 983048 | tf_op jit(solution)/shard_map/ppermute | solution.py:302
  395.0 8.2 %collective-permute-start.36 = (bf16[128,768]{1,0:T(8,128)(2,1)S(1)}, bf16[128,768]{1,0:T(8,128)(2,1)S(1)}, u32[]{:S(2)}, u32[]{:S(2)}) collective-permute-start(bf16[128,768]{1,0:T(8,128)(2,1)S(1)} %get-tuple-element.92), channel_id=1, source_target_pairs={{0,2},{2,4},{4,6},{6,0},{1,3},{3,5},{5,7},{7,1},{8,10},{10,12},{12... | collective-permute-start | bytes 589832 | tf_op jit(solution)/shard_map/ppermute | solution.py:302
  403.2 17.5 %collective-permute-done.55 = bf16[128,1280]{1,0:T(8,128)(2,1)S(1)} collective-permute-done((bf16[128,1280]{1,0:T(8,128)(2,1)S(1)}, bf16[128,1280]{1,0:T(8,128)(2,1)S(1)}, u32[]{:S(2)}, u32[]{:S(2)}) %collective-permute-start.55) | collective-permute-done | bytes 327712 | tf_op jit(solution)/shard_map/ppermute | solution.py:302
  421.0 6.6 %collective-permute-start.58 = (bf16[128,1280]{1,0:T(8,128)(2,1)S(1)}, bf16[128,1280]{1,0:T(8,128)(2,1)S(1)}, u32[]{:S(2)}, u32[]{:S(2)}) collective-permute-start(bf16[128,1280]{1,0:T(8,128)(2,1)S(1)} %fusion.104), channel_id=1, source_target_pairs={{4,0},{6,2},{0,4},{2,6},{5,1},{7,3},{1,5},{3,7},{12,8},{14,10},{8,... | collective-permute-start | bytes 983048 | tf_op jit(solution)/shard_map/ppermute | solution.py:305
  427.7 10.9 %collective-permute-done.37 = bf16[128,768]{1,0:T(8,128)(2,1)S(1)} collective-permute-done((bf16[128,768]{1,0:T(8,128)(2,1)S(1)}, bf16[128,768]{1,0:T(8,128)(2,1)S(1)}, u32[]{:S(2)}, u32[]{:S(2)}) %collective-permute-start.37) | collective-permute-done | bytes 196640 | tf_op jit(solution)/shard_map/ppermute | solution.py:302
  439.5 6.6 %collective-permute-start.41 = (bf16[128,768]{1,0:T(8,128)(2,1)S(1)}, bf16[128,768]{1,0:T(8,128)(2,1)S(1)}, u32[]{:S(2)}, u32[]{:S(2)}) collective-permute-start(bf16[128,768]{1,0:T(8,128)(2,1)S(1)} %fusion.123), channel_id=1, source_target_pairs={{6,0},{0,2},{2,4},{4,6},{7,1},{1,3},{3,5},{5,7},{14,8},{8,10},{10,... | collective-permute-start | bytes 589832 | tf_op jit(solution)/shard_map/ppermute | solution.py:305
  448.0 12.2 %collective-permute-start.39 = (bf16[128,768]{1,0:T(8,128)(2,1)S(1)}, bf16[128,768]{1,0:T(8,128)(2,1)S(1)}, u32[]{:S(2)}, u32[]{:S(2)}) collective-permute-start(bf16[128,768]{1,0:T(8,128)(2,1)S(1)} %fusion.123), channel_id=1, source_target_pairs={{2,0},{4,2},{6,4},{0,6},{3,1},{5,3},{7,5},{1,7},{10,8},{12,10},{14... | collective-permute-start | bytes 589832 | tf_op jit(solution)/shard_map/ppermute | solution.py:305
  471.8 14.6 %collective-permute-done.76.by_x = bf16[2048,256]{1,0:T(8,128)(2,1)S(1)} collective-permute-done((bf16[2048,256]{1,0:T(8,128)(2,1)S(1)}, bf16[2048,256]{1,0:T(8,128)(2,1)S(1)}, u32[]{:S(2)}, u32[]{:S(2)}) %collective-permute-start.76) | collective-permute-done | bytes 1048608 | tf_op jit(solution)/shard_map/ppermute | solution.py:299
  487.9 12.4 %collective-permute-done.43.by_y = bf16[512,768]{1,0:T(8,128)(2,1)S(1)} collective-permute-done((bf16[512,768]{1,0:T(8,128)(2,1)S(1)}, bf16[512,768]{1,0:T(8,128)(2,1)S(1)}, u32[]{:S(2)}, u32[]{:S(2)}) %collective-permute-start.43) | collective-permute-done | bytes 786464 | tf_op jit(solution)/shard_map/ppermute | solution.py:299
  500.3 31.1 %collective-permute-done.42.by_x = bf16[512,768]{1,0:T(8,128)(2,1)S(1)} collective-permute-done((bf16[512,768]{1,0:T(8,128)(2,1)S(1)}, bf16[512,768]{1,0:T(8,128)(2,1)S(1)}, u32[]{:S(2)}, u32[]{:S(2)}) %collective-permute-start.42) | collective-permute-done | bytes 786464 | tf_op jit(solution)/shard_map/ppermute | solution.py:299
  541.7 4.6 collective-permute-done.26.far_low
  550.3 5.0 place.4
  556.1 6.8 %place.7 = f32[2048,1024]{1,0:T(8,128)} custom-call(s32[2]{0:T(128)} %pad_add_fusion.1.meta, bf16[2048,256]{1,0:T(8,128)(2,1)} %copy-done.15, bf16[2048,256]{1,0:T(8,128)(2,1)} %copy-done.27, bf16[2048,256]{1,0:T(8,128)(2,1)} %copy-done.26, bf16[1024,256]{1,0:T(8,128)(2,1)} %copy-done.44, bf16[1024,256]{1,0:T(8,128)(2,1)} %copy-done.45), custom_call_target="tpu_custom_call" | custom-call | bytes 12582912 | tf_op jit(solution)/shard_map/place/pallas_call | solution.py:243
  562.9 5.8 %place.5 = f32[512,3072]{1,0:T(8,128)} custom-call(s32[2]{0:T(128)} %pad_add_fusion.1.meta, bf16[512,768]{1,0:T(8,128)(2,1)} %copy-done.21, bf16[512,768]{1,0:T(8,128)(2,1)} %copy-done.30, bf16[512,768]{1,0:T(8,128)(2,1)} %copy-done.29, bf16[256,768]{1,0:T(8,128)(2,1)} %collective-permute-done.44.far_low, bf16[256,768]{1,0:T(8,128)(2,1)} %collective-permute-done.45.far_high), custom_call_target="tpu_custom_call" | custom-call | bytes 9437184 | tf_op jit(solution)/shard_map/place/pallas_call | solution.py:243
  570.4 7.6 %place.6 = (f32[512,4096]{1,0:T(8,128)}, f32[512,1024]{1,0:T(8,128)}) custom-call(s32[2]{0:T(128)} %pad_add_fusion.1.meta, bf16[512,1280]{1,0:T(8,128)(2,1)} %copy-done.11, bf16[512,1280]{1,0:T(8,128)(2,1)} %copy-done.25, bf16[512,1280]{1,0:T(8,128)(2,1)} %copy-done.24, bf16[256,1280]{1,0:T(8,128)(2,1)} %copy-done.42, bf16[256,1280]{1,0:T(8,128)(2,1)} %copy-done.43), custom_call_target="tpu_custom_call" | custom-call | bytes 15728640 | tf_op jit(solution)/shard_map/place/pallas_call | solution.py:243
  (473 shorter events, 252.0 us)
Async XLA Ops:
  14.4 43.7 %collective-permute-start.12 = (bf16[192,1024]{1,0:T(8,128)(2,1)}, bf16[192,1024]{1,0:T(8,128)(2,1)}, u32[]{:S(2)}, u32[]{:S(2)}) collective-permute-start(bf16[192,1024]{1,0:T(8,128)(2,1)} %get-tuple-element.101), channel_id=1, source_target_pairs={{0,1},{1,0},{2,3},{3,2},{4,5},{5,4},{6,7},{7,6},{8,9},{9,8},{10,11... | collective-permute-start | bytes 1179656 | tf_op jit(solution)/shard_map/ppermute | solution.py:296
  20.9 51.9 %collective-permute-start.6 = (bf16[2048,1024]{1,0:T(8,128)(2,1)}, bf16[2048,1024]{1,0:T(8,128)(2,1)S(1)}, u32[]{:S(2)}, u32[]{:S(2)}) collective-permute-start(bf16[2048,1024]{1,0:T(8,128)(2,1)} %param.25), channel_id=1, source_target_pairs={{0,1},{1,0},{2,3},{3,2},{4,5},{5,4},{6,7},{7,6},{8,9},{9,8},{10,11... | collective-permute-start | bytes 12582920 | tf_op jit(solution)/shard_map/ppermute | solution.py:296
  27.7 28.4 %collective-permute-start.4 = (bf16[192,1024]{1,0:T(8,128)(2,1)S(1)}, bf16[192,1024]{1,0:T(8,128)(2,1)S(1)}, u32[]{:S(2)}, u32[]{:S(2)}) collective-permute-start(bf16[192,1024]{1,0:T(8,128)(2,1)S(1)} %add_convert_fusion.3), channel_id=1, source_target_pairs={{4,0},{6,2},{0,4},{2,6},{5,1},{7,3},{1,5},{3,7},{12,8},{14,10},{8,... | collective-permute-start | bytes 1179656 | tf_op jit(solution)/shard_map/ppermute | solution.py:305
  30.3 25.8 %collective-permute-start.3 = (bf16[192,1024]{1,0:T(8,128)(2,1)S(1)}, bf16[192,1024]{1,0:T(8,128)(2,1)S(1)}, u32[]{:S(2)}, u32[]{:S(2)}) collective-permute-start(bf16[192,1024]{1,0:T(8,128)(2,1)S(1)} %add_convert_fusion.3), channel_id=1, source_target_pairs={{2,0},{4,2},{6,4},{0,6},{3,1},{5,3},{7,5},{1,7},{10,8},{12,10},{14... | collective-permute-start | bytes 1179656 | tf_op jit(solution)/shard_map/ppermute | solution.py:305
  80.0 31.1 %collective-permute-start.8 = (bf16[512,4096]{1,0:T(8,128)(2,1)}, bf16[512,4096]{1,0:T(8,128)(2,1)}, u32[]{:S(2)}, u32[]{:S(2)}) collective-permute-start(bf16[512,4096]{1,0:T(8,128)(2,1)} %refs_2_), channel_id=1, source_target_pairs={{0,1},{1,0},{2,3},{3,2},{4,5},{5,4},{6,7},{7,6},{8,9},{9,8},{10,11... | collective-permute-start | bytes 12582920 | tf_op jit(solution)/shard_map/ppermute | solution.py:296
  147.1 76.7 %collective-permute-start.29 = (bf16[192,1024]{1,0:T(8,128)(2,1)}, bf16[192,1024]{1,0:T(8,128)(2,1)}, u32[]{:S(2)}, u32[]{:S(2)}) collective-permute-start(bf16[192,1024]{1,0:T(8,128)(2,1)} %get-tuple-element.42), channel_id=1, source_target_pairs={{0,1},{1,0},{2,3},{3,2},{4,5},{5,4},{6,7},{7,6},{8,9},{9,8},{10,11... | collective-permute-start | bytes 1179656 | tf_op jit(solution)/shard_map/ppermute | solution.py:296
  147.2 73.8 %collective-permute-start.49 = (bf16[192,1024]{1,0:T(8,128)(2,1)}, bf16[192,1024]{1,0:T(8,128)(2,1)}, u32[]{:S(2)}, u32[]{:S(2)}) collective-permute-start(bf16[192,1024]{1,0:T(8,128)(2,1)} %get-tuple-element.54), channel_id=1, source_target_pairs={{0,1},{1,0},{2,3},{3,2},{4,5},{5,4},{6,7},{7,6},{8,9},{9,8},{10,11... | collective-permute-start | bytes 1179656 | tf_op jit(solution)/shard_map/ppermute | solution.py:296
  173.9 34.6 %collective-permute-start.10 = (bf16[192,1024]{1,0:T(8,128)(2,1)S(1)}, bf16[192,1024]{1,0:T(8,128)(2,1)S(1)}, u32[]{:S(2)}, u32[]{:S(2)}) collective-permute-start(bf16[192,1024]{1,0:T(8,128)(2,1)S(1)} %get-tuple-element.78), channel_id=1, source_target_pairs={{0,4},{2,6},{4,0},{6,2},{1,5},{3,7},{5,1},{7,3},{8,12},{10,14},{12... | collective-permute-start | bytes 1179656 | tf_op jit(solution)/shard_map/ppermute | solution.py:302
  183.8 75.7 %collective-permute-start.47 = (bf16[192,4096]{1,0:T(8,128)(2,1)}, bf16[192,4096]{1,0:T(8,128)(2,1)}, u32[]{:S(2)}, u32[]{:S(2)}) collective-permute-start(bf16[192,4096]{1,0:T(8,128)(2,1)} %get-tuple-element.43), channel_id=1, source_target_pairs={{0,1},{1,0},{2,3},{3,2},{4,5},{5,4},{6,7},{7,6},{8,9},{9,8},{10,11... | collective-permute-start | bytes 4718600 | tf_op jit(solution)/shard_map/ppermute | solution.py:296
  191.6 42.0 %collective-permute-start.64 = (bf16[192,2048]{1,0:T(8,128)(2,1)}, bf16[192,2048]{1,0:T(8,128)(2,1)}, u32[]{:S(2)}, u32[]{:S(2)}) collective-permute-start(bf16[192,2048]{1,0:T(8,128)(2,1)} %get-tuple-element.72), channel_id=1, source_target_pairs={{0,1},{1,0},{2,3},{3,2},{4,5},{5,4},{6,7},{7,6},{8,9},{9,8},{10,11... | collective-permute-start | bytes 2359304 | tf_op jit(solution)/shard_map/ppermute | solution.py:296
  247.4 25.3 %collective-permute-start.68 = (bf16[1024,512]{1,0:T(8,128)(2,1)S(1)}, bf16[1024,512]{1,0:T(8,128)(2,1)S(1)}, u32[]{:S(2)}, u32[]{:S(2)}) collective-permute-start(bf16[1024,512]{1,0:T(8,128)(2,1)S(1)} %convolution_convert_fusion.2), channel_id=1, source_target_pairs={{0,16},{8,24},{16,0},{24,8},{1,17},{9,25},{17,1},{25,9},{2,18},{10... | collective-permute-start | bytes 3145736 | tf_op jit(solution)/shard_map/ppermute | solution.py:299
  248.0 25.9 %collective-permute-start.66 = (bf16[1024,512]{1,0:T(8,128)(2,1)S(1)}, bf16[1024,512]{1,0:T(8,128)(2,1)S(1)}, u32[]{:S(2)}, u32[]{:S(2)}) collective-permute-start(bf16[1024,512]{1,0:T(8,128)(2,1)S(1)} %convolution_convert_fusion.3), channel_id=1, source_target_pairs={{0,8},{8,0},{16,24},{24,16},{1,9},{9,1},{17,25},{25,17},{2,10},{10... | collective-permute-start | bytes 3145736 | tf_op jit(solution)/shard_map/ppermute | solution.py:299
  276.8 67.8 %collective-permute-start.31 = (bf16[768,2048]{1,0:T(8,128)(2,1)S(1)}, bf16[768,2048]{1,0:T(8,128)(2,1)S(1)}, u32[]{:S(2)}, u32[]{:S(2)}) collective-permute-start(bf16[768,2048]{1,0:T(8,128)(2,1)S(1)} %copy-done.1), channel_id=1, source_target_pairs={{0,1},{1,0},{2,3},{3,2},{4,5},{5,4},{6,7},{7,6},{8,9},{9,8},{10,11... | collective-permute-start | bytes 9437192 | tf_op jit(solution)/shard_map/ppermute | solution.py:296
  277.4 51.9 %collective-permute-start.52 = (bf16[256,2560]{1,0:T(8,128)(2,1)S(1)}, bf16[256,2560]{1,0:T(8,128)(2,1)S(1)}, u32[]{:S(2)}, u32[]{:S(2)}) collective-permute-start(bf16[256,2560]{1,0:T(8,128)(2,1)S(1)} %pad_maximum_fusion.6), channel_id=1, source_target_pairs={{0,16},{8,24},{16,0},{24,8},{1,17},{9,25},{17,1},{25,9},{2,18},{10... | collective-permute-start | bytes 3932168 | tf_op jit(solution)/shard_map/ppermute | solution.py:299
  300.5 30.5 %collective-permute-start.50 = (bf16[256,2560]{1,0:T(8,128)(2,1)S(1)}, bf16[256,2560]{1,0:T(8,128)(2,1)S(1)}, u32[]{:S(2)}, u32[]{:S(2)}) collective-permute-start(bf16[256,2560]{1,0:T(8,128)(2,1)S(1)} %pad_maximum_fusion.5), channel_id=1, source_target_pairs={{0,8},{8,0},{16,24},{24,16},{1,9},{9,1},{17,25},{25,17},{2,10},{10... | collective-permute-start | bytes 3932168 | tf_op jit(solution)/shard_map/ppermute | solution.py:299
  305.4 23.7 %collective-permute-start.71 = (bf16[512,256]{1,0:T(8,128)(2,1)S(1)}, bf16[512,256]{1,0:T(8,128)(2,1)S(1)}, u32[]{:S(2)}, u32[]{:S(2)}) collective-permute-start(bf16[512,256]{1,0:T(8,128)(2,1)S(1)} %get-tuple-element.84), channel_id=1, source_target_pairs={{0,4},{2,6},{4,0},{6,2},{1,5},{3,7},{5,1},{7,3},{8,12},{10,14},{12... | collective-permute-start | bytes 786440 | tf_op jit(solution)/shard_map/ppermute | solution.py:302
  314.1 80.9 %collective-permute-start.85 = (f32[1,5632]{1,0:T(1,128)S(1)}, f32[1,5632]{1,0:T(1,128)S(1)}, u32[]{:S(2)}, u32[]{:S(2)}) collective-permute-start(f32[1,5632]{1,0:T(1,128)S(1)} %add.462), channel_id=1, source_target_pairs={{6,0},{0,2},{2,4},{4,6},{7,1},{1,3},{3,5},{5,7},{14,8},{8,10},{10,... | collective-permute-start | bytes 67592 | tf_op jit(solution)/shard_map/ppermute | solution.py:305
  337.7 83.3 %collective-permute-start.25 = (bf16[1024,256]{1,0:T(8,128)(2,1)S(1)}, bf16[1024,256]{1,0:T(8,128)(2,1)S(1)}, u32[]{:S(2)}, u32[]{:S(2)}) collective-permute-start(bf16[1024,256]{1,0:T(8,128)(2,1)S(1)} %pad_maximum_fusion.14.own), channel_id=1, source_target_pairs={{0,16},{8,24},{16,0},{24,8},{1,17},{9,25},{17,1},{25,9},{2,18},{10... | collective-permute-start | bytes 1572872 | tf_op jit(solution)/shard_map/ppermute | solution.py:299
  346.3 28.1 %collective-permute-start.34 = (bf16[256,1536]{1,0:T(8,128)(2,1)S(1)}, bf16[256,1536]{1,0:T(8,128)(2,1)S(1)}, u32[]{:S(2)}, u32[]{:S(2)}) collective-permute-start(bf16[256,1536]{1,0:T(8,128)(2,1)S(1)} %pad_maximum_fusion.10), channel_id=1, source_target_pairs={{0,16},{8,24},{16,0},{24,8},{1,17},{9,25},{17,1},{25,9},{2,18},{10... | collective-permute-start | bytes 2359304 | tf_op jit(solution)/shard_map/ppermute | solution.py:299
  387.3 33.4 %collective-permute-start.55 = (bf16[128,1280]{1,0:T(8,128)(2,1)S(1)}, bf16[128,1280]{1,0:T(8,128)(2,1)S(1)}, u32[]{:S(2)}, u32[]{:S(2)}) collective-permute-start(bf16[128,1280]{1,0:T(8,128)(2,1)S(1)} %get-tuple-element.75), channel_id=1, source_target_pairs={{0,4},{2,6},{4,0},{6,2},{1,5},{3,7},{5,1},{7,3},{8,12},{10,14},{12... | collective-permute-start | bytes 983048 | tf_op jit(solution)/shard_map/ppermute | solution.py:302
  394.9 71.0 %collective-permute-start.77 = (bf16[2048,256]{1,0:T(8,128)(2,1)S(1)}, bf16[2048,256]{1,0:T(8,128)(2,1)S(1)}, u32[]{:S(2)}, u32[]{:S(2)}) collective-permute-start(bf16[2048,256]{1,0:T(8,128)(2,1)S(1)} %pad_maximum_fusion.8.own), channel_id=1, source_target_pairs={{0,16},{8,24},{16,0},{24,8},{1,17},{9,25},{17,1},{25,9},{2,18},{10... | collective-permute-start | bytes 3145736 | tf_op jit(solution)/shard_map/ppermute | solution.py:299
  395.0 26.0 %collective-permute-start.36 = (bf16[128,768]{1,0:T(8,128)(2,1)S(1)}, bf16[128,768]{1,0:T(8,128)(2,1)S(1)}, u32[]{:S(2)}, u32[]{:S(2)}) collective-permute-start(bf16[128,768]{1,0:T(8,128)(2,1)S(1)} %get-tuple-element.92), channel_id=1, source_target_pairs={{0,2},{2,4},{4,6},{6,0},{1,3},{3,5},{5,7},{7,1},{8,10},{10,12},{12... | collective-permute-start | bytes 589832 | tf_op jit(solution)/shard_map/ppermute | solution.py:302
  403.2 24.4 %collective-permute-start.38 = (bf16[128,768]{1,0:T(8,128)(2,1)S(1)}, bf16[128,768]{1,0:T(8,128)(2,1)S(1)}, u32[]{:S(2)}, u32[]{:S(2)}) collective-permute-start(bf16[128,768]{1,0:T(8,128)(2,1)S(1)} %get-tuple-element.93), channel_id=1, source_target_pairs={{0,6},{2,0},{4,2},{6,4},{1,7},{3,1},{5,3},{7,5},{8,14},{10,8},{12,... | collective-permute-start | bytes 589832 | tf_op jit(solution)/shard_map/ppermute | solution.py:302
  421.0 26.7 %collective-permute-start.58 = (bf16[128,1280]{1,0:T(8,128)(2,1)S(1)}, bf16[128,1280]{1,0:T(8,128)(2,1)S(1)}, u32[]{:S(2)}, u32[]{:S(2)}) collective-permute-start(bf16[128,1280]{1,0:T(8,128)(2,1)S(1)} %fusion.104), channel_id=1, source_target_pairs={{4,0},{6,2},{0,4},{2,6},{5,1},{7,3},{1,5},{3,7},{12,8},{14,10},{8,... | collective-permute-start | bytes 983048 | tf_op jit(solution)/shard_map/ppermute | solution.py:305
  438.5 27.1 %collective-permute-start.24 = (bf16[1024,256]{1,0:T(8,128)(2,1)S(1)}, bf16[1024,256]{1,0:T(8,128)(2,1)S(1)}, u32[]{:S(2)}, u32[]{:S(2)}) collective-permute-start(bf16[1024,256]{1,0:T(8,128)(2,1)S(1)} %pad_maximum_fusion.14.own), channel_id=1, source_target_pairs={{0,8},{8,0},{16,24},{24,16},{1,9},{9,1},{17,25},{25,17},{2,10},{10... | collective-permute-start | bytes 1572872 | tf_op jit(solution)/shard_map/ppermute | solution.py:299
  460.3 26.1 %collective-permute-start.76 = (bf16[2048,256]{1,0:T(8,128)(2,1)S(1)}, bf16[2048,256]{1,0:T(8,128)(2,1)S(1)}, u32[]{:S(2)}, u32[]{:S(2)}) collective-permute-start(bf16[2048,256]{1,0:T(8,128)(2,1)S(1)} %pad_maximum_fusion.8.own), channel_id=1, source_target_pairs={{0,8},{8,0},{16,24},{24,16},{1,9},{9,1},{17,25},{25,17},{2,10},{10... | collective-permute-start | bytes 3145736 | tf_op jit(solution)/shard_map/ppermute | solution.py:299
  460.9 70.5 %collective-permute-start.61 = (bf16[512,1280]{1,0:T(8,128)(2,1)S(1)}, bf16[512,1280]{1,0:T(8,128)(2,1)S(1)}, u32[]{:S(2)}, u32[]{:S(2)}) collective-permute-start(bf16[512,1280]{1,0:T(8,128)(2,1)S(1)} %pad_maximum_fusion.7.own), channel_id=1, source_target_pairs={{0,16},{8,24},{16,0},{24,8},{1,17},{9,25},{17,1},{25,9},{2,18},{10... | collective-permute-start | bytes 3932168 | tf_op jit(solution)/shard_map/ppermute | solution.py:299
  464.4 67.6 %collective-permute-start.60 = (bf16[512,1280]{1,0:T(8,128)(2,1)S(1)}, bf16[512,1280]{1,0:T(8,128)(2,1)S(1)}, u32[]{:S(2)}, u32[]{:S(2)}) collective-permute-start(bf16[512,1280]{1,0:T(8,128)(2,1)S(1)} %pad_maximum_fusion.7.own), channel_id=1, source_target_pairs={{0,8},{8,0},{16,24},{24,16},{1,9},{9,1},{17,25},{25,17},{2,10},{10... | collective-permute-start | bytes 3932168 | tf_op jit(solution)/shard_map/ppermute | solution.py:299
  465.6 34.6 %collective-permute-start.43 = (bf16[512,768]{1,0:T(8,128)(2,1)S(1)}, bf16[512,768]{1,0:T(8,128)(2,1)S(1)}, u32[]{:S(2)}, u32[]{:S(2)}) collective-permute-start(bf16[512,768]{1,0:T(8,128)(2,1)S(1)} %pad_maximum_fusion.11.own), channel_id=1, source_target_pairs={{0,16},{8,24},{16,0},{24,8},{1,17},{9,25},{17,1},{25,9},{2,18},{10... | collective-permute-start | bytes 2359304 | tf_op jit(solution)/shard_map/ppermute | solution.py:299
  466.0 65.4 %collective-permute-start.42 = (bf16[512,768]{1,0:T(8,128)(2,1)S(1)}, bf16[512,768]{1,0:T(8,128)(2,1)S(1)}, u32[]{:S(2)}, u32[]{:S(2)}) collective-permute-start(bf16[512,768]{1,0:T(8,128)(2,1)S(1)} %pad_maximum_fusion.11.own), channel_id=1, source_target_pairs={{0,8},{8,0},{16,24},{24,16},{1,9},{9,1},{17,25},{25,17},{2,10},{10... | collective-permute-start | bytes 2359304 | tf_op jit(solution)/shard_map/ppermute | solution.py:299
  486.4 61.0 %collective-permute-start.78 = (bf16[1024,256]{1,0:T(8,128)(2,1)S(1)}, bf16[1024,256]{1,0:T(8,128)(2,1)S(1)}, u32[]{:S(2)}, u32[]{:S(2)}) collective-permute-start(bf16[1024,256]{1,0:T(8,128)(2,1)S(1)} %slice.589), channel_id=1, source_target_pairs={{0,8},{8,0},{16,24},{24,16},{1,9},{9,1},{17,25},{25,17},{2,10},{10... | collective-permute-start | bytes 1572872 | tf_op jit(solution)/shard_map/ppermute | solution.py:299
  500.2 38.4 %collective-permute-start.84 = (f32[1,5632]{1,0:T(1,128)S(1)}, f32[1,5632]{1,0:T(1,128)S(1)}, u32[]{:S(2)}, u32[]{:S(2)}) collective-permute-start(f32[1,5632]{1,0:T(1,128)S(1)} %add.462), channel_id=1, source_target_pairs={{4,0},{6,2},{0,4},{2,6},{5,1},{7,3},{1,5},{3,7},{12,8},{14,10},{8,... | collective-permute-start | bytes 67592 | tf_op jit(solution)/shard_map/ppermute | solution.py:305
  (118 other events, 1594.9 us)

commit v2 on v1

v2 whole, which is shorter than its diff:
```python
import functools

import jax
import jax.numpy as jnp
from jax import lax
from jax.experimental import pallas as pl
from jax.experimental.pallas import tpu as pltpu
from jax.sharding import PartitionSpec as P

HEADS = 16
HD = 64
UTTS = 3
EPS = 1e-05
MASKED = 1e12
BF16 = jnp.bfloat16
F32 = jnp.float32
INV_SQRT2 = 0.7071067811865476
INV_SQRT_2PI = 0.3989422804014327
ERFC_STEP = 0.4
ERFC_TERMS = (
    0.22567586186829244 / 2,
    0.22566960544571626 / 2,
    0.20784251123900896 / 2,
    0.16854379658168633 / 2,
    0.14142295790506823 / 2,
    -0.005586494604590357 / 2,
    0.16905696704198306 / 2,
    -0.18288169574958996 / 2,
    0.05025661354969599 / 2,
)


def contract_rows(left_side, right_side):
    return lax.dot_general(
        left_side, right_side, (((0,), (0,)), ((), ())), preferred_element_type=F32
    )


def times_transposed(left_side, right_side):
    return lax.dot_general(
        left_side, right_side, (((1,), (1,)), ((), ())), preferred_element_type=F32
    )


def times(left_side, right_side):
    return jnp.dot(left_side, right_side, preferred_element_type=F32)


def pair_rows(block, lane):
    zero = jnp.zeros_like(block)
    return jnp.concatenate(
        [jnp.where(lane < HD, block, zero), jnp.where(lane >= HD, block, zero)], axis=0
    )


def attend_forward_kernel(n_seq, meta, q_ref, k_ref, v_ref, slope_ref, out_ref, prob_ref, dist):
    tok = q_ref.shape[0]
    length = k_ref.shape[0]

    @pl.when(pl.program_id(0) == 0)
    def _():
        shard = meta[0]
        row = lax.broadcasted_iota(jnp.int32, (length, 2 * tok), 0)
        col = lax.broadcasted_iota(jnp.int32, (length, 2 * tok), 1)
        k_pos = row + shard * tok
        k_pos = jnp.where(k_pos >= length, k_pos - length, k_pos)
        q_pos = jnp.where(col >= tok, col - tok, col) + shard * tok
        k_seg = jnp.zeros_like(k_pos)
        q_seg = jnp.zeros_like(q_pos)
        for j in range(UTTS):
            k_seg = k_seg + (k_pos >= meta[1 + j]).astype(jnp.int32)
            q_seg = q_seg + (q_pos >= meta[1 + j]).astype(jnp.int32)
        allowed = (k_seg == q_seg) & (k_seg < UTTS)
        dist[...] = jnp.where(allowed, jnp.abs(k_pos - q_pos).astype(F32), MASKED)

    lane = lax.broadcasted_iota(jnp.int32, (tok, 2 * HD), 1)
    pair = pair_rows(q_ref[...] * jnp.asarray(HD**-0.5, BF16), lane)
    scores = times_transposed(k_ref[...], pair) - slope_ref[0] * dist[...]
    top = jnp.max(scores, axis=0, keepdims=True)
    exp_scores = jnp.exp(scores - top)
    total = jnp.sum(exp_scores, axis=0, keepdims=True)
    prob = (exp_scores * (1.0 / total)).astype(BF16)
    prob_ref[0] = prob
    mixed = times(v_ref[...].T, prob).T
    mixed = jnp.where(lane < HD, mixed[:tok], mixed[tok:])
    row = lax.broadcasted_iota(jnp.int32, (tok, 2 * HD), 0) + meta[0] * tok
    out_ref[...] = jnp.where(row < meta[UTTS], mixed, 0.0).astype(BF16)


def attend_backward_kernel(q_ref, k_ref, v_ref, grad_ref, prob_ref, gq_ref, gkv_ref):
    tok = q_ref.shape[0]
    lane = lax.broadcasted_iota(jnp.int32, (tok, 2 * HD), 1)
    scale = jnp.asarray(HD**-0.5, BF16)
    pair_q = pair_rows(q_ref[...] * scale, lane)
    pair_g = pair_rows(grad_ref[...], lane)
    prob_low = prob_ref[0]
    prob = prob_low.astype(F32)
    prob_grad = times_transposed(v_ref[...], pair_g)
    weighted = prob * prob_grad
    delta = jnp.sum(weighted, axis=0, keepdims=True)
    score_low = (weighted - prob * delta).astype(BF16)
    gkv_ref[1] = times(prob_low, pair_g).astype(BF16)
    gkv_ref[0] = times(score_low, pair_q).astype(BF16)
    mixed = times((k_ref[...] * scale).T, score_low).T
    gq_ref[...] = jnp.where(lane < HD, mixed[:tok], mixed[tok:]).astype(BF16)


def attend_forward(meta, queries, key_rows, value_rows, slopes, n_seq):
    tok, width = queries.shape
    length = key_rows.shape[0]
    pairs = width // (2 * HD)
    return pl.pallas_call(
        functools.partial(attend_forward_kernel, n_seq),
        grid_spec=pltpu.PrefetchScalarGridSpec(
            num_scalar_prefetch=1,
            grid=(pairs,),
            in_specs=[
                pl.BlockSpec((tok, 2 * HD), lambda g, m: (0, g)),
                pl.BlockSpec((length, 2 * HD), lambda g, m: (0, g)),
                pl.BlockSpec((length, 2 * HD), lambda g, m: (0, g)),
                pl.BlockSpec((1, 1, 2 * tok), lambda g, m: (g, 0, 0)),
            ],
            out_specs=[
                pl.BlockSpec((tok, 2 * HD), lambda g, m: (0, g)),
                pl.BlockSpec((1, length, 2 * tok), lambda g, m: (g, 0, 0)),
            ],
            scratch_shapes=[pltpu.VMEM((length, 2 * tok), F32)],
        ),
        out_shape=[
            jax.ShapeDtypeStruct((tok, width), BF16),
            jax.ShapeDtypeStruct((pairs, length, 2 * tok), BF16),
        ],
        cost_estimate=pl.CostEstimate(
            flops=8 * tok * length * width * 2,
            bytes_accessed=4 * length * width + pairs * length * tok * 4,
            transcendentals=tok * length * HEADS,
        ),
        name="attend_forward",
    )(meta, queries, key_rows, value_rows, slopes)


def attend_backward(queries, key_rows, value_rows, grad_heads, prob):
    tok, width = queries.shape
    length = key_rows.shape[0]
    pairs = width // (2 * HD)
    q_spec = pl.BlockSpec((tok, 2 * HD), lambda g: (0, g))
    k_spec = pl.BlockSpec((length, 2 * HD), lambda g: (0, g))
    return pl.pallas_call(
        attend_backward_kernel,
        grid=(pairs,),
        in_specs=[
            q_spec,
            k_spec,
            k_spec,
            q_spec,
            pl.BlockSpec((1, length, 2 * tok), lambda g: (g, 0, 0)),
        ],
        out_specs=[q_spec, pl.BlockSpec((2, length, 2 * HD), lambda g: (0, 0, g))],
        out_shape=[
            jax.ShapeDtypeStruct((tok, width), BF16),
            jax.ShapeDtypeStruct((2, length, width), BF16),
        ],
        cost_estimate=pl.CostEstimate(
            flops=16 * tok * length * width * 2,
            bytes_accessed=8 * length * width + pairs * length * tok * 4,
            transcendentals=0,
        ),
        name="attend_backward",
    )(queries, key_rows, value_rows, grad_heads, prob)


def statistics(values):
    mean = jnp.mean(values, axis=-1, keepdims=True)
    centred = values - mean
    variance = jnp.mean(centred * centred, axis=-1, keepdims=True)
    return centred, lax.rsqrt(variance + EPS)


def norm_back(unit, rstd, gain, grad):
    scaled = grad * gain
    mean_e = jnp.mean(scaled, axis=-1, keepdims=True)
    mean_eu = jnp.mean(scaled * unit, axis=-1, keepdims=True)
    return rstd * (scaled - mean_e - unit * mean_eu)


def bases(core, n_pieces, rows):
    if n_pieces == 1:
        return [0]
    return [pl.multiple_of(core * rows, 128), pl.multiple_of((1 - core) * rows, 128)]


def front_kernel(n, *refs):
    x_refs, w_refs = refs[:n], refs[n : 2 * n]
    bias, gain, shift, z_ref, n1_ref = refs[2 * n :]
    step = pl.program_id(0)
    part = times(x_refs[0][...], w_refs[0][...])
    for x_ref, w_ref in zip(x_refs[1:], w_refs[1:]):
        part = part + times(x_ref[...], w_ref[...])

    @pl.when(step == 0)
    def _():
        z_ref[...] = part + bias[...]

    @pl.when(step > 0)
    def _():
        z_ref[...] += part

    @pl.when(step == pl.num_programs(0) - 1)
    def _():
        centred, rstd = statistics(z_ref[...])
        n1_ref[...] = (centred * rstd * gain[...] + shift[...]).astype(BF16)


def front(inputs, weights, bias, gain, shift):
    tok = inputs[0].shape[0]
    rows, width = weights[0].shape
    n = len(weights)
    steps = 4
    block = rows // steps
    vector = pl.BlockSpec((1, width), lambda k: (0, 0))
    whole = pl.BlockSpec((tok, width), lambda k: (0, 0))
    return pl.pallas_call(
        functools.partial(front_kernel, n),
        grid=(steps,),
        in_specs=[pl.BlockSpec((tok, block), lambda k: (0, k))] * n
        + [pl.BlockSpec((block, width), lambda k: (k, 0))] * n
        + [vector] * 3,
        out_specs=[whole, whole],
        out_shape=[
            jax.ShapeDtypeStruct((tok, width), F32),
            jax.ShapeDtypeStruct((tok, width), BF16),
        ],
        name="front",
    )(*inputs, *weights, bias, gain, shift)


def project_kernel(n, chunks, meta, *refs):
    x_refs = refs[:chunks]
    w_refs = refs[chunks : chunks + 3 * n]
    q_ref, k_ref, v_ref = refs[chunks + 3 * n :]
    rows = w_refs[0].shape[0]
    tok = q_ref.shape[0]
    starts = bases(meta[0], n, rows)
    for c in range(chunks):
        for i, out in enumerate((q_ref, k_ref, v_ref)):
            if i == 0 and c > 0:
                continue
            total = None
            for p, start in enumerate(starts):
                term = times(x_refs[c][:, pl.ds(start, rows)], w_refs[3 * p + i][...])
                total = term if total is None else total + term
            out[c * tok : (c + 1) * tok] = total.astype(BF16)


def project(meta, chunks, weights):
    tok, width = chunks[0].shape
    rows = weights[0].shape[0]
    n = len(weights)
    tile = 256
    tiles = width // tile

    def w_spec(i):
        return pl.BlockSpec((rows, tile), lambda t, m: (0, t + i * tiles))

    length = tok * len(chunks)
    return pl.pallas_call(
        functools.partial(project_kernel, n, len(chunks)),
        grid_spec=pltpu.PrefetchScalarGridSpec(
            num_scalar_prefetch=1,
            grid=(tiles,),
            in_specs=[pl.BlockSpec((tok, width), lambda t, m: (0, 0))] * len(chunks)
            + [w_spec(i) for i in range(3)] * n,
            out_specs=[
                pl.BlockSpec((tok, tile), lambda t, m: (0, t)),
                pl.BlockSpec((length, tile), lambda t, m: (0, t)),
                pl.BlockSpec((length, tile), lambda t, m: (0, t)),
            ],
        ),
        out_shape=[
            jax.ShapeDtypeStruct((tok, width), BF16),
            jax.ShapeDtypeStruct((length, width), BF16),
            jax.ShapeDtypeStruct((length, width), BF16),
        ],
        name="project",
    )(meta, *chunks, *[w for w in weights for _ in range(3)])


def centre_kernel(n, meta, *refs):
    refs = list(refs)

    def take(count):
        taken = refs[:count]
        del refs[:count]
        return taken

    att, z_ref, cotan = take(3)
    w_out, w_up, gact = take(n), take(n), take(n)
    up_bias, out_bias, gain, shift = take(4)
    resid, n2, act, gup_ref, gres, gbranch, gatt, up_sum, sums = take(9)
    gn2, unit, rstd = refs
    core, live = meta[0], meta[1]
    step, steps = pl.program_id(0), pl.num_programs(0)
    tok = att.shape[0]
    rows = w_out[0].shape[0]
    starts = bases(core, n, rows)

    @pl.when(step == 0)
    def _():
        total = z_ref[...] + out_bias[...]
        for start, w_ref in zip(starts, w_out):
            total = total + times(att[:, pl.ds(start, rows)], w_ref[...])
        resid[...] = total
        centred, scale = statistics(total)
        unit[...] = centred * scale
        rstd[...] = scale
        n2[...] = (unit[...] * gain[...] + shift[...]).astype(BF16)
        gn2[...] = jnp.zeros_like(gn2)

    pre = up_bias[...]
    for start, w_ref in zip(starts, w_up):
        pre = pre + times(n2[:, pl.ds(start, rows)], w_ref[...])
    gauss = jnp.exp(pre * pre * (-0.5))
    t = 1.0 / (1.0 + (ERFC_STEP * INV_SQRT2) * jnp.abs(pre))
    tail = jnp.full_like(t, ERFC_TERMS[-1])
    for term in ERFC_TERMS[-2::-1]:
        tail = tail * t + term
    tail = tail * t * gauss
    cdf = jnp.where(pre < 0.0, tail, 1.0 - tail)
    act[...] = (pre * cdf).astype(BF16)
    if n == 1:
        grad = gact[0][...]
    else:
        mine = (step // (steps // 2)) == core
        grad = jnp.where(mine, gact[0][...], gact[1][...])
    gup = (grad * (cdf + pre * gauss * INV_SQRT_2PI)).astype(BF16)
    gup_ref[...] = gup
    up_sum[...] = jnp.sum(gup.astype(F32), axis=0, keepdims=True)
    for start, w_ref in zip(starts, w_up):
        gn2[:, pl.ds(start, rows)] += times_transposed(gup, w_ref[...])

    @pl.when(step == steps - 1)
    def _():
        grad_n2 = gn2[...]
        total = cotan[...].astype(F32) + norm_back(unit[...], rstd[...], gain[...], grad_n2)
        gres[...] = total
        low = total.astype(BF16)
        gbranch[...] = low
        alive = lax.broadcasted_iota(jnp.int32, (tok, 1), 0) < live
        for start, w_ref in zip(starts, w_out):
            term = times_transposed(low, w_ref[...])
            gatt[:, pl.ds(start, rows)] = jnp.where(alive, term, 0.0).astype(BF16)
        sums[0:1] = jnp.sum(low.astype(F32), axis=0, keepdims=True)
        sums[1:2] = jnp.sum(unit[...] * grad_n2, axis=0, keepdims=True)
        sums[2:3] = jnp.sum(grad_n2, axis=0, keepdims=True)


def centre(meta, att, z, cotan, w_out, w_up, gact, up_bias, out_bias, gain, shift, tile=512):
    tok, width = att.shape
    n = len(w_out)
    rows = w_out[0].shape[0]
    hidden = w_up[0].shape[1]
    steps = hidden // tile
    per = steps // n
    whole = pl.BlockSpec((tok, width), lambda t, m: (0, 0))
    vector = pl.BlockSpec((1, width), lambda t, m: (0, 0))
    tiled = pl.BlockSpec((tok, tile), lambda t, m: (0, t))

    def gact_spec(i):
        def index(t, m):
            half = m[0] if i == 0 else 1 - m[0]
            return (0, jnp.clip(t - half * per, 0, per - 1))

        return tiled if n == 1 else pl.BlockSpec((tok, tile), index)

    low = jax.ShapeDtypeStruct((tok, width), BF16)
    wide = jax.ShapeDtypeStruct((tok, width), F32)
    return pl.pallas_call(
        functools.partial(centre_kernel, n),
        grid_spec=pltpu.PrefetchScalarGridSpec(
            num_scalar_prefetch=1,
            grid=(steps,),
            in_specs=[whole, whole, whole]
            + [pl.BlockSpec((rows, width), lambda t, m: (0, 0))] * n
            + [pl.BlockSpec((rows, tile), lambda t, m: (0, t))] * n
            + [gact_spec(i) for i in range(n)]
            + [pl.BlockSpec((1, tile), lambda t, m: (0, t)), vector, vector, vector],
            out_specs=[
                whole,
                whole,
                tiled,
                tiled,
                whole,
                whole,
                whole,
                pl.BlockSpec((1, tile), lambda t, m: (0, t)),
                pl.BlockSpec((8, width), lambda t, m: (0, 0)),
            ],
            scratch_shapes=[
                pltpu.VMEM((tok, width), F32),
                pltpu.VMEM((tok, width), F32),
                pltpu.VMEM((tok, 1), F32),
            ],
        ),
        out_shape=[
            wide,
            low,
            jax.ShapeDtypeStruct((tok, hidden), BF16),
            jax.ShapeDtypeStruct((tok, hidden), BF16),
            wide,
            low,
            low,
            jax.ShapeDtypeStruct((1, hidden), F32),
            jax.ShapeDtypeStruct((8, width), F32),
        ],
        name="centre",
    )(meta, att, z, cotan, *w_out, *w_up, *gact, up_bias, out_bias, gain, shift)


def unproject_kernel(n, chunks, meta, gq_ref, gkv_ref, *refs):
    w_refs, (own_ref, rest_ref) = refs[:n], refs[n:]
    rows = w_refs[0].shape[0]
    width = gq_ref.shape[1]
    step = pl.program_id(0)
    for start, w_ref in zip(bases(meta[0], n, rows), w_refs):
        term = times_transposed(gkv_ref[0], w_ref[:, width : 2 * width])
        term = term + times_transposed(gkv_ref[1], w_ref[:, 2 * width :])

        @pl.when(step < chunks - 1)
        def _():
            rest_ref[:, pl.ds(start, rows)] = term.astype(BF16)

        @pl.when(step == chunks - 1)
        def _():
            own_ref[:, pl.ds(start, rows)] = term + times_transposed(
                gq_ref[...], w_ref[:, :width]
            )


def unproject(meta, gq, gkv, weights):
    tok, width = gq.shape
    chunks = gkv.shape[1] // tok
    rows = weights[0].shape[0]
    n = len(weights)
    return pl.pallas_call(
        functools.partial(unproject_kernel, n, chunks),
        grid_spec=pltpu.PrefetchScalarGridSpec(
            num_scalar_prefetch=1,
            grid=(chunks,),
            in_specs=[
                pl.BlockSpec((tok, width), lambda c, m: (0, 0)),
                pl.BlockSpec((2, tok, width), lambda c, m: (0, lax.rem(c + 1, chunks), 0)),
            ]
            + [pl.BlockSpec((rows, 3 * width), lambda c, m: (0, 0))] * n,
            out_specs=[
                pl.BlockSpec((tok, width), lambda c, m: (0, 0)),
                pl.BlockSpec((tok, width), lambda c, m: (jnp.minimum(c, chunks - 2), 0)),
            ],
        ),
        out_shape=[
            jax.ShapeDtypeStruct((tok, width), F32),
            jax.ShapeDtypeStruct(((chunks - 1) * tok, width), BF16),
        ],
        name="unproject",
    )(meta, gq, gkv, *weights)


def rear_kernel(others, own, *refs):
    parts = refs[:others]
    z_ref, gres, gain, gz_ref, sums = refs[others:]
    grad = own[...]
    for part in parts:
        grad = grad + part[...].astype(F32)
    centred, rstd = statistics(z_ref[...])
    unit = centred * rstd
    low = (gres[...] + norm_back(unit, rstd, gain[...], grad)).astype(BF16)
    gz_ref[...] = low
    sums[0:1] = jnp.sum(low.astype(F32), axis=0, keepdims=True)
    sums[1:2] = jnp.sum(unit * grad, axis=0, keepdims=True)
    sums[2:3] = jnp.sum(grad, axis=0, keepdims=True)


def rear(own, parts, z, gres, gain):
    tok, width = own.shape
    return pl.pallas_call(
        functools.partial(rear_kernel, len(parts)),
        out_shape=[
            jax.ShapeDtypeStruct((tok, width), BF16),
            jax.ShapeDtypeStruct((8, width), F32),
        ],
        name="rear",
    )(own, *parts, z, gres, gain)


def input_grads_kernel(n, meta, gz, first, second, input_ref, skip_ref):
    low = times_transposed(gz[...], first[...])
    high = times_transposed(gz[...], second[...])
    if n == 1:
        input_ref[...] = low
        skip_ref[...] = high
        return

    @pl.when(meta[0] == 0)
    def _():
        input_ref[...] = low
        skip_ref[...] = high

    @pl.when(meta[0] != 0)
    def _():
        input_ref[...] = high
        skip_ref[...] = low


def input_grads(meta, gz, weights):
    tok, width = gz.shape
    n = len(weights)
    steps = 4
    tile = width // steps
    if n == 1:
        weights = [weights[0], weights[0]]
    out = pl.BlockSpec((tok, tile), lambda t, m: (0, t))
    return pl.pallas_call(
        functools.partial(input_grads_kernel, n),
        grid_spec=pltpu.PrefetchScalarGridSpec(
            num_scalar_prefetch=1,
            grid=(steps,),
            in_specs=[
                pl.BlockSpec((tok, width), lambda t, m: (0, 0)),
                pl.BlockSpec((tile, width), lambda t, m: (t, 0)),
                pl.BlockSpec((tile, width), lambda t, m: (t + (steps if n == 1 else 0), 0)),
            ],
            out_specs=[out, out],
        ),
        out_shape=[jax.ShapeDtypeStruct((tok, width), F32)] * 2,
        name="input_grads",
    )(meta, gz, *weights)


def pack_kernel(*refs):
    out = refs[-1]
    start = 0
    for ref in refs[:-1]:
        size = ref.shape[1]
        out[:, start : start + size] = ref[...]
        start = start + size


def pack(vectors):
    total = sum(v.shape[0] for v in vectors)
    return pl.pallas_call(
        pack_kernel, out_shape=jax.ShapeDtypeStruct((1, total), vectors[0].dtype), name="pack"
    )(*[v.reshape(1, -1) for v in vectors])


def unpack_kernel(sizes, meta, own, other, *outs):
    start = 0
    for size, out in zip(sizes, outs):
        for ref, core in ((own, meta[0]), (other, 1 - meta[0])):
            at = pl.multiple_of(core * size, 128)
            out[:, pl.ds(at, size)] = ref[:, start : start + size].astype(F32)
        start = start + size


def unpack(meta, own, other, sizes):
    vmem = pl.BlockSpec(memory_space=pltpu.VMEM)
    return pl.pallas_call(
        functools.partial(unpack_kernel, sizes),
        in_specs=[pl.BlockSpec(memory_space=pltpu.SMEM), vmem, vmem],
        out_specs=[vmem] * len(sizes),
        out_shape=[jax.ShapeDtypeStruct((1, 2 * n), F32) for n in sizes],
        name="unpack",
    )(meta, own, other)


def place_kernel(places, meta, own, by_x, by_y, far_low, far_high, *outs):
    plane = meta[0]
    lower = pl.program_id(0) < pl.num_programs(0) // 2

    def put(ref, index):
        start = 0
        for width, out, base in places:
            at = pl.multiple_of(base + index * width, 128)
            outs[out][:, pl.ds(at, width)] = ref[:, start : start + width].astype(F32)
            start = start + width

    put(own, plane)
    put(by_x, plane ^ 1)
    put(by_y, plane ^ 2)

    @pl.when(lower)
    def _():
        put(far_low, plane ^ 3)

    @pl.when(jnp.logical_not(lower))
    def _():
        put(far_high, plane ^ 3)


def place(meta, parts, places, out_widths, n_seq):
    rows, width = parts[0].shape
    block = rows // n_seq
    half = n_seq // 2
    whole = pl.BlockSpec((block, width), lambda j, m: (j, 0))
    low = pl.BlockSpec((block, width), lambda j, m: (jnp.minimum(j, half - 1), 0))
    high = pl.BlockSpec((block, width), lambda j, m: (jnp.maximum(j - half, 0), 0))
    return pl.pallas_call(
        functools.partial(place_kernel, places),
        grid_spec=pltpu.PrefetchScalarGridSpec(
            num_scalar_prefetch=1,
            grid=(n_seq,),
            in_specs=[whole, whole, whole, low, high],
            out_specs=[
                pl.BlockSpec((block, w), lambda j, m: (j, 0))
                for w in out_widths
            ],
        ),
        out_shape=[jax.ShapeDtypeStruct((rows, w), F32) for w in out_widths],
        cost_estimate=pl.CostEstimate(
            flops=0, bytes_accessed=rows * sum(out_widths) * 6, transcendentals=0
        ),
        name="place",
    )(meta, *parts)


class Links:
    def __init__(self):
        self.last = {}

    def send(self, link, array, move, *pins):
        waits = [p for p in pins if p is not None]
        if link in self.last:
            waits.append(self.last[link])
        if waits:
            array = lax.optimization_barrier((array, *waits))[0]
        moved = move(array)
        self.last[link] = moved
        return moved


def tie(array, *others):
    return lax.optimization_barrier((array, *others))[0]


def body(
    frames_in,
    skip_in,
    lengths,
    cotangent,
    w_skip,
    w_qkv,
    w_out,
    w_up,
    w_down,
    skip_bias,
    norm1_gain,
    norm1_bias,
    out_bias,
    norm2_gain,
    norm2_bias,
    up_bias,
    down_bias,
):
    tok = frames_in.shape[3]
    width = frames_in.shape[4]
    hidden = w_up.shape[1]
    frames = frames_in.reshape(tok, width)
    skips = skip_in.reshape(tok, width)
    cotan = cotangent.reshape(tok, width)
    n_batch = lax.axis_size("batch")
    n_seq = lax.axis_size("seq")
    n_frames = lax.axis_size("frames")
    assert n_batch == 4 and n_seq % 2 == 0
    paired = n_frames == 2
    plane = lax.axis_index("batch").astype(jnp.int32)
    shard = lax.axis_index("seq").astype(jnp.int32)
    core = lax.axis_index("frames").astype(jnp.int32)
    links = Links()

    def swap_frames(array):
        return lax.ppermute(array, "frames", [(0, 1), (1, 0)])

    def over_x(array):
        return lax.ppermute(array, "batch", [(i, i ^ 1) for i in range(n_batch)])

    def over_y(array):
        return lax.ppermute(array, "batch", [(i, i ^ 2) for i in range(n_batch)])

    def to_seq(step):
        return lambda array: lax.ppermute(
            array, "seq", [(i, (i + step) % n_seq) for i in range(n_seq)]
        )

    def from_seq(step):
        return to_seq(n_seq - step)

    def exchange_seq(array):
        return lax.all_to_all(array, "seq", split_axis=0, concat_axis=0, tiled=True)

    def gather_frames(array, *pins):
        if paired:
            return [array, links.send("frames", array, swap_frames, *pins)]
        return [lax.all_gather(array, "frames", axis=0, tiled=True)]

    def split_columns(array):
        half = array.shape[1] // 2
        return (
            lax.dynamic_slice_in_dim(array, core * half, half, 1),
            lax.dynamic_slice_in_dim(array, (1 - core) * half, half, 1),
        )

    def product(array, weights):
        pieces = split_columns(array) if paired else [array]
        total = times(pieces[0], weights[0])
        for piece, weight in zip(pieces[1:], weights[1:]):
            total = total + times(piece, weight)
        return total

    def left_rows(array, *pins):
        if paired:
            own, other = split_columns(array)
            return jnp.concatenate([own, links.send("frames", other, swap_frames, *pins)], axis=0)
        split = array.reshape(array.shape[0], n_frames, array.shape[1] // n_frames)
        moved = lax.all_to_all(split, "frames", split_axis=1, concat_axis=0, tiled=True)
        return moved.reshape(array.shape[0] * n_frames, array.shape[1] // n_frames)

    def right_rows(array, *pins):
        if paired:
            return jnp.concatenate([array, links.send("frames", array, swap_frames, *pins)], axis=0)
        return lax.all_gather(array, "frames", axis=0, tiled=True)

    def by_plane(right):
        block = right.shape[1] // n_batch
        return jnp.concatenate(
            [
                lax.dynamic_slice_in_dim(right, (plane ^ bits) * block, block, 1)
                for bits in (0, 1, 3, 2)
            ],
            axis=1,
        )

    class Chain:
        def __init__(self, terms):
            self.terms = [(left, by_plane(right)) for left, right in terms]
            self.rows = terms[0][0].shape[1]

        def gemm(self, low, high, first, last):
            outs = []
            for left, right in self.terms:
                block = right.shape[1] // n_batch
                outs.append(
                    contract_rows(left[:, low:high], right[:, first * block : last * block])
                )
            return outs

        def send(self, link, arrays, move, *pins):
            sizes = [a.shape[1] for a in arrays]
            arrays = [a.astype(BF16) for a in arrays]
            joined = jnp.concatenate(arrays, axis=1) if len(arrays) > 1 else arrays[0]
            moved = links.send(link, joined, move, *pins)
            ends = [sum(sizes[: i + 1]) for i in range(len(sizes))]
            return [moved[:, e - s : e] for e, s in zip(ends, sizes)]

        def first(self, *pins):
            half, rows = self.rows // 2, self.rows
            self.from_x = self.send("x", self.gemm(0, half, 1, 3), over_x, *pins)
            self.from_y = self.send("y", self.gemm(half, rows, 2, 4), over_y, *pins)

        def second(self, *pins):
            half, rows = self.rows // 2, self.rows
            low = [
                g + r[:, g.shape[1] :].astype(F32)
                for g, r in zip(self.gemm(0, half, 3, 4), self.from_x)
            ]
            high = [
                g + r[:, : g.shape[1]].astype(F32)
                for g, r in zip(self.gemm(half, rows, 1, 2), self.from_y)
            ]
            self.then_y = self.send("y", low, over_y, *pins)
            self.then_x = self.send("x", high, over_x, *pins)

        def across(self, *pins):
            own = []
            for g, fx, fy, ty, tx in zip(
                self.gemm(0, self.rows, 0, 1), self.from_x, self.from_y, self.then_y, self.then_x
            ):
                n = g.shape[1]
                low = fx[:, :n].astype(F32) + ty.astype(F32)
                high = fy[:, n:].astype(F32) + tx.astype(F32)
                own.append((g + jnp.concatenate([low, high], axis=0)).astype(BF16))
            own = jnp.concatenate(own, axis=1) if len(own) > 1 else own[0]
            own = own.reshape(n_seq, self.rows // n_seq, own.shape[1])
            self.terms_seq = links.send("z", own, exchange_seq, *pins)

        def along(self, *pins):
            total = jnp.sum(self.terms_seq.astype(F32), axis=0).astype(BF16)
            copies = jnp.broadcast_to(total[None], self.terms_seq.shape)
            whole = links.send("z", copies, exchange_seq, *pins)
            self.whole = whole.reshape(self.rows, whole.shape[2])

        def spread(self, *pins):
            self.by_x = links.send("x", self.whole, over_x, *pins)
            self.by_y = links.send("y", self.whole, over_y, *pins)

        def finish(self, *pins):
            half = self.rows // 2
            self.far_low = links.send("x", self.by_y[:half], over_x, *pins)
            self.far_high = links.send("y", self.by_x[half:], over_y, *pins)

        def parts(self):
            return self.whole, self.by_x, self.by_y, self.far_low, self.far_high

    vectors_in = (
        skip_bias,
        norm1_gain,
        norm1_bias,
        out_bias,
        norm2_gain,
        norm2_bias,
        up_bias,
        down_bias,
    )
    sizes = [v.shape[0] for v in vectors_in]
    starts = [sum(sizes[:i]) for i in range(len(sizes))]
    packed = pack(vectors_in)
    bounds = jnp.cumsum(lengths.reshape(-1), dtype=jnp.int32)
    core_meta = core.reshape(1)
    if paired:
        full_skip = [w_skip, swap_frames(w_skip)]
        links.last["frames"] = full_skip[1]
        vectors = unpack(core_meta, packed, swap_frames(packed), sizes)
        inputs = [jnp.where(core == 0, frames, skips), jnp.where(core == 0, skips, frames)]
    else:
        full_skip = gather_frames(w_skip)
        packed = lax.all_gather(packed, "frames", axis=0, tiled=True).astype(F32)
        vectors = [packed[:, b : b + n].reshape(1, -1) for b, n in zip(starts, sizes)]
        inputs = [jnp.concatenate([frames, skips], axis=1)]
    sbias, gain1, bias1, obias, gain2, bias2, ubias, dbias = vectors
    full_qkv = gather_frames(w_qkv)

    hidden_z, n1 = front(inputs, full_skip, sbias, gain1, bias1)
    n1_all = [n1] + [from_seq(j)(n1) for j in range(1, n_seq)]
    full_down = gather_frames(w_down, n1)
    full_out = gather_frames(w_out)
    full_up = gather_frames(w_up)
    gact = [times_transposed(cotan, weight) for weight in full_down]
    n1_all[-1] = tie(n1_all[-1], *gact)
    queries, key_rows, value_rows = project(core_meta, n1_all, full_qkv)
    attend_meta = jnp.concatenate([shard.reshape(1), bounds])
    slopes = 2.0 ** (-8.0 * jnp.arange(1, HEADS + 1, dtype=F32) / HEADS)
    slopes = jnp.repeat(slopes, tok).reshape(HEADS // 2, 1, 2 * tok)
    attended, prob = attend_forward(attend_meta, queries, key_rows, value_rows, slopes, n_seq)
    both_cotan = right_rows(cotan, queries)
    left_n1 = left_rows(jnp.concatenate(n1_all, axis=0), queries)
    left_att = left_rows(attended)
    centre_meta = jnp.stack([core, bounds[UTTS - 1] - shard * tok])
    resid, n2, activ, gup, grad_resid, grad_branch, grad_heads, up_sum, sums2 = centre(
        centre_meta, attended, hidden_z, cotan, full_out, full_up, gact, ubias, obias, gain2, bias2
    )

    down = Chain([(left_rows(activ), both_cotan)])
    down.first()
    gq, gkv = attend_backward(queries, key_rows, value_rows, grad_heads, prob)
    up = Chain(
        [
            (left_rows(n2, gq), right_rows(gup, gq)),
            (left_att, right_rows(grad_branch, gq)),
        ]
    )
    gn1_own, gn1_rest = unproject(core_meta, gq, gkv, full_qkv)
    gn1_parts = [
        to_seq(j)(gn1_rest[(j - 1) * tok : j * tok]) for j in range(1, n_seq)
    ]
    down.second(gn1_rest)
    up.first()
    grad_z, sums1 = rear(gn1_own, gn1_parts, hidden_z, grad_resid, gain1)
    if paired:
        both_gkv = links.send("frames", gkv, swap_frames, gn1_rest)
        left_q = left_n1.reshape(2, n_seq * tok, -1)[:, :tok].reshape(2 * tok, -1)
        both_k = jnp.concatenate([gkv[0], both_gkv[0]], axis=0)
        both_v = jnp.concatenate([gkv[1], both_gkv[1]], axis=0)
    else:
        left_q = left_rows(n1)
        both_k, both_v = right_rows(gkv[0]), right_rows(gkv[1])
    qkv = Chain([(left_q, right_rows(gq)), (left_n1, both_k), (left_n1, both_v)])
    links.last["z"] = grad_z
    down.across()
    up.second(grad_z)
    qkv.first()
    down.along()
    if paired:
        left_joined = jnp.concatenate(
            [inputs[0], links.send("frames", inputs[1], swap_frames)], axis=0
        )
    else:
        left_joined = left_rows(inputs[0])
    skip = Chain([(left_joined, right_rows(grad_z))])
    up.across()
    qkv.second()
    skip.first()
    up.along()
    skip.second()
    output = (resid + product(activ, full_down) + dbias).astype(BF16)
    down.spread(output)
    qkv.across()
    down.finish()
    qkv.along()
    place_meta = plane.reshape(1)
    quarter = width // n_batch
    (grad_w_down,) = place(place_meta, down.parts(), ((quarter, 0, 0),), (width,), n_seq)
    input_grad, skip_grad = input_grads(core_meta, grad_z, full_skip)
    up.spread(input_grad)
    skip.across()
    up.finish(grad_w_down)
    skip.along()
    grad_w_up, grad_w_out = place(
        place_meta,
        up.parts(),
        ((hidden // n_batch, 0, 0), (quarter, 1, 0)),
        (hidden, width),
        n_seq,
    )

    vector_sums = (
        sums1[0],
        sums1[1],
        sums1[2],
        sums2[0],
        sums2[1],
        sums2[2],
        up_sum[0],
        jnp.sum(cotan, axis=0, dtype=F32),
    )
    stacked = jnp.concatenate([v.reshape(n_frames, -1) for v in vector_sums], axis=1)
    if paired:
        mine = lax.dynamic_slice_in_dim(stacked, core, 1, 0)
        theirs = lax.dynamic_slice_in_dim(stacked, 1 - core, 1, 0)
        mine = mine + links.send("frames", theirs, swap_frames)
    else:
        mine = lax.psum_scatter(stacked, "frames", scatter_dimension=0, tiled=True)
    mine = mine + links.send("x", mine, over_x)
    mine = mine + links.send("y", mine, over_y)
    copies = jnp.broadcast_to(mine[None], (n_seq,) + mine.shape)
    total = jnp.sum(links.send("z", copies, exchange_seq), axis=0).reshape(-1)
    vector_grads = [total[b : b + n] for b, n in zip(starts, sizes)]

    qkv.spread(grad_w_up, grad_w_out)
    qkv.finish()
    (grad_w_qkv,) = place(
        place_meta,
        qkv.parts(),
        ((quarter, 0, 0), (quarter, 0, width), (quarter, 0, 2 * width)),
        (3 * width,),
        n_seq,
    )
    skip.spread()
    skip.finish(grad_w_qkv)
    (grad_w_skip,) = place(place_meta, skip.parts(), ((quarter, 0, 0),), (width,), n_seq)

    def back(array):
        return array.reshape(1, 1, 1, tok, width)

    return (
        back(output),
        back(input_grad),
        back(skip_grad),
        grad_w_skip,
        grad_w_qkv,
        grad_w_out,
        grad_w_up,
        grad_w_down,
        *vector_grads,
    )


def solution(mesh):
    rows = P("batch", "seq", "frames", None, None)
    in_specs = (
        (rows, rows, P("batch", "frames", None), rows)
        + (P("frames", None),) * 5
        + (P("frames"),) * 8
    )
    out_specs = (rows,) * 3 + (P("frames", None),) * 5 + (P("frames"),) * 8
    return jax.shard_map(body, mesh=mesh, in_specs=in_specs, out_specs=out_specs, check_vma=False)
```

time: 584 us -> 518 us (0.89)
  waiting for transfers between devices: 237 us -> 158 us
  starting transfers between devices: 126 us -> 84.8 us
  Pallas kernels: 60.3 us -> 99.7 us
  local copies, waits for them, and re-layouts: 41.9 us -> 68.3 us
  other arithmetic: 48.1 us -> 35.7 us
    ppermute x71 -> x52, waiting for transfers between devices: 166 us -> 110 us  [the longest x17 52.7 us: over_y(): return lax.ppermute(array, 'batch', [(i, i ^ 2) for i in range(n_batch)])]
    pallas_call x1 -> x8, Pallas kernels: 12.9 us -> 55.1 us  [the longest x1 17.8 us: centre(): pl.pallas_call(functools.partial(centre_kernel, n), grid_spec=pltpu.Prefe...]
    ppermute x71 -> x52, starting transfers between devices: 79.6 us -> 39 us  [the longest x17 18.5 us: over_y(): return lax.ppermute(array, 'batch', [(i, i ^ 2) for i in range(n_batch)])]
    ppermute x15 -> x6, starting transfers between devices: 46.3 us -> 8.52 us  [to_seq(): lax.ppermute(array, 'seq', [(i, (i + step) % n_seq) for i in range(n_seq)])]
    all_to_all x0 -> x9, starting transfers between devices: none -> 37.3 us  [exchange_seq(): return lax.all_to_all(array, 'seq', split_axis=0, concat_axis=0, tiled=True)]
    ppermute x15 -> x6, waiting for transfers between devices: 70.7 us -> 38.6 us  [to_seq(): lax.ppermute(array, 'seq', [(i, (i + step) % n_seq) for i in range(n_seq)])]
    dot_general x30 -> x35, matrix products: 17.6 us -> 46.3 us  [contract_rows(): lax.dot_general(left_side, right_side, (((0,), (0,)), ((), ())), preferre...]
    dot_general x12 -> x2, matrix products: 25.3 us -> 9.87 us  [times_transposed(): lax.dot_general(left_side, right_side, (((1,), (1,)), ((), ())), preferre...]
  transfers between devices with their start and end apart: 86 -> 67, of which waited for: 32 -> 32; matrix products, arithmetic and copies ran while one was open for 23% -> 30% of each run, Pallas kernels for 5% -> 19%
where the time goes in v2:
time: 518 us; the launch traced here: 511 us
  waiting for transfers between devices  158 us (31%)
  Pallas kernels  99.7 us (19%)
  starting transfers between devices  84.8 us (16%)
  local copies, waits for them, and re-layouts  68.3 us (13%)
  matrix products  61.6 us (12%)
  other arithmetic  35.7 us (7%)
    ppermute x17, waiting for transfers between devices, over_y(): return lax.ppermute(array, 'batch', [(i, i ^ 2) for i in range(n_batch)])  52.7 us
    dot_general x35, matrix products, contract_rows(): lax.dot_general(left_side, right_side, (((0,), (0,)), ((), ())), preferre...  46.3 us
    ppermute x17, waiting for transfers between devices, over_x(): return lax.ppermute(array, 'batch', [(i, i ^ 1) for i in range(n_batch)])  43.4 us
    ppermute x6, waiting for transfers between devices, to_seq(): lax.ppermute(array, 'seq', [(i, (i + step) % n_seq) for i in range(n_seq)])  38.6 us
    all_to_all x9, starting transfers between devices, exchange_seq(): return lax.all_to_all(array, 'seq', split_axis=0, concat_axis=0, tiled=True)  37.3 us
    unnamed x234, local copies, waits for them, and re-layouts  24.7 us
    pallas_call x4, Pallas kernels, place(): pl.pallas_call(functools.partial(place_kernel, places), grid_spec=pltpu.P...  22.6 us
    ppermute x17, starting transfers between devices, over_y(): return lax.ppermute(array, 'batch', [(i, i ^ 2) for i in range(n_batch)])  18.5 us
  transfers between devices with their start and end apart: 67, of which 32 were waited for; matrix products, arithmetic and copies ran while one was open for 30% of the time, Pallas kernels for 19%

profile of v2, /device:TPU:0, one launch (start us, length us, event | category | flops | bytes accessed | tf_op | source)
XLA Modules:
  0.0 511.4 jit_solution(567255120154107069)
XLA Ops:
  21.4 5.4 %front.1 = (f32[192,1024]{1,0:T(8,128)}, bf16[192,1024]{1,0:T(8,128)(2,1)}) custom-call(bf16[192,1024]{1,0:T(8,128)(2,1)} %get-tuple-element.247.refs_0_, bf16[192,1024]{1,0:T(8,128)(2,1)} %get-tuple-element.151.refs_1_, bf16[1024,1024]{1,0:T(8,128)(2,1)} %first.1, bf16[1024,1024]{1,0:T(8,128)(2,1)} %collective-permute-done.refs_3_.second, ...), custom_call_target="tpu_custom_call" | custom-call | tf_op jit(solution)/shard_map/front/pallas_call | solution.py:222
  27.3 7.1 %collective-permute-done.6 = bf16[2048,1024]{1,0:T(8,128)(2,1)} collective-permute-done((bf16[2048,1024]{1,0:T(8,128)(2,1)}, bf16[2048,1024]{1,0:T(8,128)(2,1)}, u32[]{:S(2)}, u32[]{:S(2)}) %collective-permute-start.6) | collective-permute-done | bytes 4194336 | tf_op jit(solution)/shard_map/ppermute | solution.py:679
  37.8 4.9 fusion.140.refs_7_
  42.7 4.7 collective-permute-start.2
  58.3 23.4 %collective-permute-done.3.refs_2_ = bf16[192,1024]{1,0:T(8,128)(2,1)S(1)} collective-permute-done((bf16[192,1024]{1,0:T(8,128)(2,1)}, bf16[192,1024]{1,0:T(8,128)(2,1)S(1)}, u32[]{:S(2)}, u32[]{:S(2)}) %collective-permute-start.3) | collective-permute-done | bytes 393248 | tf_op jit(solution)/shard_map/ppermute | solution.py:688
  81.7 5.0 convolution_bitcast_fusion.refs_8_
  87.5 8.1 %project.1 = (bf16[192,1024]{1,0:T(8,128)(2,1)}, bf16[768,1024]{1,0:T(8,128)(2,1)}, bf16[768,1024]{1,0:T(8,128)(2,1)}) custom-call(s32[1]{0:T(128)} %bitcast.meta, bf16[192,1024]{1,0:T(8,128)(2,1)} %get-tuple-element.111.refs_0_, bf16[192,1024]{1,0:T(8,128)(2,1)} %collective-permute-done.2.refs_1_, bf16[192,1024]{1,0:T(8,128)(2,1)} %copy-done.37, ...), custom_call_target="tpu_custom_call" | custom-call | tf_op jit(solution)/shard_map/project/pallas_call | solution.py:266
  96.7 11.1 %attend_forward.1 = (bf16[192,1024]{1,0:T(8,128)(2,1)}, bf16[8,768,384]{2,1,0:T(8,128)(2,1)}) custom-call(s32[4]{0:T(128)} %pad_add_fusion.1.meta, bf16[192,1024]{1,0:T(8,128)(2,1)} %get-tuple-element.115.q_ref, bf16[768,1024]{1,0:T(8,128)(2,1)} %get-tuple-element.116.k_ref, bf16[768,1024]{1,0:T(8,128)(2,1)} %get-tuple-element.117.v_ref, ...), custom_call_target="tpu_custom_call" | custom-call | flops 2415919104 | bytes 7864320 | tf_op jit(solution)/shard_map/attend_forward/pallas_call | solution.py:112
  110.9 17.8 %centre.1 = (f32[192,1024]{1,0:T(8,128)}, bf16[192,1024]{1,0:T(8,128)(2,1)}, bf16[192,4096]{1,0:T(8,128)(2,1)}, bf16[192,4096]{1,0:T(8,128)(2,1)}, f32[192,1024]...) custom-call(s32[2]{0:T(128)} %pad_add_fusion.meta, ...), custom_call_target="tpu_custom_call" | custom-call | tf_op jit(solution)/shard_map/centre/pallas_call | solution.py:377
  128.7 10.8 %attend_backward.1 = (bf16[192,1024]{1,0:T(8,128)(2,1)}, bf16[2,768,1024]{2,1,0:T(8,128)(2,1)}) custom-call(bf16[192,1024]{1,0:T(8,128)(2,1)} %get-tuple-element.115.q_ref, bf16[768,1024]{1,0:T(8,128)(2,1)} %get-tuple-element.116.k_ref, bf16[768,1024]{1,0:T(8,128)(2,1)} %get-tuple-element.117.v_ref, bf16[192,1024]{1,0:T(8,128)(2,1)} %get-tuple-element.129.grad_ref, ...), custom_call_target="tpu_custom_call" | custom-call | flops 4831838208 | bytes 11010048 | tf_op jit(solution)/shard_map/attend_backward/pallas_call | solution.py:148
  139.5 12.3 %unproject.1 = (f32[192,1024]{1,0:T(8,128)}, bf16[576,1024]{1,0:T(8,128)(2,1)}) custom-call(s32[1]{0:T(128)} %bitcast.meta, bf16[192,1024]{1,0:T(8,128)(2,1)} %get-tuple-element.150.gq_ref, bf16[2,768,1024]{2,1,0:T(8,128)(2,1)} %get-tuple-element.149.gkv_ref, bf16[512,3072]{1,0:T(8,128)(2,1)} %refs_0_.1, bf16[512,3072]{1,0:T(8,128)(2,1)} %copy-done), custom_call_target="tpu_custom_call" | custom-call | tf_op jit(solution)/shard_map/unproject/pallas_call | solution.py:444
  177.0 11.4 %collective-permute-done.10.refs_1_ = bf16[192,1024]{1,0:T(8,128)(2,1)S(1)} collective-permute-done((bf16[192,1024]{1,0:T(8,128)(2,1)S(1)}, bf16[192,1024]{1,0:T(8,128)(2,1)S(1)}, u32[]{:S(2)}, u32[]{:S(2)}) %collective-permute-start.10) | collective-permute-done | bytes 393248 | tf_op jit(solution)/shard_map/ppermute | solution.py:688
  224.0 4.4 all-to-all-start
  228.4 16.7 %collective-permute-done.28 = bf16[256,2560]{1,0:T(8,128)(2,1)} collective-permute-done((bf16[256,2560]{1,0:T(8,128)(2,1)}, bf16[256,2560]{1,0:T(8,128)(2,1)}, u32[]{:S(2)}, u32[]{:S(2)}) %collective-permute-start.28) | collective-permute-done | bytes 1310752 | tf_op jit(solution)/shard_map/ppermute | solution.py:685
  261.5 4.7 all-to-all-start.1
  290.6 4.4 all-to-all-start.2
  295.3 5.2 %collective-permute-done.30 = bf16[256,1536]{0,1:T(8,128)(2,1)} collective-permute-done((bf16[256,1536]{0,1:T(8,128)(2,1)}, bf16[256,1536]{0,1:T(8,128)(2,1)}, u32[]{:S(2)}, u32[]{:S(2)}) %collective-permute-start.30) | collective-permute-done | bytes 786464 | tf_op jit(solution)/shard_map/ppermute | solution.py:685
  319.1 8.6 %all-to-all-done.2 = bf16[4,128,1280]{2,1,0:T(8,128)(2,1)} async-done(((bf16[4,128,1280]{2,1,0:T(8,128)(2,1)}), bf16[4,128,1280]{2,1,0:T(8,128)(2,1)}, u32[]{:S(2)}, u32[]{:S(2)}) %all-to-all-start.2) | async-done | bytes 1310752 | tf_op jit(solution)/shard_map/all_to_all | solution.py:696
  332.2 4.6 all-to-all-start.3
  341.9 10.5 %collective-permute-done.36 = bf16[512,512]{1,0:T(8,128)(2,1)S(1)} collective-permute-done((bf16[512,512]{1,0:T(8,128)(2,1)S(1)}, bf16[512,512]{1,0:T(8,128)(2,1)S(1)}, u32[]{:S(2)}, u32[]{:S(2)}) %collective-permute-start.36) | collective-permute-done | bytes 524320 | tf_op jit(solution)/shard_map/ppermute | solution.py:685
  369.4 4.3 all-to-all-start.4
  376.1 5.1 %input_grads.1 = (f32[192,1024]{1,0:T(8,128)}, f32[192,1024]{1,0:T(8,128)}) custom-call(s32[1]{0:T(128)} %bitcast.meta, bf16[192,1024]{1,0:T(8,128)(2,1)} %get-tuple-element.152.gz, bf16[1024,1024]{1,0:T(8,128)(2,1)} %first.1, bf16[1024,1024]{1,0:T(8,128)(2,1)} %collective-permute-done.refs_3_.second), custom_call_target="tpu_custom_call" | custom-call | tf_op jit(solution)/shard_map/input_grads/pallas_call | solution.py:521
  393.4 6.2 %collective-permute-done.41.far_low = bf16[1024,256]{1,0:T(8,128)(2,1)S(1)} collective-permute-done((bf16[1024,256]{1,0:T(8,128)(2,1)S(1)}, bf16[1024,256]{1,0:T(8,128)(2,1)S(1)}, u32[]{:S(2)}, u32[]{:S(2)}) %collective-permute-start.41) | collective-permute-done | bytes 524320 | tf_op jit(solution)/shard_map/ppermute | solution.py:682
  405.3 4.4 all-to-all-start.5
  414.5 6.1 %place.4 = f32[2048,1024]{1,0:T(8,128)} custom-call(s32[1]{0:T(128)} %bitcast.14.meta, bf16[2048,256]{1,0:T(8,128)(2,1)} %bitcast.27.own, bf16[2048,256]{1,0:T(8,128)(2,1)} %copy-done.21, bf16[2048,256]{1,0:T(8,128)(2,1)} %collective-permute-done.39.by_y, bf16[1024,256]{1,0:T(8,128)(2,1)} %copy-done.61, bf16[1024,256]{1,0:T(8,128)(2,1)} %collective-permute-done.43.far_high), custom_call_target="tpu_custom_call" | custom-call | bytes 12582912 | tf_op jit(solution)/shard_map/place/pallas_call | solution.py:605
  420.6 8.3 %collective-permute-done.42.by_x = bf16[512,1280]{1,0:T(8,128)(2,1)} collective-permute-done((bf16[512,1280]{1,0:T(8,128)(2,1)}, bf16[512,1280]{1,0:T(8,128)(2,1)}, u32[]{:S(2)}, u32[]{:S(2)}) %collective-permute-start.42) | collective-permute-done | bytes 1310752 | tf_op jit(solution)/shard_map/ppermute | solution.py:682
  438.1 5.5 %collective-permute-done.45.far_low = bf16[256,1280]{1,0:T(8,128)(2,1)} collective-permute-done((bf16[256,1280]{1,0:T(8,128)(2,1)}, bf16[256,1280]{1,0:T(8,128)(2,1)}, u32[]{:S(2)}, u32[]{:S(2)}) %collective-permute-start.45) | collective-permute-done | bytes 655392 | tf_op jit(solution)/shard_map/ppermute | solution.py:682
  449.4 7.0 %place.5 = (f32[512,4096]{1,0:T(8,128)}, f32[512,1024]{1,0:T(8,128)}) custom-call(s32[1]{0:T(128)} %bitcast.14.meta, bf16[512,1280]{1,0:T(8,128)(2,1)} %bitcast.26.own, bf16[512,1280]{1,0:T(8,128)(2,1)} %collective-permute-done.42.by_x, bf16[512,1280]{1,0:T(8,128)(2,1)} %copy-done.20, bf16[256,1280]{1,0:T(8,128)(2,1)} %collective-permute-done.45.far_low, ...), custom_call_target="tpu_custom_call" | custom-call | bytes 15728640 | tf_op jit(solution)/shard_map/place/pallas_call | solution.py:605
  461.4 11.0 %collective-permute-done.51.by_x = bf16[512,768]{1,0:T(8,128)(2,1)S(1)} collective-permute-done((bf16[512,768]{1,0:T(8,128)(2,1)S(1)}, bf16[512,768]{1,0:T(8,128)(2,1)S(1)}, u32[]{:S(2)}, u32[]{:S(2)}) %collective-permute-start.51) | collective-permute-done | bytes 786464 | tf_op jit(solution)/shard_map/ppermute | solution.py:682
  476.8 8.9 %collective-permute-done.54.far_high = bf16[256,768]{1,0:T(8,128)(2,1)S(1)} collective-permute-done((bf16[256,768]{1,0:T(8,128)(2,1)S(1)}, bf16[256,768]{1,0:T(8,128)(2,1)S(1)}, u32[]{:S(2)}, u32[]{:S(2)}) %collective-permute-start.54) | collective-permute-done | bytes 393248 | tf_op jit(solution)/shard_map/ppermute | solution.py:685
  491.8 5.1 %place.6 = f32[512,3072]{1,0:T(8,128)} custom-call(s32[1]{0:T(128)} %bitcast.14.meta, bf16[512,768]{1,0:T(8,128)(2,1)} %bitcast.86, bf16[512,768]{1,0:T(8,128)(2,1)} %copy-done.23, bf16[512,768]{1,0:T(8,128)(2,1)} %collective-permute-done.50.by_y, bf16[256,768]{1,0:T(8,128)(2,1)} %copy-done.63, bf16[256,768]{1,0:T(8,128)(2,1)} %copy-done.62), custom_call_target="tpu_custom_call" | custom-call | bytes 9437184 | tf_op jit(solution)/shard_map/place/pallas_call | solution.py:605
  506.8 4.3 place.7
  (488 shorter events, 250.9 us)
Async XLA Ops:
  5.3 21.5 %collective-permute-start.5 = (bf16[512,3072]{1,0:T(8,128)(2,1)}, bf16[512,3072]{1,0:T(8,128)(2,1)S(1)}, u32[]{:S(2)}, u32[]{:S(2)}) collective-permute-start(bf16[512,3072]{1,0:T(8,128)(2,1)} %refs_0_.1), channel_id=1, source_target_pairs={{0,1},{1,0},{2,3},{3,2},{4,5},{5,4},{6,7},{7,6},{8,9},{9,8},{10,11... | collective-permute-start | bytes 9437192 | tf_op jit(solution)/shard_map/ppermute | solution.py:679
  37.5 73.5 %collective-permute-start.8 = (bf16[512,4096]{1,0:T(8,128)(2,1)}, bf16[512,4096]{1,0:T(8,128)(2,1)}, u32[]{:S(2)}, u32[]{:S(2)}) collective-permute-start(bf16[512,4096]{1,0:T(8,128)(2,1)} %refs_5_.3), channel_id=1, source_target_pairs={{0,1},{1,0},{2,3},{3,2},{4,5},{5,4},{6,7},{7,6},{8,9},{9,8},{10,11... | collective-permute-start | bytes 12582920 | tf_op jit(solution)/shard_map/ppermute | solution.py:679
  48.8 32.9 %collective-permute-start.3 = (bf16[192,1024]{1,0:T(8,128)(2,1)}, bf16[192,1024]{1,0:T(8,128)(2,1)S(1)}, u32[]{:S(2)}, u32[]{:S(2)}) collective-permute-start(bf16[192,1024]{1,0:T(8,128)(2,1)} %get-tuple-element.111.refs_0_), channel_id=1, source_target_pairs={{0,4},{2,6},{4,0},{6,2},{1,5},{3,7},{5,1},{7,3},{8,12},{10,14},{12... | collective-permute-start | bytes 1179656 | tf_op jit(solution)/shard_map/ppermute | solution.py:688
  50.9 35.9 %collective-permute-start.4 = (bf16[192,1024]{1,0:T(8,128)(2,1)}, bf16[192,1024]{1,0:T(8,128)(2,1)S(1)}, u32[]{:S(2)}, u32[]{:S(2)}) collective-permute-start(bf16[192,1024]{1,0:T(8,128)(2,1)} %get-tuple-element.111.refs_0_), channel_id=1, source_target_pairs={{0,2},{2,4},{4,6},{6,0},{1,3},{3,5},{5,7},{7,1},{8,10},{10,12},{12... | collective-permute-start | bytes 1179656 | tf_op jit(solution)/shard_map/ppermute | solution.py:688
  110.9 40.9 %collective-permute-start.12 = (bf16[192,1024]{1,0:T(8,128)(2,1)S(1)}, bf16[192,1024]{1,0:T(8,128)(2,1)S(1)}, u32[]{:S(2)}, u32[]{:S(2)}) collective-permute-start(bf16[192,1024]{1,0:T(8,128)(2,1)S(1)} %bitcast.80), channel_id=1, source_target_pairs={{0,1},{1,0},{2,3},{3,2},{4,5},{5,4},{6,7},{7,6},{8,9},{9,8},{10,11... | collective-permute-start | bytes 1179656 | tf_op jit(solution)/shard_map/ppermute | solution.py:679
  153.9 19.6 %collective-permute-start.11 = (bf16[192,1024]{1,0:T(8,128)(2,1)S(1)}, bf16[192,1024]{1,0:T(8,128)(2,1)S(1)}, u32[]{:S(2)}, u32[]{:S(2)}) collective-permute-start(bf16[192,1024]{1,0:T(8,128)(2,1)S(1)} %get-tuple-element.231), channel_id=1, source_target_pairs={{0,6},{2,0},{4,2},{6,4},{1,7},{3,1},{5,3},{7,5},{8,14},{10,8},{12,... | collective-permute-start | bytes 1179656 | tf_op jit(solution)/shard_map/ppermute | solution.py:688
  153.9 34.4 %collective-permute-start.10 = (bf16[192,1024]{1,0:T(8,128)(2,1)S(1)}, bf16[192,1024]{1,0:T(8,128)(2,1)S(1)}, u32[]{:S(2)}, u32[]{:S(2)}) collective-permute-start(bf16[192,1024]{1,0:T(8,128)(2,1)S(1)} %get-tuple-element.232), channel_id=1, source_target_pairs={{0,4},{2,6},{4,0},{6,2},{1,5},{3,7},{5,1},{7,3},{8,12},{10,14},{12... | collective-permute-start | bytes 1179656 | tf_op jit(solution)/shard_map/ppermute | solution.py:688
  154.0 34.3 %collective-permute-start.9 = (bf16[192,1024]{1,0:T(8,128)(2,1)S(1)}, bf16[192,1024]{1,0:T(8,128)(2,1)S(1)}, u32[]{:S(2)}, u32[]{:S(2)}) collective-permute-start(bf16[192,1024]{1,0:T(8,128)(2,1)S(1)} %get-tuple-element.233), channel_id=1, source_target_pairs={{0,2},{2,4},{4,6},{6,0},{1,3},{3,5},{5,7},{7,1},{8,10},{10,12},{12... | collective-permute-start | bytes 1179656 | tf_op jit(solution)/shard_map/ppermute | solution.py:688
  169.2 28.3 %collective-permute-start.24 = (bf16[1024,512]{1,0:T(8,128)(2,1)}, bf16[1024,512]{1,0:T(8,128)(2,1)}, u32[]{:S(2)}, u32[]{:S(2)}) collective-permute-start(bf16[1024,512]{1,0:T(8,128)(2,1)} %convolution_convert_fusion.2), channel_id=1, source_target_pairs={{0,8},{8,0},{16,24},{24,16},{1,9},{9,1},{17,25},{25,17},{2,10},{10... | collective-permute-start | bytes 3145736 | tf_op jit(solution)/shard_map/ppermute | solution.py:682
  170.7 33.2 %collective-permute-start.17 = (bf16[192,4096]{1,0:T(8,128)(2,1)}, bf16[192,4096]{1,0:T(8,128)(2,1)}, u32[]{:S(2)}, u32[]{:S(2)}) collective-permute-start(bf16[192,4096]{1,0:T(8,128)(2,1)} %get-tuple-element.147), channel_id=1, source_target_pairs={{0,1},{1,0},{2,3},{3,2},{4,5},{5,4},{6,7},{7,6},{8,9},{9,8},{10,11... | collective-permute-start | bytes 4718600 | tf_op jit(solution)/shard_map/ppermute | solution.py:679
  173.5 25.8 %collective-permute-start.23 = (bf16[1024,512]{1,0:T(8,128)(2,1)}, bf16[1024,512]{1,0:T(8,128)(2,1)}, u32[]{:S(2)}, u32[]{:S(2)}) collective-permute-start(bf16[1024,512]{1,0:T(8,128)(2,1)} %convolution_convert_fusion.3), channel_id=1, source_target_pairs={{0,16},{8,24},{16,0},{24,8},{1,17},{9,25},{17,1},{25,9},{2,18},{10... | collective-permute-start | bytes 3145736 | tf_op jit(solution)/shard_map/ppermute | solution.py:685
  215.6 29.5 %collective-permute-start.28 = (bf16[256,2560]{1,0:T(8,128)(2,1)}, bf16[256,2560]{1,0:T(8,128)(2,1)}, u32[]{:S(2)}, u32[]{:S(2)}) collective-permute-start(bf16[256,2560]{1,0:T(8,128)(2,1)} %pad_maximum_fusion.4), channel_id=1, source_target_pairs={{0,16},{8,24},{16,0},{24,8},{1,17},{9,25},{17,1},{25,9},{2,18},{10... | collective-permute-start | bytes 3932168 | tf_op jit(solution)/shard_map/ppermute | solution.py:685
  219.3 30.0 %collective-permute-start.26 = (bf16[256,2560]{1,0:T(8,128)(2,1)}, bf16[256,2560]{1,0:T(8,128)(2,1)}, u32[]{:S(2)}, u32[]{:S(2)}) collective-permute-start(bf16[256,2560]{1,0:T(8,128)(2,1)} %pad_maximum_fusion.3), channel_id=1, source_target_pairs={{0,8},{8,0},{16,24},{24,16},{1,9},{9,1},{17,25},{25,17},{2,10},{10... | collective-permute-start | bytes 3932168 | tf_op jit(solution)/shard_map/ppermute | solution.py:682
  219.9 50.3 %collective-permute-start.19 = (bf16[2,768,1024]{2,1,0:T(8,128)(2,1)S(1)}, bf16[2,768,1024]{2,1,0:T(8,128)(2,1)}, u32[]{:S(2)}, u32[]{:S(2)}) collective-permute-start(bf16[2,768,1024]{2,1,0:T(8,128)(2,1)S(1)} %copy-done.2), channel_id=1, source_target_pairs={{0,1},{1,0},{2,3},{3,2},{4,5},{5,4},{6,7},{7,6},{8,9},{9,8},{10,11... | collective-permute-start | bytes 9437192 | tf_op jit(solution)/shard_map/ppermute | solution.py:679
  224.0 33.4 %all-to-all-start = ((bf16[4,512,256]{2,1,0:T(8,128)(2,1)}), bf16[4,512,256]{2,1,0:T(8,128)(2,1)}, u32[]{:S(2)}, u32[]{:S(2)}) async-start(bf16[4,512,256]{2,1,0:T(8,128)(2,1)} %bitcast.96), calls=%async_computation | async-start | bytes 2097152 | tf_op jit(solution)/shard_map/all_to_all | solution.py:696
  261.5 29.1 %all-to-all-start.1 = ((bf16[4,512,256]{2,1,0:T(8,128)(2,1)}), bf16[4,512,256]{2,1,0:T(8,128)(2,1)}, u32[]{:S(2)}, u32[]{:S(2)}) async-start(bf16[4,512,256]{2,1,0:T(8,128)(2,1)} %broadcast_in_dim.18), calls=%async_computation.1 | async-start | bytes 2097152 | tf_op jit(solution)/shard_map/all_to_all | solution.py:696
  280.6 19.8 %collective-permute-start.30 = (bf16[256,1536]{0,1:T(8,128)(2,1)}, bf16[256,1536]{0,1:T(8,128)(2,1)}, u32[]{:S(2)}, u32[]{:S(2)}) collective-permute-start(bf16[256,1536]{0,1:T(8,128)(2,1)} %pad_maximum_fusion.8), channel_id=1, source_target_pairs={{0,16},{8,24},{16,0},{24,8},{1,17},{9,25},{17,1},{25,9},{2,18},{10... | collective-permute-start | bytes 2359304 | tf_op jit(solution)/shard_map/ppermute | solution.py:685
  282.5 19.6 %collective-permute-start.32 = (bf16[256,1536]{0,1:T(8,128)(2,1)}, bf16[256,1536]{0,1:T(8,128)(2,1)}, u32[]{:S(2)}, u32[]{:S(2)}) collective-permute-start(bf16[256,1536]{0,1:T(8,128)(2,1)} %pad_maximum_fusion.9), channel_id=1, source_target_pairs={{0,8},{8,0},{16,24},{24,16},{1,9},{9,1},{17,25},{25,17},{2,10},{10... | collective-permute-start | bytes 2359304 | tf_op jit(solution)/shard_map/ppermute | solution.py:682
  290.6 37.1 %all-to-all-start.2 = ((bf16[4,128,1280]{2,1,0:T(8,128)(2,1)}), bf16[4,128,1280]{2,1,0:T(8,128)(2,1)}, u32[]{:S(2)}, u32[]{:S(2)}) async-start(bf16[4,128,1280]{2,1,0:T(8,128)(2,1)} %bitcast.83), calls=%async_computation.2 | async-start | bytes 2621440 | tf_op jit(solution)/shard_map/all_to_all | solution.py:696
  295.0 19.5 %collective-permute-start.22 = (bf16[192,1024]{1,0:T(8,128)(2,1)}, bf16[192,1024]{1,0:T(8,128)(2,1)S(1)}, u32[]{:S(2)}, u32[]{:S(2)}) collective-permute-start(bf16[192,1024]{1,0:T(8,128)(2,1)} %get-tuple-element.152.gz), channel_id=1, source_target_pairs={{0,1},{1,0},{2,3},{3,2},{4,5},{5,4},{6,7},{7,6},{8,9},{9,8},{10,11... | collective-permute-start | bytes 1179656 | tf_op jit(solution)/shard_map/ppermute | solution.py:679
  311.2 27.4 %collective-permute-start.33 = (bf16[256,768]{0,1:T(8,128)(2,1)}, bf16[256,768]{0,1:T(8,128)(2,1)}, u32[]{:S(2)}, u32[]{:S(2)}) collective-permute-start(bf16[256,768]{0,1:T(8,128)(2,1)} %pad_maximum_fusion.17), channel_id=1, source_target_pairs={{0,8},{8,0},{16,24},{24,16},{1,9},{9,1},{17,25},{25,17},{2,10},{10... | collective-permute-start | bytes 1179656 | tf_op jit(solution)/shard_map/ppermute | solution.py:682
  312.9 25.7 %collective-permute-start.35 = (bf16[256,768]{0,1:T(8,128)(2,1)}, bf16[256,768]{0,1:T(8,128)(2,1)}, u32[]{:S(2)}, u32[]{:S(2)}) collective-permute-start(bf16[256,768]{0,1:T(8,128)(2,1)} %pad_maximum_fusion.18), channel_id=1, source_target_pairs={{0,16},{8,24},{16,0},{24,8},{1,17},{9,25},{17,1},{25,9},{2,18},{10... | collective-permute-start | bytes 1179656 | tf_op jit(solution)/shard_map/ppermute | solution.py:685
  332.2 36.3 %all-to-all-start.3 = ((bf16[4,128,1280]{2,1,0:T(8,128)(2,1)}), bf16[4,128,1280]{2,1,0:T(8,128)(2,1)}, u32[]{:S(2)}, u32[]{:S(2)}) async-start(bf16[4,128,1280]{2,1,0:T(8,128)(2,1)} %broadcast_in_dim.19), calls=%async_computation.3 | async-start | bytes 2621440 | tf_op jit(solution)/shard_map/all_to_all | solution.py:696
  362.9 23.7 %collective-permute-start.40 = (bf16[2048,256]{1,0:T(8,128)(2,1)}, bf16[2048,256]{1,0:T(8,128)(2,1)S(1)}, u32[]{:S(2)}, u32[]{:S(2)}) collective-permute-start(bf16[2048,256]{1,0:T(8,128)(2,1)} %bitcast.27.own), channel_id=1, source_target_pairs={{0,8},{8,0},{16,24},{24,16},{1,9},{9,1},{17,25},{25,17},{2,10},{10... | collective-permute-start | bytes 3145736 | tf_op jit(solution)/shard_map/ppermute | solution.py:682
  363.2 23.6 %collective-permute-start.39 = (bf16[2048,256]{1,0:T(8,128)(2,1)}, bf16[2048,256]{1,0:T(8,128)(2,1)}, u32[]{:S(2)}, u32[]{:S(2)}) collective-permute-start(bf16[2048,256]{1,0:T(8,128)(2,1)} %bitcast.27.own), channel_id=1, source_target_pairs={{0,16},{8,24},{16,0},{24,8},{1,17},{9,25},{17,1},{25,9},{2,18},{10... | collective-permute-start | bytes 3145736 | tf_op jit(solution)/shard_map/ppermute | solution.py:685
  369.4 34.5 %all-to-all-start.4 = ((bf16[4,128,768]{1,2,0:T(8,128)(2,1)}), bf16[4,128,768]{1,2,0:T(8,128)(2,1)S(1)}, u32[]{:S(2)}, u32[]{:S(2)}) async-start(bf16[4,128,768]{1,2,0:T(8,128)(2,1)} %copy.75), calls=%async_computation.4 | async-start | bytes 1572864 | tf_op jit(solution)/shard_map/all_to_all | solution.py:696
  400.8 30.0 %collective-permute-start.44 = (bf16[512,1280]{1,0:T(8,128)(2,1)}, bf16[512,1280]{1,0:T(8,128)(2,1)S(1)}, u32[]{:S(2)}, u32[]{:S(2)}) collective-permute-start(bf16[512,1280]{1,0:T(8,128)(2,1)} %bitcast.26.own), channel_id=1, source_target_pairs={{0,16},{8,24},{16,0},{24,8},{1,17},{9,25},{17,1},{25,9},{2,18},{10... | collective-permute-start | bytes 3932168 | tf_op jit(solution)/shard_map/ppermute | solution.py:685
  402.2 26.6 %collective-permute-start.42 = (bf16[512,1280]{1,0:T(8,128)(2,1)}, bf16[512,1280]{1,0:T(8,128)(2,1)}, u32[]{:S(2)}, u32[]{:S(2)}) collective-permute-start(bf16[512,1280]{1,0:T(8,128)(2,1)} %bitcast.26.own), channel_id=1, source_target_pairs={{0,8},{8,0},{16,24},{24,16},{1,9},{9,1},{17,25},{25,17},{2,10},{10... | collective-permute-start | bytes 3932168 | tf_op jit(solution)/shard_map/ppermute | solution.py:682
  405.3 28.4 %all-to-all-start.5 = ((bf16[4,128,768]{2,1,0:T(8,128)(2,1)}), bf16[4,128,768]{2,1,0:T(8,128)(2,1)S(1)}, u32[]{:S(2)}, u32[]{:S(2)}) async-start(bf16[4,128,768]{2,1,0:T(8,128)(2,1)} %broadcast_in_dim.20), calls=%async_computation.5 | async-start | bytes 1572864 | tf_op jit(solution)/shard_map/all_to_all | solution.py:696
  411.0 26.3 %collective-permute-start.47 = (f32[1,5632]{1,0:T(1,128)}, f32[1,5632]{1,0:T(1,128)}, u32[]{:S(2)}, u32[]{:S(2)}) collective-permute-start(f32[1,5632]{1,0:T(1,128)} %constant_dynamic-slice_fusion), channel_id=1, source_target_pairs={{0,1},{1,0},{2,3},{3,2},{4,5},{5,4},{6,7},{7,6},{8,9},{9,8},{10,11... | collective-permute-start | bytes 67592 | tf_op jit(solution)/shard_map/ppermute | solution.py:679
  433.6 23.3 %all-to-all-start.6 = ((bf16[4,256,256]{2,1,0:T(8,128)(2,1)}), bf16[4,256,256]{2,1,0:T(8,128)(2,1)S(1)}, u32[]{:S(2)}, u32[]{:S(2)}) async-start(bf16[4,256,256]{2,1,0:T(8,128)(2,1)} %bitcast.21), calls=%async_computation.6 | async-start | bytes 1048576 | tf_op jit(solution)/shard_map/all_to_all | solution.py:696
  457.8 27.9 %all-to-all-start.7 = ((bf16[4,256,256]{2,1,0:T(8,128)(2,1)}), bf16[4,256,256]{2,1,0:T(8,128)(2,1)S(1)}, u32[]{:S(2)}, u32[]{:S(2)}) async-start(bf16[4,256,256]{2,1,0:T(8,128)(2,1)} %broadcast_in_dim.42), calls=%async_computation.7 | async-start | bytes 1048576 | tf_op jit(solution)/shard_map/all_to_all | solution.py:696
  (145 other events, 868.5 us)

commit v3 on v2

v3 whole, which is shorter than its diff:
```python
import functools

import jax
import jax.numpy as jnp
from jax import lax
from jax.experimental import pallas as pl
from jax.experimental.pallas import tpu as pltpu
from jax.sharding import PartitionSpec as P

HEADS = 16
HD = 64
UTTS = 3
EPS = 1e-05
MASKED = 1e12
BF16 = jnp.bfloat16
F32 = jnp.float32
INV_SQRT2 = 0.7071067811865476
INV_SQRT_2PI = 0.3989422804014327
ERFC_STEP = 0.4
ERFC_TERMS = (
    0.22567586186829244 / 2,
    0.22566960544571626 / 2,
    0.20784251123900896 / 2,
    0.16854379658168633 / 2,
    0.14142295790506823 / 2,
    -0.005586494604590357 / 2,
    0.16905696704198306 / 2,
    -0.18288169574958996 / 2,
    0.05025661354969599 / 2,
)


def contract_rows(left_side, right_side):
    return lax.dot_general(
        left_side, right_side, (((0,), (0,)), ((), ())), preferred_element_type=F32
    )


def times_transposed(left_side, right_side):
    return lax.dot_general(
        left_side, right_side, (((1,), (1,)), ((), ())), preferred_element_type=F32
    )


def times(left_side, right_side):
    return jnp.dot(left_side, right_side, preferred_element_type=F32)


def ordered(kernel, count, after):
    n = len(after)

    def run(*refs):
        kernel(*refs[:count], *refs[count + n :])

    return run, [pl.BlockSpec(memory_space=pl.ANY)] * n


TURNS = (0, 1, 3, 2)


def turn(block, plane):
    bits = block ^ plane
    return bits ^ (bits >> 1)


def put_turned(part, read, plane):
    block = part.shape[-1] // len(TURNS)
    for i, bits in enumerate(TURNS):
        at = pl.multiple_of((plane ^ bits) * block, 128)
        part[:, i * block : (i + 1) * block] = read(at, block)


def pair_rows(block, lane):
    zero = jnp.zeros_like(block)
    return jnp.concatenate(
        [jnp.where(lane < HD, block, zero), jnp.where(lane >= HD, block, zero)], axis=0
    )


def utterance_ends(meta):
    ends = [meta[3]]
    for j in range(1, UTTS):
        ends.append(ends[-1] + meta[3 + j])
    return ends


def attend_forward_kernel(meta, q_ref, k_ref, v_ref, out_ref, prob_ref, dist):
    tok = q_ref.shape[0]
    length = k_ref.shape[0]
    shard = meta[1]
    ends = utterance_ends(meta)

    @pl.when(pl.program_id(0) == 0)
    def _():
        row = lax.broadcasted_iota(jnp.int32, (length, 2 * tok), 0)
        col = lax.broadcasted_iota(jnp.int32, (length, 2 * tok), 1)
        k_pos = row + shard * tok
        k_pos = jnp.where(k_pos >= length, k_pos - length, k_pos)
        q_pos = jnp.where(col >= tok, col - tok, col) + shard * tok
        k_seg = jnp.zeros_like(k_pos)
        q_seg = jnp.zeros_like(q_pos)
        for j in range(UTTS):
            k_seg = k_seg + (k_pos >= ends[j]).astype(jnp.int32)
            q_seg = q_seg + (q_pos >= ends[j]).astype(jnp.int32)
        allowed = (k_seg == q_seg) & (k_seg < UTTS)
        dist[...] = jnp.where(allowed, jnp.abs(k_pos - q_pos).astype(F32), MASKED)

    lane = lax.broadcasted_iota(jnp.int32, (tok, 2 * HD), 1)
    pair = pair_rows(q_ref[...] * jnp.asarray(HD**-0.5, BF16), lane)
    head = 2 * pl.program_id(0) + 1 + (lax.broadcasted_iota(jnp.int32, (1, 2 * tok), 1) >= tok)
    slope = jnp.exp2(head.astype(F32) * (-8.0 / HEADS))
    scores = times_transposed(k_ref[...], pair) - slope * dist[...]
    top = jnp.max(scores, axis=0, keepdims=True)
    exp_scores = jnp.exp(scores - top)
    total = jnp.sum(exp_scores, axis=0, keepdims=True)
    prob = (exp_scores * (1.0 / total)).astype(BF16)
    prob_ref[0] = prob
    mixed = times(v_ref[...].T, prob).T
    mixed = jnp.where(lane < HD, mixed[:tok], mixed[tok:])
    row = lax.broadcasted_iota(jnp.int32, (tok, 2 * HD), 0) + shard * tok
    out_ref[...] = jnp.where(row < ends[UTTS - 1], mixed, 0.0).astype(BF16)


def attend_backward_kernel(q_ref, k_ref, v_ref, grad_ref, prob_ref, out_ref):
    tok = q_ref.shape[0]
    lane = lax.broadcasted_iota(jnp.int32, (tok, 2 * HD), 1)
    scale = jnp.asarray(HD**-0.5, BF16)
    pair_q = pair_rows(q_ref[...] * scale, lane)
    pair_g = pair_rows(grad_ref[...], lane)
    prob_low = prob_ref[0]
    prob = prob_low.astype(F32)
    prob_grad = times_transposed(v_ref[...], pair_g)
    weighted = prob * prob_grad
    delta = jnp.sum(weighted, axis=0, keepdims=True)
    score_low = (weighted - prob * delta).astype(BF16)
    out_ref[2] = times(prob_low, pair_g).astype(BF16)
    out_ref[1] = times(score_low, pair_q).astype(BF16)
    mixed = times((k_ref[...] * scale).T, score_low).T
    out_ref[0, :tok] = jnp.where(lane < HD, mixed[:tok], mixed[tok:]).astype(BF16)
    out_ref[0, tok:] = jnp.zeros_like(out_ref[0, tok:])


def attend_forward(meta, queries, key_rows, value_rows, after=()):
    tok, width = queries.shape
    length = key_rows.shape[0]
    pairs = width // (2 * HD)
    kernel, waits = ordered(attend_forward_kernel, 4, after)
    return pl.pallas_call(
        kernel,
        grid_spec=pltpu.PrefetchScalarGridSpec(
            num_scalar_prefetch=1,
            grid=(pairs,),
            in_specs=[
                pl.BlockSpec((tok, 2 * HD), lambda g, m: (0, g)),
                pl.BlockSpec((length, 2 * HD), lambda g, m: (0, g)),
                pl.BlockSpec((length, 2 * HD), lambda g, m: (0, g)),
            ]
            + waits,
            out_specs=[
                pl.BlockSpec((tok, 2 * HD), lambda g, m: (0, g)),
                pl.BlockSpec((1, length, 2 * tok), lambda g, m: (g, 0, 0)),
            ],
            scratch_shapes=[pltpu.VMEM((length, 2 * tok), F32)],
        ),
        out_shape=[
            jax.ShapeDtypeStruct((tok, width), BF16),
            jax.ShapeDtypeStruct((pairs, length, 2 * tok), BF16),
        ],
        name="attend_forward",
    )(meta, queries, key_rows, value_rows, *after)


def attend_backward(queries, key_rows, value_rows, grad_heads, prob, after=()):
    tok, width = queries.shape
    length = key_rows.shape[0]
    pairs = width // (2 * HD)
    q_spec = pl.BlockSpec((tok, 2 * HD), lambda g: (0, g))
    k_spec = pl.BlockSpec((length, 2 * HD), lambda g: (0, g))
    kernel, waits = ordered(attend_backward_kernel, 5, after)
    return pl.pallas_call(
        kernel,
        grid=(pairs,),
        in_specs=[
            q_spec,
            k_spec,
            k_spec,
            q_spec,
            pl.BlockSpec((1, length, 2 * tok), lambda g: (g, 0, 0)),
        ]
        + waits,
        out_specs=pl.BlockSpec((3, length, 2 * HD), lambda g: (0, 0, g)),
        out_shape=jax.ShapeDtypeStruct((3, length, width), BF16),
        name="attend_backward",
    )(queries, key_rows, value_rows, grad_heads, prob, *after)


def statistics(values):
    mean = jnp.mean(values, axis=-1, keepdims=True)
    centred = values - mean
    variance = jnp.mean(centred * centred, axis=-1, keepdims=True)
    return centred, lax.rsqrt(variance + EPS)


def norm_back(unit, rstd, gain, grad):
    scaled = grad * gain
    mean_e = jnp.mean(scaled, axis=-1, keepdims=True)
    mean_eu = jnp.mean(scaled * unit, axis=-1, keepdims=True)
    return rstd * (scaled - mean_e - unit * mean_eu)


def bases(core, n_pieces, rows):
    if n_pieces == 1:
        return [0]
    return [pl.multiple_of(core * rows, 128), pl.multiple_of((1 - core) * rows, 128)]


def front_kernel(n, sizes, meta, *refs):
    x_refs, refs = refs[:2], refs[2:]
    w_refs, packs, outs = refs[:n], refs[n : 2 * n], refs[2 * n :]
    z_ref, n1_ref, own_ref, other_ref = outs
    step = pl.program_id(0)
    first = meta[0] == 0

    def vector(i):
        start = sum(sizes[:i])
        parts = [ref[:, start : start + sizes[i]].astype(F32) for ref in packs]
        low = jnp.where(first, parts[0], parts[1])
        high = jnp.where(first, parts[1], parts[0])
        return jnp.concatenate([low, high], axis=1)

    x, s = x_refs[0][...], x_refs[1][...]
    own = jnp.where(first, x, s)
    other = jnp.where(first, s, x)
    own_ref[...] = own
    other_ref[...] = other
    part = times(own, w_refs[0][...]) + times(other, w_refs[1][...])

    @pl.when(step == 0)
    def _():
        z_ref[...] = part + vector(0)

    @pl.when(step > 0)
    def _():
        z_ref[...] += part

    @pl.when(step == pl.num_programs(0) - 1)
    def _():
        centred, rstd = statistics(z_ref[...])
        n1_ref[...] = (centred * rstd * vector(1) + vector(2)).astype(BF16)


def front(meta, frames, skips, weights, packs, sizes, after=()):
    tok = frames.shape[0]
    rows, width = weights[0].shape
    n = len(weights)
    steps = 4
    block = rows // steps
    packed = pl.BlockSpec(packs[0].shape, lambda k, m: (0, 0))
    whole = pl.BlockSpec((tok, width), lambda k, m: (0, 0))
    columns = pl.BlockSpec((tok, block), lambda k, m: (0, k))
    turned = pl.BlockSpec((tok, block), lambda k, m: (0, turn(k, m[2])))
    kernel, waits = ordered(functools.partial(front_kernel, n, sizes), 3 + 2 * n, after)
    return pl.pallas_call(
        kernel,
        grid_spec=pltpu.PrefetchScalarGridSpec(
            num_scalar_prefetch=1,
            grid=(steps,),
            in_specs=[columns] * 2
            + [pl.BlockSpec((block, width), lambda k, m: (k, 0))] * n
            + [packed] * n
            + waits,
            out_specs=[whole, whole, turned, turned],
        ),
        out_shape=[
            jax.ShapeDtypeStruct((tok, width), F32),
            jax.ShapeDtypeStruct((tok, width), BF16),
            jax.ShapeDtypeStruct((tok, rows), BF16),
            jax.ShapeDtypeStruct((tok, rows), BF16),
        ],
        name="front",
    )(meta, frames, skips, *weights, *packs, *after)


def front_whole_kernel(x_ref, s_ref, first_ref, second_ref, bias, gain, shift, z_ref, n1_ref):
    step = pl.program_id(0)
    part = times(x_ref[...], first_ref[...]) + times(s_ref[...], second_ref[...])

    @pl.when(step == 0)
    def _():
        z_ref[...] = part + bias[...]

    @pl.when(step > 0)
    def _():
        z_ref[...] += part

    @pl.when(step == pl.num_programs(0) - 1)
    def _():
        centred, rstd = statistics(z_ref[...])
        n1_ref[...] = (centred * rstd * gain[...] + shift[...]).astype(BF16)


def front_whole(frames, skips, weight, bias, gain, shift):
    tok, width = frames.shape
    steps = 4
    block = width // steps
    vector = pl.BlockSpec((1, width), lambda k: (0, 0))
    whole = pl.BlockSpec((tok, width), lambda k: (0, 0))
    return pl.pallas_call(
        front_whole_kernel,
        grid=(steps,),
        in_specs=[pl.BlockSpec((tok, block), lambda k: (0, k))] * 2
        + [
            pl.BlockSpec((block, width), lambda k: (k, 0)),
            pl.BlockSpec((block, width), lambda k: (k + steps, 0)),
        ]
        + [vector] * 3,
        out_specs=[whole, whole],
        out_shape=[
            jax.ShapeDtypeStruct((tok, width), F32),
            jax.ShapeDtypeStruct((tok, width), BF16),
        ],
        name="front",
    )(frames, skips, weight, weight, bias, gain, shift)


def project_kernel(n, chunks, meta, *refs):
    x_refs = refs[:chunks]
    w_refs = refs[chunks : chunks + 3 * n]
    q_ref, k_ref, v_ref = refs[chunks + 3 * n : chunks + 3 * n + 3]
    parts = refs[chunks + 3 * n + 3 :]
    rows = w_refs[0].shape[0]
    tok = q_ref.shape[0]
    starts = bases(meta[0], n, rows)

    @pl.when(pl.program_id(0) == 0)
    def _():
        for start, part in zip(starts, parts):
            for c in range(chunks):
                if n == 1:
                    part[c * tok : (c + 1) * tok] = x_refs[c][...]
                    continue
                put_turned(
                    part.at[c * tok : (c + 1) * tok],
                    lambda at, block: x_refs[c][:, pl.ds(pl.multiple_of(start + at, 128), block)],
                    meta[2],
                )

    for c in range(chunks):
        for i, out in enumerate((q_ref, k_ref, v_ref)):
            if i == 0 and c > 0:
                continue
            total = None
            for p, start in enumerate(starts):
                term = times(x_refs[c][:, pl.ds(start, rows)], w_refs[3 * p + i][...])
                total = term if total is None else total + term
            out[c * tok : (c + 1) * tok] = total.astype(BF16)


def project(meta, chunks, weights, after=()):
    tok, width = chunks[0].shape
    rows = weights[0].shape[0]
    n = len(weights)
    tile = 256
    tiles = width // tile

    def w_spec(i):
        return pl.BlockSpec((rows, tile), lambda t, m: (0, t + i * tiles))

    length = tok * len(chunks)
    kernel, waits = ordered(
        functools.partial(project_kernel, n, len(chunks)), 1 + len(chunks) + 3 * n, after
    )
    return pl.pallas_call(
        kernel,
        grid_spec=pltpu.PrefetchScalarGridSpec(
            num_scalar_prefetch=1,
            grid=(tiles,),
            in_specs=[pl.BlockSpec((tok, width), lambda t, m: (0, 0))] * len(chunks)
            + [w_spec(i) for i in range(3)] * n
            + waits,
            out_specs=[
                pl.BlockSpec((tok, tile), lambda t, m: (0, t)),
                pl.BlockSpec((length, tile), lambda t, m: (0, t)),
                pl.BlockSpec((length, tile), lambda t, m: (0, t)),
            ]
            + [pl.BlockSpec((length, rows), lambda t, m: (0, 0))] * n,
        ),
        out_shape=[
            jax.ShapeDtypeStruct((tok, width), BF16),
            jax.ShapeDtypeStruct((length, width), BF16),
            jax.ShapeDtypeStruct((length, width), BF16),
        ]
        + [jax.ShapeDtypeStruct((length, rows), BF16)] * n,
        name="project",
    )(meta, *chunks, *[w for w in weights for _ in range(3)], *after)


def centre_kernel(n, meta, *refs):
    refs = list(refs)

    def take(count):
        taken = refs[:count]
        del refs[:count]
        return taken

    att, z_ref, cotan = take(3)
    w_out, w_up, gact = take(n), take(n), take(n)
    up_bias, out_bias, gain, shift = take(4)
    resid, gup_ref, gres, gbranch, gatt, up_sum, sums = take(7)
    acts, n2_parts, att_parts = take(n), take(n), take(n)
    n2, gn2, unit, rstd = refs
    step, steps = pl.program_id(0), pl.num_programs(0)
    tok = att.shape[0]
    core, live = meta[0], utterance_ends(meta)[-1] - meta[1] * tok
    rows = w_out[0].shape[0]
    starts = bases(core, n, rows)

    @pl.when(step == 0)
    def _():
        total = z_ref[...] + out_bias[...]
        for start, w_ref, part in zip(starts, w_out, att_parts):
            total = total + times(att[:, pl.ds(start, rows)], w_ref[...])
        resid[...] = total
        centred, scale = statistics(total)
        unit[...] = centred * scale
        rstd[...] = scale
        n2[...] = (unit[...] * gain[...] + shift[...]).astype(BF16)
        for start, n2_part, att_part in zip(starts, n2_parts, att_parts):
            for part, source in ((n2_part, n2), (att_part, att)):
                if n == 1:
                    part[...] = source[...]
                    continue
                put_turned(
                    part,
                    lambda at, block: source[:, pl.ds(pl.multiple_of(start + at, 128), block)],
                    meta[2],
                )
        gn2[...] = jnp.zeros_like(gn2)

    pre = up_bias[...]
    for start, w_ref in zip(starts, w_up):
        pre = pre + times(n2[:, pl.ds(start, rows)], w_ref[...])
    gauss = jnp.exp(pre * pre * (-0.5))
    t = 1.0 / (1.0 + (ERFC_STEP * INV_SQRT2) * jnp.abs(pre))
    tail = jnp.full_like(t, ERFC_TERMS[-1])
    for term in ERFC_TERMS[-2::-1]:
        tail = tail * t + term
    tail = tail * t * gauss
    cdf = jnp.where(pre < 0.0, tail, 1.0 - tail)
    act = (pre * cdf).astype(BF16)
    if n == 1:
        acts[0][...] = act
        grad = gact[0][...]
    else:
        mine = (step // (steps // 2)) == core

        @pl.when(mine)
        def _():
            acts[0][...] = act

        @pl.when(jnp.logical_not(mine))
        def _():
            acts[1][...] = act

        grad = jnp.where(mine, gact[0][...], gact[1][...])
    gup = (grad * (cdf + pre * gauss * INV_SQRT_2PI)).astype(BF16)
    gup_ref[...] = gup
    up_sum[...] = jnp.sum(gup.astype(F32), axis=0, keepdims=True)
    for start, w_ref in zip(starts, w_up):
        gn2[:, pl.ds(start, rows)] += times_transposed(gup, w_ref[...])

    @pl.when(step == steps - 1)
    def _():
        grad_n2 = gn2[...]
        total = cotan[...].astype(F32) + norm_back(unit[...], rstd[...], gain[...], grad_n2)
        gres[...] = total
        low = total.astype(BF16)
        gbranch[...] = low
        alive = lax.broadcasted_iota(jnp.int32, (tok, 1), 0) < live
        for start, w_ref in zip(starts, w_out):
            term = times_transposed(low, w_ref[...])
            gatt[:, pl.ds(start, rows)] = jnp.where(alive, term, 0.0).astype(BF16)
        sums[0:1] = jnp.sum(low.astype(F32), axis=0, keepdims=True)
        sums[1:2] = jnp.sum(unit[...] * grad_n2, axis=0, keepdims=True)
        sums[2:3] = jnp.sum(grad_n2, axis=0, keepdims=True)
        sums[3:4] = jnp.sum(cotan[...].astype(F32), axis=0, keepdims=True)


def centre(meta, att, z, cotan, w_out, w_up, gact, up_bias, out_bias, gain, shift, after=(), tile=512):
    tok, width = att.shape
    n = len(w_out)
    rows = w_out[0].shape[0]
    hidden = w_up[0].shape[1]
    steps = hidden // tile
    per = steps // n
    assert n == 1 or per == len(TURNS)
    whole = pl.BlockSpec((tok, width), lambda t, m: (0, 0))
    vector = pl.BlockSpec((1, width), lambda t, m: (0, 0))
    tiled = pl.BlockSpec((tok, tile), lambda t, m: (0, t))

    def gact_spec(i, by_plane=False):
        def index(t, m):
            half = m[0] if i == 0 else 1 - m[0]
            at = jnp.clip(t - half * per, 0, per - 1)
            return (0, turn(at, m[2]) if by_plane else at)

        return tiled if n == 1 else pl.BlockSpec((tok, tile), index)

    low = jax.ShapeDtypeStruct((tok, width), BF16)
    wide = jax.ShapeDtypeStruct((tok, width), F32)
    part = pl.BlockSpec((tok, rows), lambda t, m: (0, 0))
    kernel, waits = ordered(functools.partial(centre_kernel, n), 8 + 3 * n, after)
    return pl.pallas_call(
        kernel,
        grid_spec=pltpu.PrefetchScalarGridSpec(
            num_scalar_prefetch=1,
            grid=(steps,),
            in_specs=[whole, whole, whole]
            + [pl.BlockSpec((rows, width), lambda t, m: (0, 0))] * n
            + [pl.BlockSpec((rows, tile), lambda t, m: (0, t))] * n
            + [gact_spec(i) for i in range(n)]
            + [pl.BlockSpec((1, tile), lambda t, m: (0, t)), vector, vector, vector]
            + waits,
            out_specs=[
                whole,
                tiled,
                whole,
                whole,
                whole,
                pl.BlockSpec((1, tile), lambda t, m: (0, t)),
                pl.BlockSpec((8, width), lambda t, m: (0, 0)),
            ]
            + [gact_spec(i, True) for i in range(n)]
            + [part] * (2 * n),
            scratch_shapes=[
                pltpu.VMEM((tok, width), BF16),
                pltpu.VMEM((tok, width), F32),
                pltpu.VMEM((tok, width), F32),
                pltpu.VMEM((tok, 1), F32),
            ],
        ),
        out_shape=[
            wide,
            jax.ShapeDtypeStruct((tok, hidden), BF16),
            wide,
            low,
            low,
            jax.ShapeDtypeStruct((1, hidden), F32),
            jax.ShapeDtypeStruct((8, width), F32),
        ]
        + [jax.ShapeDtypeStruct((tok, hidden // n), BF16)] * n
        + [jax.ShapeDtypeStruct((tok, rows), BF16)] * (2 * n),
        name="centre",
    )(meta, att, z, cotan, *w_out, *w_up, *gact, up_bias, out_bias, gain, shift, *after)


def unproject_kernel(n, meta, grads, *refs):
    w_refs, out, flat = refs[:n], refs[n], refs[n + 1]
    rows = w_refs[0].shape[0]
    width = grads.shape[2]
    for i in range(3):
        flat[:, i * width : (i + 1) * width] = grads[i]
    for start, w_ref in zip(bases(meta[0], n, rows), w_refs):
        term = times_transposed(grads[1], w_ref[:, width : 2 * width])
        term = term + times_transposed(grads[2], w_ref[:, 2 * width :])

        @pl.when(pl.program_id(0) == 0)
        def _():
            own = term + times_transposed(grads[0], w_ref[:, :width])
            out[0, :, pl.ds(start, rows)] = own.astype(BF16)

        @pl.when(pl.program_id(0) > 0)
        def _():
            out[0, :, pl.ds(start, rows)] = term.astype(BF16)


def unproject(meta, grads, weights, chunks, after=()):
    length, width = grads.shape[1:]
    tok = length // chunks
    rows = weights[0].shape[0]
    n = len(weights)
    kernel, waits = ordered(functools.partial(unproject_kernel, n), 2 + n, after)
    return pl.pallas_call(
        kernel,
        grid_spec=pltpu.PrefetchScalarGridSpec(
            num_scalar_prefetch=1,
            grid=(chunks,),
            in_specs=[pl.BlockSpec((3, tok, width), lambda c, m: (0, c, 0))]
            + [pl.BlockSpec((rows, 3 * width), lambda c, m: (0, 0))] * n
            + waits,
            out_specs=[
                pl.BlockSpec((1, tok, width), lambda c, m: (lax.rem(c + m[1], chunks), 0, 0)),
                pl.BlockSpec((tok, 3 * width), lambda c, m: (c, 0)),
            ],
        ),
        out_shape=[
            jax.ShapeDtypeStruct((chunks, tok, width), BF16),
            jax.ShapeDtypeStruct((length, 3 * width), BF16),
        ],
        name="unproject",
    )(meta, grads, *weights, *after)


def rear_kernel(parts, z_ref, gres, gain, gz_ref, sums):
    grad = parts[0].astype(F32)
    for i in range(1, parts.shape[0]):
        grad = grad + parts[i].astype(F32)
    centred, rstd = statistics(z_ref[...])
    unit = centred * rstd
    low = (gres[...] + norm_back(unit, rstd, gain[...], grad)).astype(BF16)
    gz_ref[...] = low
    sums[0:1] = jnp.sum(low.astype(F32), axis=0, keepdims=True)
    sums[1:2] = jnp.sum(unit * grad, axis=0, keepdims=True)
    sums[2:3] = jnp.sum(grad, axis=0, keepdims=True)


def rear(parts, z, gres, gain, after=()):
    tok, width = z.shape
    count = 4
    kernel, waits = ordered(rear_kernel, count, after)
    vmem = pl.BlockSpec(memory_space=pltpu.VMEM)
    return pl.pallas_call(
        kernel,
        in_specs=[vmem] * count + waits,
        out_specs=[vmem] * 2,
        out_shape=[
            jax.ShapeDtypeStruct((tok, width), BF16),
            jax.ShapeDtypeStruct((8, width), F32),
        ],
        name="rear",
    )(parts, z, gres, gain, *after)


def forward_kernel(resid, bias, own, other, w_own, w_other, out, total):
    step = pl.program_id(0)
    part = times(own[...], w_own[...]) + times(other[...], w_other[...])

    @pl.when(step == 0)
    def _():
        total[...] = resid[...] + bias[...] + part

    @pl.when(step > 0)
    def _():
        total[...] += part

    @pl.when(step == pl.num_programs(0) - 1)
    def _():
        out[...] = total[...].astype(BF16)


def forward(meta, resid, bias, acts, weights, after=()):
    tok, width = resid.shape
    steps = len(TURNS)
    rows = weights[0].shape[0] // steps
    whole = pl.BlockSpec((tok, width), lambda k, m: (0, 0))
    kernel, waits = ordered(
        lambda meta, *refs: forward_kernel(*refs), 7, after
    )
    return pl.pallas_call(
        kernel,
        grid_spec=pltpu.PrefetchScalarGridSpec(
            num_scalar_prefetch=1,
            grid=(steps,),
            in_specs=[whole, pl.BlockSpec((1, width), lambda k, m: (0, 0))]
            + [pl.BlockSpec((tok, rows), lambda k, m: (0, k))] * 2
            + [pl.BlockSpec((rows, width), lambda k, m: (m[2] ^ k ^ (k >> 1), 0))] * 2
            + waits,
            out_specs=whole,
            scratch_shapes=[pltpu.VMEM((tok, width), F32)],
        ),
        out_shape=jax.ShapeDtypeStruct((tok, width), BF16),
        name="forward",
    )(meta, resid, bias, *acts, *weights, *after)


def sort_sums_kernel(meta, late, early, wide, mine, theirs):
    rows = [late[i : i + 1] for i in range(3)] + [early[i : i + 1] for i in range(3)]
    rows = rows + [wide[...], early[3:4]]
    first = meta[0] == 0
    start = 0
    for row in rows:
        half = row.shape[1] // 2
        low, high = row[:, :half], row[:, half:]
        mine[:, start : start + half] = jnp.where(first, low, high)
        theirs[:, start : start + half] = jnp.where(first, high, low)
        start = start + half


def sort_sums(meta, late, early, wide, after=()):
    size = (7 * late.shape[1] + wide.shape[1]) // 2
    vmem = pl.BlockSpec(memory_space=pltpu.VMEM)
    kernel, waits = ordered(sort_sums_kernel, 4, after)
    return pl.pallas_call(
        kernel,
        in_specs=[pl.BlockSpec(memory_space=pltpu.SMEM), vmem, vmem, vmem] + waits,
        out_specs=[vmem] * 2,
        out_shape=[jax.ShapeDtypeStruct((1, size), F32)] * 2,
        name="sort_sums",
    )(meta, late, early, wide, *after)


def input_grads_kernel(n, meta, gz, first, second, input_ref, skip_ref):
    low = times_transposed(gz[...], first[...])
    high = times_transposed(gz[...], second[...])
    if n == 1:
        input_ref[...] = low
        skip_ref[...] = high
        return

    @pl.when(meta[0] == 0)
    def _():
        input_ref[...] = low
        skip_ref[...] = high

    @pl.when(meta[0] != 0)
    def _():
        input_ref[...] = high
        skip_ref[...] = low


def input_grads(meta, gz, weights, after=()):
    tok, width = gz.shape
    n = len(weights)
    steps = 4
    tile = width // steps
    if n == 1:
        weights = [weights[0], weights[0]]
    out = pl.BlockSpec((tok, tile), lambda t, m: (0, t))
    kernel, waits = ordered(functools.partial(input_grads_kernel, n), 4, after)
    return pl.pallas_call(
        kernel,
        grid_spec=pltpu.PrefetchScalarGridSpec(
            num_scalar_prefetch=1,
            grid=(steps,),
            in_specs=[
                pl.BlockSpec((tok, width), lambda t, m: (0, 0)),
                pl.BlockSpec((tile, width), lambda t, m: (t, 0)),
                pl.BlockSpec((tile, width), lambda t, m: (t + (steps if n == 1 else 0), 0)),
            ]
            + waits,
            out_specs=[out, out],
        ),
        out_shape=[jax.ShapeDtypeStruct((tok, width), F32)] * 2,
        name="input_grads",
    )(meta, gz, *weights, *after)


def pack_kernel(*refs):
    out = refs[-1]
    start = 0
    for ref in refs[:-1]:
        size = ref.shape[0]
        out[0, start : start + size] = ref[...]
        start = start + size


def pack(vectors):
    total = sum(v.shape[0] for v in vectors)
    return pl.pallas_call(
        pack_kernel, out_shape=jax.ShapeDtypeStruct((1, total), vectors[0].dtype), name="pack"
    )(*vectors)


def unpack_kernel(sizes, meta, own, other, *outs):
    start = 0
    for size, out in zip(sizes, outs):
        for ref, core in ((own, meta[0]), (other, 1 - meta[0])):
            at = pl.multiple_of(core * size, 128)
            out[:, pl.ds(at, size)] = ref[:, start : start + size].astype(F32)
        start = start + size


def unpack(meta, own, other, sizes, after=()):
    vmem = pl.BlockSpec(memory_space=pltpu.VMEM)
    kernel, waits = ordered(functools.partial(unpack_kernel, sizes), 3, after)
    return pl.pallas_call(
        kernel,
        in_specs=[pl.BlockSpec(memory_space=pltpu.SMEM), vmem, vmem] + waits,
        out_specs=[vmem] * len(sizes),
        out_shape=[jax.ShapeDtypeStruct((1, 2 * n), F32) for n in sizes],
        name="unpack",
    )(meta, own, other, *after)


def fold_kernel(terms, out):
    total = terms[0].astype(F32)
    for i in range(1, terms.shape[0]):
        total = total + terms[i].astype(F32)
    total = total.astype(BF16)
    for i in range(out.shape[0]):
        out[i] = total


def fold(terms, copies, after=()):
    n, rows, width = terms.shape
    tile = width
    while tile % 256 == 0 and tile > 1024:
        tile //= 2
    kernel, waits = ordered(fold_kernel, 1, after)
    return pl.pallas_call(
        kernel,
        grid=(width // tile,),
        in_specs=[pl.BlockSpec((n, rows, tile), lambda c: (0, 0, c))] + waits,
        out_specs=pl.BlockSpec((copies, rows, tile), lambda c: (0, 0, c)),
        out_shape=jax.ShapeDtypeStruct((copies, rows, width), BF16),
        name="fold",
    )(terms, *after)


def place_kernel(meta, own, by_x, by_y, far_low, far_high, out):
    part = pl.program_id(0)
    for i, ref in enumerate((own, by_x, by_y)):

        @pl.when(part == i)
        def _(ref=ref):
            out[...] = ref[...].astype(F32)

    @pl.when(part == 3)
    def _():
        half = far_low.shape[1]
        out[:, :half] = far_low[...].astype(F32)
        out[:, half:] = far_high[...].astype(F32)


def place(meta, parts, start, rows, after=()):
    width = parts[0].shape[1]
    tile = rows
    while start % tile or tile * width > 262144:
        tile //= 2
    base, steps = start // tile, rows // tile

    def spec(i, columns):
        def index(q, c, m):
            return (base + jnp.where(q == i, c, jnp.where(q < i, 0, steps - 1)), 0)

        return pl.BlockSpec((tile, columns), index)

    kernel, waits = ordered(place_kernel, 6, after)
    return pl.pallas_call(
        kernel,
        grid_spec=pltpu.PrefetchScalarGridSpec(
            num_scalar_prefetch=1,
            grid=(4, steps),
            in_specs=[spec(i, width) for i in range(3)] + [spec(3, width // 2)] * 2 + waits,
            out_specs=pl.BlockSpec((tile, width), lambda q, c, m: ((m[0] ^ q) * steps + c, 0)),
        ),
        out_shape=jax.ShapeDtypeStruct((4 * rows, width), F32),
        name="place",
    )(meta, *parts, *after)


class Links:
    def __init__(self):
        self.sent = {"x": [], "y": [], "z": [], "frames": []}

    def send(self, link, array, move, *pins):
        waits = [p for p in pins if p is not None]
        earlier = self.sent[link]
        depth = 2 if link in ("x", "y") else 1
        if len(earlier) >= depth:
            waits.append(earlier[-depth])
        if waits:
            array = tie(array, *waits)
        moved = move(array)
        earlier.append(moved)
        return moved


def tie(array, *others):
    return lax.optimization_barrier((array, *others))[0]


def body(
    frames_in,
    skip_in,
    lengths,
    cotangent,
    w_skip,
    w_qkv,
    w_out,
    w_up,
    w_down,
    skip_bias,
    norm1_gain,
    norm1_bias,
    out_bias,
    norm2_gain,
    norm2_bias,
    up_bias,
    down_bias,
):
    tok = frames_in.shape[3]
    width = frames_in.shape[4]
    frames = frames_in.reshape(tok, width)
    skips = skip_in.reshape(tok, width)
    cotan = cotangent.reshape(tok, width)
    n_batch = lax.axis_size("batch")
    n_seq = lax.axis_size("seq")
    n_frames = lax.axis_size("frames")
    assert n_batch == 4 and n_seq % 2 == 0
    paired = n_frames == 2
    plane = lax.axis_index("batch").astype(jnp.int32)
    shard = lax.axis_index("seq").astype(jnp.int32)
    core = lax.axis_index("frames").astype(jnp.int32)
    links = Links()

    def swap_frames(array):
        return lax.ppermute(array, "frames", [(0, 1), (1, 0)])

    def over_x(array):
        return lax.ppermute(array, "batch", [(i, i ^ 1) for i in range(n_batch)])

    def over_y(array):
        return lax.ppermute(array, "batch", [(i, i ^ 2) for i in range(n_batch)])

    def from_seq(step):
        return lambda array: lax.ppermute(
            array, "seq", [((i + step) % n_seq, i) for i in range(n_seq)]
        )

    def to_seq(step):
        return from_seq(n_seq - step)

    def exchange_seq(array):
        return lax.all_to_all(array, "seq", split_axis=0, concat_axis=0, tiled=True)

    def send_rows(array, *pins):
        if paired:
            return swap_frames(tie(array, *pins) if pins else array)
        return lax.all_gather(array, "frames", axis=0, tiled=True)

    def gather_frames(array, *pins):
        moved = send_rows(array, *pins)
        return [array, moved] if paired else [moved]

    def send_left(parts, *pins):
        if paired:
            return [parts[0], swap_frames(tie(parts[1], *pins) if pins else parts[1])]
        array = parts[0]
        split = array.reshape(array.shape[0], n_frames, array.shape[1] // n_frames)
        moved = lax.all_to_all(split, "frames", split_axis=1, concat_axis=0, tiled=True)
        return [moved.reshape(array.shape[0] * n_frames, array.shape[1] // n_frames)]

    def by_plane(source):
        block = source.shape[1] // n_batch
        return jnp.concatenate(
            [
                lax.dynamic_slice_in_dim(source, (plane ^ bits) * block, block, 1)
                for bits in TURNS
            ],
            axis=1,
        )

    def turned(sources):
        return stack(sources if paired else [by_plane(source) for source in sources])

    def stack(arrays):
        return arrays[0] if len(arrays) == 1 else jnp.concatenate(arrays, axis=0)

    class Chain:
        def __init__(self, terms):
            self.terms = terms
            self.half = terms[0][1][0].shape[1] // 2
            self.blocks = [lefts[0].shape[1] // n_batch for lefts, _ in terms]
            self.block = sum(self.blocks)

        def gemm(self, plane_blocks, low, high):
            whole = len(self.terms) == 1
            first, last = plane_blocks[0], plane_blocks[-1] + 1
            spans = [(first, last)] if whole else [(p, p + 1) for p in plane_blocks]
            outs = []
            for p, q in spans:
                for (lefts, rights), block in zip(self.terms, self.blocks):
                    total = None
                    for left, right in zip(lefts, rights):
                        term = contract_rows(
                            left[:, p * block : q * block], right[:, low:high]
                        )
                        total = term if total is None else total + term
                    outs.append(total)
            return stack(outs)

        def begin(self, *pins):
            half = self.half
            if pins:
                lefts, rights = self.terms[0]
                self.terms[0] = ([tie(lefts[0], *pins), *lefts[1:]], rights)
            self.to_x = self.gemm((1, 2), 0, half).astype(BF16)
            self.to_y = self.gemm((2, 3), half, 2 * half).astype(BF16)
            return self.to_x, self.to_y

        def first(self, *pins):
            self.from_x = links.send("x", self.to_x, over_x, *pins)
            self.from_y = links.send("y", self.to_y, over_y, *pins)

        def between(self, *pins):
            half, block = self.half, self.block
            from_x, from_y = self.from_x, self.from_y
            if pins:
                from_x, from_y = tie(from_x, *pins), tie(from_y, *pins)
            low = self.gemm((3,), 0, half) + from_x[block:].astype(F32)
            high = self.gemm((1,), half, 2 * half) + from_y[:block].astype(F32)
            self.next_y, self.next_x = low.astype(BF16), high.astype(BF16)
            return self.next_x, self.next_y

        def second(self, *pins):
            self.then_y = links.send("y", self.next_y, over_y, *pins)
            self.then_x = links.send("x", self.next_x, over_x, *pins)

        def own_sum(self, *pins):
            block, half = self.block, self.half
            then_x, then_y = self.then_x, self.then_y
            if pins:
                then_x, then_y = tie(then_x, *pins), tie(then_y, *pins)
            low = self.from_x[:block].astype(F32) + then_y.astype(F32)
            high = self.from_y[block:].astype(F32) + then_x.astype(F32)
            own = self.gemm((0,), 0, 2 * half) + jnp.concatenate([low, high], axis=1)
            self.own = own.astype(BF16).reshape(n_seq, block // n_seq, 2 * half)
            return self.own

        def across(self, *pins):
            self.terms_seq = links.send("z", self.own, exchange_seq, *pins)

        def along(self, after=(), *pins):
            self.folded = fold(self.terms_seq, n_seq, after)
            whole = links.send("z", self.folded, exchange_seq, *pins)
            self.whole = whole.reshape(self.block, 2 * self.half)
            return self.folded

        def spread(self, *pins):
            self.by_x = links.send("x", self.whole, over_x, *pins)
            self.by_y = links.send("y", self.whole, over_y, *pins)

        def finish(self, *pins):
            half = self.half
            self.far_low = links.send("x", self.by_y[:, :half], over_x, *pins)
            self.far_high = links.send("y", self.by_x[:, half:], over_y, *pins)

        def place(self, after=()):
            parts = (self.whole, self.by_x, self.by_y, self.far_low, self.far_high)
            starts = [sum(self.blocks[:i]) for i in range(len(self.blocks))]
            return [
                place(plane.reshape(1), parts, start, rows, after)
                for start, rows in zip(starts, self.blocks)
            ]

    vectors_in = (
        skip_bias,
        norm1_gain,
        norm1_bias,
        out_bias,
        norm2_gain,
        norm2_bias,
        up_bias,
        down_bias,
    )
    sizes = [v.shape[0] for v in vectors_in]
    starts = [sum(sizes[:i]) for i in range(len(sizes))]
    packed = pack(vectors_in)
    meta = jnp.concatenate([jnp.stack([core, shard, plane]), lengths.reshape(-1)])
    full_skip = gather_frames(w_skip, packed)

    if paired:
        packs = [packed, swap_frames(packed)]
        full_qkv = gather_frames(w_qkv, full_skip[1])
        full_down = gather_frames(w_down, full_skip[1])
        hidden_z, n1, own_in, other_in = front(
            meta, frames, skips, full_skip, packs, tuple(sizes)
        )
        vectors = unpack(meta, *packs, sizes, after=(n1,))
        inputs = [own_in, other_in]
    else:
        packed = lax.all_gather(packed, "frames", axis=0, tiled=True).astype(F32)
        vectors = [packed[:, b : b + n].reshape(1, -1) for b, n in zip(starts, sizes)]
        hidden_z, n1 = front_whole(frames, skips, full_skip[0], *vectors[:3])
        inputs = [jnp.concatenate([frames, skips], axis=1)]
        full_qkv, full_down = gather_frames(w_qkv), gather_frames(w_down)
    obias, gain2, bias2, ubias, dbias = vectors[3:]
    gain1 = vectors[1]
    n1_all = [n1] + [from_seq(j)(n1) for j in range(1, n_seq)]
    full_up = gather_frames(w_up, full_down[-1], n1)
    gact = [times_transposed(tie(cotan, n1), full_down[0])]
    if paired:
        gact.append(times_transposed(tie(cotan, gact[0]), full_down[1]))
    queries, key_rows, value_rows, *n1_parts = project(
        meta, n1_all, full_qkv, after=(*gact, gain1)
    )
    full_out = gather_frames(w_out, queries)
    both_cotan = [cotan, swap_frames(tie(cotan, queries))] if paired else None
    if not paired:
        both_cotan = [lax.all_gather(cotan, "frames", axis=0, tiled=True)]
    left_n1 = send_left(n1_parts)
    attended, prob = attend_forward(meta, queries, key_rows, value_rows)
    both_cotan = stack(both_cotan)
    left_n1 = left_n1 if paired else [by_plane(a) for a in left_n1]
    (
        resid,
        gup,
        grad_resid,
        grad_branch,
        grad_heads,
        up_sum,
        sums2,
        *parts,
    ) = centre(
        meta,
        attended,
        hidden_z,
        cotan,
        full_out,
        full_up,
        gact,
        ubias,
        obias,
        gain2,
        bias2,
        after=(both_cotan, *left_n1),
    )
    n = len(full_out)
    acts, n2_parts, att_parts = parts[:n], parts[n : 2 * n], parts[2 * n :]

    def right_rows(array, *pins):
        moved = send_rows(array, *pins)
        return stack([array, moved] if paired else [moved])

    down = Chain([([turned(send_left(acts))], [both_cotan])])
    down_first = down.begin()
    down.first()
    both_up = right_rows(gup)
    left_n2 = turned(send_left(n2_parts))
    grads = attend_backward(queries, key_rows, value_rows, grad_heads, prob, after=down_first)
    up = Chain([([left_n2], [both_up])])
    terms_n1, flat = unproject(meta, grads, full_qkv, n_seq, after=down_first)
    down_second = down.between(flat)
    down.second()
    up_first = up.begin(*down_second)
    up.first()
    terms_n1 = links.send("z", terms_n1, exchange_seq)
    both_flat = gather_frames(flat, *up_first)
    qkv = Chain([(left_n1, both_flat)])
    down_own = down.own_sum(*up_first)
    grad_z, sums1 = rear(
        terms_n1, hidden_z, grad_resid, gain1, after=(down_own, both_flat[-1])
    )
    up.between()
    up.second()
    down.across()
    left_joined = turned(send_left(inputs, grad_z))
    left_att = turned(send_left(att_parts, grad_z))
    both_branch = right_rows(grad_branch, left_joined)
    rest = Chain([([left_joined], [right_rows(grad_z, left_att)]), ([left_att], [both_branch])])
    qkv_first = qkv.begin(up.next_x, up.next_y)
    qkv.first()
    up_own = up.own_sum(*qkv_first)
    up.across()
    rest_first = rest.begin(up_own)
    rest.first()
    qkv_second = qkv.between(*rest_first)
    qkv.second()
    down_fold = down.along(qkv_second)
    rest_second = rest.between(down_fold)
    rest.second()
    up_fold = up.along(rest_second, rest.from_x, rest.from_y, qkv.then_x, qkv.then_y)
    qkv_own = qkv.own_sum(up_fold)
    down.spread()
    if paired:
        output = forward(meta, resid, dbias, acts, full_down, after=(qkv_own,))
        mine, theirs = sort_sums(meta, sums1, sums2, up_sum, after=rest_first)
        mine = mine + swap_frames(theirs)
    else:
        output = (resid + times(acts[0], full_down[0]) + dbias).astype(BF16)
        summed = (
            *(sums1[i] for i in range(3)),
            *(sums2[i] for i in range(3)),
            up_sum[0],
            sums2[3],
        )
        summed = jnp.concatenate([v.reshape(n_frames, -1) for v in summed], axis=1)
        mine = lax.psum_scatter(summed, "frames", scatter_dimension=0, tiled=True)
    rest_own = rest.own_sum(output)
    qkv.across(rest.then_x, rest.then_y)
    up.spread()
    input_grad, skip_grad = input_grads(meta, grad_z, full_skip, after=(rest_own,))
    down.finish()
    qkv.along((input_grad,), down.by_x, down.by_y)
    rest.across(up.by_x, up.by_y)
    qkv.spread()
    (grad_w_down,) = down.place()
    up.finish(grad_w_down)
    rest.along((mine,), down.far_low, down.far_high)
    copies = jnp.broadcast_to(mine[None], (n_batch * n_seq,) + mine.shape)

    def exchange_all(array):
        return lax.all_to_all(array, ("batch", "seq"), split_axis=0, concat_axis=0, tiled=True)

    qkv.finish()
    total = links.send("z", copies, exchange_all, qkv.far_low, qkv.far_high)
    total = jnp.sum(total, axis=0).reshape(-1)
    vector_grads = [total[b : b + n] for b, n in zip(starts, sizes)]
    (grad_w_up,) = up.place()
    rest.spread(grad_w_up)
    (grad_w_qkv,) = qkv.place()
    rest.finish(grad_w_qkv, *vector_grads[:1])
    grad_w_skip, grad_w_out = rest.place(after=(grad_w_qkv,))

    def back(array):
        return array.reshape(1, 1, 1, tok, width)

    return (
        back(output),
        back(input_grad),
        back(skip_grad),
        grad_w_skip,
        grad_w_qkv,
        grad_w_out,
        grad_w_up,
        grad_w_down,
        *vector_grads,
    )


def solution(mesh):
    rows = P("batch", "seq", "frames", None, None)
    in_specs = (
        (rows, rows, P("batch", "frames", None), rows)
        + (P("frames", None),) * 5
        + (P("frames"),) * 8
    )
    out_specs = (rows,) * 3 + (P("frames", None),) * 5 + (P("frames"),) * 8
    return jax.shard_map(body, mesh=mesh, in_specs=in_specs, out_specs=out_specs, check_vma=False)
```

time: 518 us -> 495 us (0.956)
  local copies, waits for them, and re-layouts: 68.3 us -> 29.4 us
  Pallas kernels: 99.7 us -> 134 us
  other arithmetic: 35.7 us -> 17.5 us
  waiting for transfers between devices: 158 us -> 142 us
  starting transfers between devices: 84.8 us -> 97.5 us
    pallas_call x13 -> x20, Pallas kernels: 98.2 us -> 132 us  [the longest x5 30.3 us: place(): pl.pallas_call(kernel, grid_spec=pltpu.PrefetchScalarGridSpec(num_scalar_...]
    ppermute x6 -> x3, waiting for transfers between devices: 38.6 us -> 13.9 us  [from_seq(): lax.ppermute(array, 'seq', [((i + step) % n_seq, i) for i in range(n_seq)])]
    ppermute x17 -> x16, waiting for transfers between devices: 52.7 us -> 31.1 us  [over_y(): return lax.ppermute(array, 'batch', [(i, i ^ 2) for i in range(n_batch)])]
    ppermute x17 -> x16, waiting for transfers between devices: 43.4 us -> 60.4 us  [over_x(): return lax.ppermute(array, 'batch', [(i, i ^ 1) for i in range(n_batch)])]
    all_to_all x9, waiting for transfers between devices: 9.61 us -> 26.1 us  [exchange_seq(): return lax.all_to_all(array, 'seq', split_axis=0, concat_axis=0, tiled=True)]
    dot_general x35 -> x34, matrix products: 46.3 us -> 56.8 us  [contract_rows(): lax.dot_general(left_side, right_side, (((0,), (0,)), ((), ())), preferre...]
    reshape x10 -> x0, local copies, waits for them, and re-layouts: 10.3 us -> none  [the longest x8 10.1 us: pack(): v.reshape(1, -1)]
    concatenate x15 -> x6, other arithmetic: 14.6 us -> 5.06 us  [the longest x5 3.82 us: stack(): return arrays[0] if len(arrays) == 1 else jnp.concatenate(arrays, axis=0)]
  transfers between devices with their start and end apart: 67 -> 62, of which waited for: 32 -> 23; matrix products, arithmetic and copies ran while one was open for 30% -> 20% of each run, Pallas kernels for 19% -> 22%
where the time goes in v3:
time: 495 us; the launch traced here: 488 us
  waiting for transfers between devices  142 us (29%)
  Pallas kernels  134 us (27%)
  starting transfers between devices  97.5 us (20%)
  matrix products  66.6 us (13%)
  local copies, waits for them, and re-layouts  29.4 us (6%)
  other arithmetic  17.5 us (4%)
    ppermute x16, waiting for transfers between devices, over_x(): return lax.ppermute(array, 'batch', [(i, i ^ 1) for i in range(n_batch)])  60.4 us
    dot_general x34, matrix products, contract_rows(): lax.dot_general(left_side, right_side, (((0,), (0,)), ((), ())), preferre...  56.8 us
    all_to_all x9, starting transfers between devices, exchange_seq(): return lax.all_to_all(array, 'seq', split_axis=0, concat_axis=0, tiled=True)  44.6 us
    ppermute x16, waiting for transfers between devices, over_y(): return lax.ppermute(array, 'batch', [(i, i ^ 2) for i in range(n_batch)])  31.1 us
    pallas_call x5, Pallas kernels, place(): pl.pallas_call(kernel, grid_spec=pltpu.PrefetchScalarGridSpec(num_scalar_...  30.3 us
    all_to_all x9, waiting for transfers between devices, exchange_seq(): return lax.all_to_all(array, 'seq', split_axis=0, concat_axis=0, tiled=True)  26.1 us
    pallas_call x1, Pallas kernels, centre(): pl.pallas_call(kernel, grid_spec=pltpu.PrefetchScalarGridSpec(num_scalar_...  19 us
    ppermute x16, starting transfers between devices, over_y(): return lax.ppermute(array, 'batch', [(i, i ^ 2) for i in range(n_batch)])  18.9 us
  transfers between devices with their start and end apart: 62, of which 23 were waited for; matrix products, arithmetic and copies ran while one was open for 20% of the time, Pallas kernels for 22%

profile of v3, /device:TPU:0, one launch (start us, length us, event | category | flops | bytes accessed | tf_op | source)
XLA Modules:
  0.0 488.1 jit_solution(13176469386588444932)
XLA Ops:
  2.6 4.1 collective-permute-done.refs_4_.refs_3_
  8.8 5.4 %collective-permute-done.1.refs_6_.refs_2_ = bf16[1,5632]{1,0:T(2,128)(2,1)S(1)} collective-permute-done((bf16[1,5632]{1,0:T(2,128)(2,1)}, bf16[1,5632]{1,0:T(2,128)(2,1)S(1)}, u32[]{:S(2)}, u32[]{:S(2)}) %collective-permute-start.1) | collective-permute-done | bytes 11296 | tf_op jit(solution)/shard_map/ppermute | solution.py:908
  14.8 6.4 %front.1 = (f32[192,1024]{1,0:T(8,128)}, bf16[192,1024]{1,0:T(8,128)(2,1)}, bf16[192,1024]{1,0:T(8,128)(2,1)}, bf16[192,1024]{1,0:T(8,128)(2,1)}) custom-call(s32[6]{0:T(128)} %pad_add_fusion.refs_0_, bf16[192,1024]{1,0:T(8,128)(2,1)} %bitcast.62, bf16[192,1024]{1,0:T(8,128)(2,1)} %bitcast.63, bf16[1024,1024]{1,0:T(8,128)(2,1)} %refs_2_.5, ...), custom_call_target="tpu_custom_call" | custom-call | tf_op jit(solution)/shard_map/front/pallas_call | solution.py:263
  28.3 4.9 fusion.94.refs_11_.refs_8_
  34.6 4.9 fusion.95.refs_12_.refs_9_
  39.4 13.9 %collective-permute-done.3.refs_3_ = bf16[192,1024]{1,0:T(8,128)(2,1)} collective-permute-done((bf16[192,1024]{1,0:T(8,128)(2,1)}, bf16[192,1024]{1,0:T(8,128)(2,1)}, u32[]{:S(2)}, u32[]{:S(2)}) %collective-permute-start.3) | collective-permute-done | bytes 393248 | tf_op jit(solution)/shard_map/ppermute | solution.py:917
  55.0 9.7 %project.1 = (bf16[192,1024]{1,0:T(8,128)(2,1)}, bf16[768,1024]{1,0:T(8,128)(2,1)}, bf16[768,1024]{1,0:T(8,128)(2,1)}, bf16[768,512]{1,0:T(8,128)(2,1)}, bf16[768,512]{1,0:T(8,128)(2,1)}) custom-call(s32[6]{0:T(128)} %pad_add_fusion.refs_0_, bf16[192,1024]{1,0:T(8,128)(2,1)} %get-tuple-element.122.refs_3_.refs_1_, ...), custom_call_target="tpu_custom_call" | custom-call | tf_op jit(solution)/shard_map/project/pallas_call | solution.py:373
  65.3 11.1 %attend_forward.1 = (bf16[192,1024]{1,0:T(8,128)(2,1)}, bf16[8,768,384]{2,1,0:T(8,128)(2,1)}) custom-call(s32[6]{0:T(128)} %pad_add_fusion.refs_0_, bf16[192,1024]{1,0:T(8,128)(2,1)} %get-tuple-element.128.refs_1_.refs_0_, bf16[768,1024]{1,0:T(8,128)(2,1)} %get-tuple-element.129.refs_2_.refs_1_, bf16[768,1024]{1,0:T(8,128)(2,1)} %get-tuple-element.130.refs_3_.refs_2_), custom_call_target="tpu_custom_call" | custom-call | tf_op jit(solution)/shard_map/attend_forward/pallas_call | solution.py:148
  78.7 19.0 %centre.1 = (f32[192,1024]{1,0:T(8,128)}, bf16[192,4096]{1,0:T(8,128)(2,1)}, f32[192,1024]{1,0:T(8,128)}, bf16[192,1024]{1,0:T(8,128)(2,1)}, bf16[192,1024]{1,0:...) custom-call(s32[6]{0:T(128)} %pad_add_fusion.refs_0_, ...), custom_call_target="tpu_custom_call" | custom-call | tf_op jit(solution)/shard_map/centre/pallas_call | solution.py:513
  108.0 11.6 %attend_backward.1.refs_1_ = bf16[3,768,1024]{2,1,0:T(8,128)(2,1)} custom-call(bf16[192,1024]{1,0:T(8,128)(2,1)} %get-tuple-element.128.refs_1_.refs_0_, bf16[768,1024]{1,0:T(8,128)(2,1)} %get-tuple-element.129.refs_2_.refs_1_, bf16[768,1024]{1,0:T(8,128)(2,1)} %get-tuple-element.130.refs_3_.refs_2_, bf16[192,1024]{1,0:T(8,128)(2,1)} %get-tuple-element.148.refs_3_, ...), custom_call_target="tpu_custom_call" | custom-call | tf_op jit(solution)/shard_map/attend_backward/pallas_call | solution.py:180
  119.6 13.6 %unproject.1 = (bf16[4,192,1024]{2,1,0:T(8,128)(2,1)}, bf16[768,3072]{1,0:T(8,128)(2,1)}) custom-call(s32[6]{0:T(128)} %pad_add_fusion.refs_0_, bf16[3,768,1024]{2,1,0:T(8,128)(2,1)} %attend_backward.1.refs_1_, bf16[512,3072]{1,0:T(8,128)(2,1)} %refs_2_.4, bf16[512,3072]{1,0:T(8,128)(2,1)} %copy-done, ...), custom_call_target="tpu_custom_call" | custom-call | tf_op jit(solution)/shard_map/unproject/pallas_call | solution.py:583
  143.3 11.2 %all-to-all-start = ((bf16[4,192,1024]{2,1,0:T(8,128)(2,1)}), bf16[4,192,1024]{2,1,0:T(8,128)(2,1)}, u32[]{:S(2)}, u32[]{:S(2)}) async-start(bf16[4,192,1024]{2,1,0:T(8,128)(2,1)} %get-tuple-element.162), calls=%async_computation | async-start | bytes 3145728 | tf_op jit(solution)/shard_map/all_to_all | solution.py:925
  163.7 5.8 %collective-permute-done.21 = bf16[512,512]{1,0:T(8,128)(2,1)S(1)} collective-permute-done((bf16[512,512]{1,0:T(8,128)(2,1)}, bf16[512,512]{1,0:T(8,128)(2,1)S(1)}, u32[]{:S(2)}, u32[]{:S(2)}) %collective-permute-start.21) | collective-permute-done | bytes 524320 | tf_op jit(solution)/shard_map/ppermute | solution.py:911
  174.6 16.6 %collective-permute-done.17 = bf16[256,2048]{1,0:T(8,128)(2,1)S(1)} collective-permute-done((bf16[256,2048]{1,0:T(8,128)(2,1)}, bf16[256,2048]{1,0:T(8,128)(2,1)S(1)}, u32[]{:S(2)}, u32[]{:S(2)}) %collective-permute-start.17) | collective-permute-done | bytes 1048608 | tf_op jit(solution)/shard_map/ppermute | solution.py:911
  195.1 4.8 all-to-all-start.1
  248.3 5.4 %all-to-all-done.2.refs_0_ = bf16[4,32,4096]{2,1,0:T(8,128)(2,1)S(1)} async-done(((bf16[4,32,4096]{2,1,0:T(8,128)(2,1)}), bf16[4,32,4096]{2,1,0:T(8,128)(2,1)S(1)}, u32[]{:S(2)}, u32[]{:S(2)}) %all-to-all-start.2) | async-done | bytes 1048608 | tf_op jit(solution)/shard_map/all_to_all | solution.py:925
  254.7 4.3 all-to-all-start.3
  267.8 15.1 %collective-permute-done.31 = bf16[768,512]{1,0:T(8,128)(2,1)S(1)} collective-permute-done((bf16[768,512]{1,0:T(8,128)(2,1)S(1)}, bf16[768,512]{1,0:T(8,128)(2,1)S(1)}, u32[]{:S(2)}, u32[]{:S(2)}) %collective-permute-start.31) | collective-permute-done | bytes 786464 | tf_op jit(solution)/shard_map/ppermute | solution.py:911
  290.4 4.7 all-to-all-start.4
  308.4 10.5 %all-to-all-done.4 = bf16[4,32,4096]{2,1,0:T(8,128)(2,1)} async-done(((bf16[4,32,4096]{2,1,0:T(8,128)(2,1)}), bf16[4,32,4096]{2,1,0:T(8,128)(2,1)}, u32[]{:S(2)}, u32[]{:S(2)}) %all-to-all-start.4) | async-done | bytes 1048608 | tf_op jit(solution)/shard_map/all_to_all | solution.py:925
  323.8 7.5 %forward.1 = bf16[192,1024]{1,0:T(8,128)(2,1)} custom-call(s32[6]{0:T(128)} %pad_add_fusion.refs_0_, f32[192,1024]{1,0:T(8,128)} %get-tuple-element.142.refs_1_, f32[1,1024]{1,0:T(1,128)} %get-tuple-element.143.refs_2_, bf16[192,2048]{1,0:T(8,128)(2,1)} %get-tuple-element.144.refs_3_, bf16[192,2048]{1,0:T(8,128)(2,1)} %get-tuple-element.145.refs_4_, ...), custom_call_target="tpu_custom_call" | custom-call | tf_op jit(solution)/shard_map/forward/pallas_call | solution.py:659
  334.8 5.8 %input_grads.1 = (f32[192,1024]{1,0:T(8,128)}, f32[192,1024]{1,0:T(8,128)}) custom-call(s32[6]{0:T(128)} %pad_add_fusion.refs_0_, bf16[192,1024]{1,0:T(8,128)(2,1)} %get-tuple-element.176.refs_1_, bf16[1024,1024]{1,0:T(8,128)(2,1)} %refs_2_.5, bf16[1024,1024]{1,0:T(8,128)(2,1)} %collective-permute-done.refs_4_.refs_3_, bf16[4,96,1024]{2,1,0:T(8,128)(2,1)} %fusion.24.refs_4_), custom_call_target="tpu_custom_call" | custom-call | tf_op jit(solution)/shard_map/input_grads/pallas_call | solution.py:730
  352.0 22.2 %collective-permute-done.36.refs_3_ = bf16[128,4096]{1,0:T(8,128)(2,1)S(1)} collective-permute-done((bf16[128,4096]{1,0:T(8,128)(2,1)}, bf16[128,4096]{1,0:T(8,128)(2,1)S(1)}, u32[]{:S(2)}, u32[]{:S(2)}) %collective-permute-start.36) | collective-permute-done | bytes 1048608 | tf_op jit(solution)/shard_map/ppermute | solution.py:914
  375.5 4.7 all-to-all-start.7
  390.8 7.2 %all-to-all-done.7.refs_0_ = bf16[4,96,1024]{2,1,0:T(8,128)(2,1)S(1)} async-done(((bf16[4,96,1024]{2,1,0:T(8,128)(2,1)}), bf16[4,96,1024]{2,1,0:T(8,128)(2,1)S(1)}, u32[]{:S(2)}, u32[]{:S(2)}) %all-to-all-start.7) | async-done | bytes 786464 | tf_op jit(solution)/shard_map/all_to_all | solution.py:925
  404.8 8.0 %place.5 = f32[2048,1024]{1,0:T(8,128)} custom-call(s32[1]{0:T(128)} %bitcast.2.refs_0_, bf16[512,1024]{1,0:T(8,128)(2,1)} %bitcast.17.refs_1_, bf16[512,1024]{1,0:T(8,128)(2,1)} %collective-permute-done.37.refs_2_, bf16[512,1024]{1,0:T(8,128)(2,1)} %collective-permute-done.38.refs_3_, bf16[512,512]{1,0:T(8,128)(2,1)} %copy-done.41, ...), custom_call_target="tpu_custom_call" | custom-call | tf_op jit(solution)/shard_map/place/pallas_call | solution.py:839
  420.9 14.5 %collective-permute-done.48.refs_4_ = bf16[128,1536]{1,0:T(8,128)(2,1)S(1)} collective-permute-done((bf16[128,1536]{1,0:T(8,128)(2,1)S(1)}, bf16[128,1536]{1,0:T(8,128)(2,1)S(1)}, u32[]{:S(2)}, u32[]{:S(2)}) %collective-permute-start.48) | collective-permute-done | bytes 393248 | tf_op jit(solution)/shard_map/ppermute | solution.py:911
  436.7 5.7 %all-to-all-start.9 = ((f32[16,1,5632]{2,1,0:T(1,128)}), f32[16,1,5632]{2,1,0:T(1,128)S(1)}, u32[]{:S(2)}, u32[]{:S(2)}) async-start(f32[16,1,5632]{2,1,0:T(1,128)} %broadcast_in_dim.9), calls=%async_computation.9 | async-start | bytes 720896 | tf_op jit(solution)/shard_map/all_to_all | solution.py:1194
  444.0 7.9 %place.6 = f32[512,4096]{1,0:T(8,128)} custom-call(s32[1]{0:T(128)} %bitcast.2.refs_0_, bf16[128,4096]{1,0:T(8,128)(2,1)} %bitcast.16.refs_1_, bf16[128,4096]{1,0:T(8,128)(2,1)} %collective-permute-done.35.refs_2_, bf16[128,4096]{1,0:T(8,128)(2,1)} %copy-done.21, bf16[128,2048]{1,0:T(8,128)(2,1)} %copy-done.42, bf16[128,2048]{1,0:T(8,128)(2,1)} %copy-done.43), custom_call_target="tpu_custom_call" | custom-call | tf_op jit(solution)/shard_map/place/pallas_call | solution.py:839
  455.4 7.4 %place.7.refs_6_ = f32[512,3072]{1,0:T(8,128)} custom-call(s32[1]{0:T(128)} %bitcast.2.refs_0_, bf16[128,3072]{1,0:T(8,128)(2,1)} %bitcast.57, bf16[128,3072]{1,0:T(8,128)(2,1)} %collective-permute-done.46.refs_2_, bf16[128,3072]{1,0:T(8,128)(2,1)} %collective-permute-done.47.refs_3_, bf16[128,1536]{1,0:T(8,128)(2,1)} %copy-done.44, bf16[128,1536]{1,0:T(8,128)(2,1)} %copy-done.45), custom_call_target="tpu_custom_call" | custom-call | tf_op jit(solution)/shard_map/place/pallas_call | solution.py:839
  463.6 5.1 %collective-permute-done.44.refs_2_ = bf16[384,1024]{1,0:T(8,128)(2,1)S(1)} collective-permute-done((bf16[384,1024]{1,0:T(8,128)(2,1)S(1)}, bf16[384,1024]{1,0:T(8,128)(2,1)S(1)}, u32[]{:S(2)}, u32[]{:S(2)}) %collective-permute-start.44) | collective-permute-done | bytes 786464 | tf_op jit(solution)/shard_map/ppermute | solution.py:911
  473.4 4.5 collective-permute-done.51.refs_5_
  (298 shorter events, 202.7 us)
Async XLA Ops:
  8.4 44.9 %collective-permute-start.5 = (bf16[512,3072]{1,0:T(8,128)(2,1)}, bf16[512,3072]{1,0:T(8,128)(2,1)S(1)}, u32[]{:S(2)}, u32[]{:S(2)}) collective-permute-start(bf16[512,3072]{1,0:T(8,128)(2,1)} %refs_2_.4), channel_id=1, source_target_pairs={{0,1},{1,0},{2,3},{3,2},{4,5},{5,4},{6,7},{7,6},{8,9},{9,8},{10,11... | collective-permute-start | bytes 9437192 | tf_op jit(solution)/shard_map/ppermute | solution.py:908
  21.2 56.2 %collective-permute-start.8 = (bf16[512,4096]{1,0:T(8,128)(2,1)}, bf16[512,4096]{1,0:T(8,128)(2,1)}, u32[]{:S(2)}, u32[]{:S(2)}) collective-permute-start(bf16[512,4096]{1,0:T(8,128)(2,1)} %refs_6_.5), channel_id=1, source_target_pairs={{0,1},{1,0},{2,3},{3,2},{4,5},{5,4},{6,7},{7,6},{8,9},{9,8},{10,11... | collective-permute-start | bytes 12582920 | tf_op jit(solution)/shard_map/ppermute | solution.py:908
  24.4 29.0 %collective-permute-start.3 = (bf16[192,1024]{1,0:T(8,128)(2,1)}, bf16[192,1024]{1,0:T(8,128)(2,1)}, u32[]{:S(2)}, u32[]{:S(2)}) collective-permute-start(bf16[192,1024]{1,0:T(8,128)(2,1)} %get-tuple-element.122.refs_3_.refs_1_), channel_id=1, source_target_pairs={{4,0},{6,2},{0,4},{2,6},{5,1},{7,3},{1,5},{3,7},{12,8},{14,10},{8,... | collective-permute-start | bytes 1179656 | tf_op jit(solution)/shard_map/ppermute | solution.py:917
  27.0 26.4 %collective-permute-start.2 = (bf16[192,1024]{1,0:T(8,128)(2,1)}, bf16[192,1024]{1,0:T(8,128)(2,1)}, u32[]{:S(2)}, u32[]{:S(2)}) collective-permute-start(bf16[192,1024]{1,0:T(8,128)(2,1)} %get-tuple-element.122.refs_3_.refs_1_), channel_id=1, source_target_pairs={{2,0},{4,2},{6,4},{0,6},{3,1},{5,3},{7,5},{1,7},{10,8},{12,10},{14... | collective-permute-start | bytes 1179656 | tf_op jit(solution)/shard_map/ppermute | solution.py:917
  98.4 34.9 %collective-permute-start.15 = (bf16[192,4096]{1,0:T(8,128)(2,1)}, bf16[192,4096]{1,0:T(8,128)(2,1)}, u32[]{:S(2)}, u32[]{:S(2)}) collective-permute-start(bf16[192,4096]{1,0:T(8,128)(2,1)} %get-tuple-element.154), channel_id=1, source_target_pairs={{0,1},{1,0},{2,3},{3,2},{4,5},{5,4},{6,7},{7,6},{8,9},{9,8},{10,11... | collective-permute-start | bytes 4718600 | tf_op jit(solution)/shard_map/ppermute | solution.py:908
  102.2 32.7 %collective-permute-start.13 = (bf16[1024,512]{1,0:T(8,128)(2,1)}, bf16[1024,512]{1,0:T(8,128)(2,1)}, u32[]{:S(2)}, u32[]{:S(2)}) collective-permute-start(bf16[1024,512]{1,0:T(8,128)(2,1)} %convolution_convert_fusion.3.refs_6_.refs_5_), channel_id=1, source_target_pairs={{0,16},{8,24},{16,0},{24,8},{1,17},{9,25},{17,1},{25,9},{2,18},{10... | collective-permute-start | bytes 3145736 | tf_op jit(solution)/shard_map/ppermute | solution.py:914
  105.6 29.3 %collective-permute-start.14 = (bf16[1024,512]{1,0:T(8,128)(2,1)}, bf16[1024,512]{1,0:T(8,128)(2,1)}, u32[]{:S(2)}, u32[]{:S(2)}) collective-permute-start(bf16[1024,512]{1,0:T(8,128)(2,1)} %convolution_convert_fusion.2.refs_5_.refs_4_), channel_id=1, source_target_pairs={{0,8},{8,0},{16,24},{24,16},{1,9},{9,1},{17,25},{25,17},{2,10},{10... | collective-permute-start | bytes 3145736 | tf_op jit(solution)/shard_map/ppermute | solution.py:911
  143.3 56.6 %collective-permute-start.18 = (bf16[768,3072]{1,0:T(8,128)(2,1)}, bf16[768,3072]{1,0:T(8,128)(2,1)}, u32[]{:S(2)}, u32[]{:S(2)}) collective-permute-start(bf16[768,3072]{1,0:T(8,128)(2,1)} %get-tuple-element.158), channel_id=1, source_target_pairs={{0,1},{1,0},{2,3},{3,2},{4,5},{5,4},{6,7},{7,6},{8,9},{9,8},{10,11... | collective-permute-start | bytes 14155784 | tf_op jit(solution)/shard_map/ppermute | solution.py:908
  143.3 51.8 %all-to-all-start = ((bf16[4,192,1024]{2,1,0:T(8,128)(2,1)}), bf16[4,192,1024]{2,1,0:T(8,128)(2,1)}, u32[]{:S(2)}, u32[]{:S(2)}) async-start(bf16[4,192,1024]{2,1,0:T(8,128)(2,1)} %get-tuple-element.162), calls=%async_computation | async-start | bytes 3145728 | tf_op jit(solution)/shard_map/all_to_all | solution.py:925
  155.8 35.4 %collective-permute-start.17 = (bf16[256,2048]{1,0:T(8,128)(2,1)}, bf16[256,2048]{1,0:T(8,128)(2,1)S(1)}, u32[]{:S(2)}, u32[]{:S(2)}) collective-permute-start(bf16[256,2048]{1,0:T(8,128)(2,1)} %convolution_convert_fusion), channel_id=1, source_target_pairs={{0,8},{8,0},{16,24},{24,16},{1,9},{9,1},{17,25},{25,17},{2,10},{10... | collective-permute-start | bytes 3145736 | tf_op jit(solution)/shard_map/ppermute | solution.py:911
  158.8 34.2 %collective-permute-start.16 = (bf16[256,2048]{1,0:T(8,128)(2,1)}, bf16[256,2048]{1,0:T(8,128)(2,1)S(1)}, u32[]{:S(2)}, u32[]{:S(2)}) collective-permute-start(bf16[256,2048]{1,0:T(8,128)(2,1)} %convolution_convert_fusion.1), channel_id=1, source_target_pairs={{0,16},{8,24},{16,0},{24,8},{1,17},{9,25},{17,1},{25,9},{2,18},{10... | collective-permute-start | bytes 3145736 | tf_op jit(solution)/shard_map/ppermute | solution.py:914
  192.5 24.9 %collective-permute-start.23 = (bf16[128,2048]{1,0:T(8,128)(2,1)}, bf16[128,2048]{1,0:T(8,128)(2,1)}, u32[]{:S(2)}, u32[]{:S(2)}) collective-permute-start(bf16[128,2048]{1,0:T(8,128)(2,1)} %fusion.10), channel_id=1, source_target_pairs={{0,16},{8,24},{16,0},{24,8},{1,17},{9,25},{17,1},{25,9},{2,18},{10... | collective-permute-start | bytes 1572872 | tf_op jit(solution)/shard_map/ppermute | solution.py:914
  195.1 29.4 %all-to-all-start.1 = ((bf16[4,128,1024]{2,1,0:T(8,128)(2,1)}), bf16[4,128,1024]{2,1,0:T(8,128)(2,1)}, u32[]{:S(2)}, u32[]{:S(2)}) async-start(bf16[4,128,1024]{2,1,0:T(8,128)(2,1)} %bitcast.53), calls=%async_computation.1 | async-start | bytes 2097152 | tf_op jit(solution)/shard_map/all_to_all | solution.py:925
  203.3 27.4 %collective-permute-start.25 = (bf16[192,512]{1,0:T(8,128)(2,1)}, bf16[192,512]{1,0:T(8,128)(2,1)}, u32[]{:S(2)}, u32[]{:S(2)}) collective-permute-start(bf16[192,512]{1,0:T(8,128)(2,1)} %get-tuple-element.175), channel_id=1, source_target_pairs={{0,1},{1,0},{2,3},{3,2},{4,5},{5,4},{6,7},{7,6},{8,9},{9,8},{10,11... | collective-permute-start | bytes 589832 | tf_op jit(solution)/shard_map/ppermute | solution.py:908
  203.3 30.8 %collective-permute-start.22 = (bf16[192,1024]{1,0:T(8,128)(2,1)}, bf16[192,1024]{1,0:T(8,128)(2,1)}, u32[]{:S(2)}, u32[]{:S(2)}) collective-permute-start(bf16[192,1024]{1,0:T(8,128)(2,1)} %get-tuple-element.167), channel_id=1, source_target_pairs={{0,1},{1,0},{2,3},{3,2},{4,5},{5,4},{6,7},{7,6},{8,9},{9,8},{10,11... | collective-permute-start | bytes 1179656 | tf_op jit(solution)/shard_map/ppermute | solution.py:908
  209.9 30.1 %collective-permute-start.28 = (bf16[256,1536]{1,0:T(8,128)(2,1)}, bf16[256,1536]{1,0:T(8,128)(2,1)}, u32[]{:S(2)}, u32[]{:S(2)}) collective-permute-start(bf16[256,1536]{1,0:T(8,128)(2,1)} %fusion.4), channel_id=1, source_target_pairs={{0,16},{8,24},{16,0},{24,8},{1,17},{9,25},{17,1},{25,9},{2,18},{10... | collective-permute-start | bytes 2359304 | tf_op jit(solution)/shard_map/ppermute | solution.py:914
  224.4 29.3 %all-to-all-start.2 = ((bf16[4,32,4096]{2,1,0:T(8,128)(2,1)}), bf16[4,32,4096]{2,1,0:T(8,128)(2,1)S(1)}, u32[]{:S(2)}, u32[]{:S(2)}) async-start(bf16[4,32,4096]{2,1,0:T(8,128)(2,1)} %bitcast.52), calls=%async_computation.2 | async-start | bytes 2097152 | tf_op jit(solution)/shard_map/all_to_all | solution.py:925
  254.7 35.7 %all-to-all-start.3 = ((bf16[4,128,1024]{2,1,0:T(8,128)(2,1)}), bf16[4,128,1024]{2,1,0:T(8,128)(2,1)}, u32[]{:S(2)}, u32[]{:S(2)}) async-start(bf16[4,128,1024]{2,1,0:T(8,128)(2,1)} %fold.4), calls=%async_computation.3 | async-start | bytes 2097152 | tf_op jit(solution)/shard_map/all_to_all | solution.py:925
  265.7 24.7 %collective-permute-start.29 = (bf16[128,1536]{1,0:T(8,128)(2,1)}, bf16[128,1536]{1,0:T(8,128)(2,1)}, u32[]{:S(2)}, u32[]{:S(2)}) collective-permute-start(bf16[128,1536]{1,0:T(8,128)(2,1)} %fusion.7.refs_2_), channel_id=1, source_target_pairs={{0,16},{8,24},{16,0},{24,8},{1,17},{9,25},{17,1},{25,9},{2,18},{10... | collective-permute-start | bytes 1179656 | tf_op jit(solution)/shard_map/ppermute | solution.py:914
  266.3 24.1 %collective-permute-start.32 = (bf16[128,1536]{1,0:T(8,128)(2,1)}, bf16[128,1536]{1,0:T(8,128)(2,1)}, u32[]{:S(2)}, u32[]{:S(2)}) collective-permute-start(bf16[128,1536]{1,0:T(8,128)(2,1)} %fusion.8.refs_1_), channel_id=1, source_target_pairs={{0,8},{8,0},{16,24},{24,16},{1,9},{9,1},{17,25},{25,17},{2,10},{10... | collective-permute-start | bytes 1179656 | tf_op jit(solution)/shard_map/ppermute | solution.py:911
  290.4 28.5 %all-to-all-start.4 = ((bf16[4,32,4096]{2,1,0:T(8,128)(2,1)}), bf16[4,32,4096]{2,1,0:T(8,128)(2,1)}, u32[]{:S(2)}, u32[]{:S(2)}) async-start(bf16[4,32,4096]{2,1,0:T(8,128)(2,1)} %fold.5), calls=%async_computation.4 | async-start | bytes 2097152 | tf_op jit(solution)/shard_map/all_to_all | solution.py:925
  306.5 39.7 %collective-permute-start.37 = (bf16[512,1024]{1,0:T(8,128)(2,1)}, bf16[512,1024]{1,0:T(8,128)(2,1)}, u32[]{:S(2)}, u32[]{:S(2)}) collective-permute-start(bf16[512,1024]{1,0:T(8,128)(2,1)} %bitcast.17.refs_1_), channel_id=1, source_target_pairs={{0,8},{8,0},{16,24},{24,16},{1,9},{9,1},{17,25},{25,17},{2,10},{10... | collective-permute-start | bytes 3145736 | tf_op jit(solution)/shard_map/ppermute | solution.py:911
  307.9 38.3 %collective-permute-start.38 = (bf16[512,1024]{1,0:T(8,128)(2,1)}, bf16[512,1024]{1,0:T(8,128)(2,1)}, u32[]{:S(2)}, u32[]{:S(2)}) collective-permute-start(bf16[512,1024]{1,0:T(8,128)(2,1)} %bitcast.17.refs_1_), channel_id=1, source_target_pairs={{0,16},{8,24},{16,0},{24,8},{1,17},{9,25},{17,1},{25,9},{2,18},{10... | collective-permute-start | bytes 3145736 | tf_op jit(solution)/shard_map/ppermute | solution.py:914
  346.2 29.3 %all-to-all-start.6 = ((bf16[4,32,3072]{2,1,0:T(8,128)(2,1)}), bf16[4,32,3072]{2,1,0:T(8,128)(2,1)S(1)}, u32[]{:S(2)}, u32[]{:S(2)}) async-start(bf16[4,32,3072]{2,1,0:T(8,128)(2,1)} %fold.6), calls=%async_computation.6 | async-start | bytes 1572864 | tf_op jit(solution)/shard_map/all_to_all | solution.py:925
  349.8 24.3 %collective-permute-start.36 = (bf16[128,4096]{1,0:T(8,128)(2,1)}, bf16[128,4096]{1,0:T(8,128)(2,1)S(1)}, u32[]{:S(2)}, u32[]{:S(2)}) collective-permute-start(bf16[128,4096]{1,0:T(8,128)(2,1)} %bitcast.16.refs_1_), channel_id=1, source_target_pairs={{0,16},{8,24},{16,0},{24,8},{1,17},{9,25},{17,1},{25,9},{2,18},{10... | collective-permute-start | bytes 3145736 | tf_op jit(solution)/shard_map/ppermute | solution.py:914
  351.3 24.1 %collective-permute-start.35 = (bf16[128,4096]{1,0:T(8,128)(2,1)}, bf16[128,4096]{1,0:T(8,128)(2,1)}, u32[]{:S(2)}, u32[]{:S(2)}) collective-permute-start(bf16[128,4096]{1,0:T(8,128)(2,1)} %bitcast.16.refs_1_), channel_id=1, source_target_pairs={{0,8},{8,0},{16,24},{24,16},{1,9},{9,1},{17,25},{25,17},{2,10},{10... | collective-permute-start | bytes 3145736 | tf_op jit(solution)/shard_map/ppermute | solution.py:911
  386.8 29.8 %collective-permute-start.46 = (bf16[128,3072]{1,0:T(8,128)(2,1)S(1)}, bf16[128,3072]{1,0:T(8,128)(2,1)}, u32[]{:S(2)}, u32[]{:S(2)}) collective-permute-start(bf16[128,3072]{1,0:T(8,128)(2,1)S(1)} %bitcast.55), channel_id=1, source_target_pairs={{0,8},{8,0},{16,24},{24,16},{1,9},{9,1},{17,25},{25,17},{2,10},{10... | collective-permute-start | bytes 2359304 | tf_op jit(solution)/shard_map/ppermute | solution.py:911
  387.9 29.7 %collective-permute-start.47 = (bf16[128,3072]{1,0:T(8,128)(2,1)S(1)}, bf16[128,3072]{1,0:T(8,128)(2,1)}, u32[]{:S(2)}, u32[]{:S(2)}) collective-permute-start(bf16[128,3072]{1,0:T(8,128)(2,1)S(1)} %bitcast.56), channel_id=1, source_target_pairs={{0,16},{8,24},{16,0},{24,8},{1,17},{9,25},{17,1},{25,9},{2,18},{10... | collective-permute-start | bytes 2359304 | tf_op jit(solution)/shard_map/ppermute | solution.py:914
  401.0 34.6 %all-to-all-start.8 = ((bf16[4,96,1024]{2,1,0:T(8,128)(2,1)}), bf16[4,96,1024]{2,1,0:T(8,128)(2,1)S(1)}, u32[]{:S(2)}, u32[]{:S(2)}) async-start(bf16[4,96,1024]{2,1,0:T(8,128)(2,1)} %fold.7), calls=%async_computation.8 | async-start | bytes 1572864 | tf_op jit(solution)/shard_map/all_to_all | solution.py:925
  414.7 27.7 %collective-permute-start.42 = (bf16[128,2048]{1,0:T(8,128)(2,1)}, bf16[128,2048]{1,0:T(8,128)(2,1)S(1)}, u32[]{:S(2)}, u32[]{:S(2)}) collective-permute-start(bf16[128,2048]{1,0:T(8,128)(2,1)} %slice.380), channel_id=1, source_target_pairs={{0,8},{8,0},{16,24},{24,16},{1,9},{9,1},{17,25},{25,17},{2,10},{10... | collective-permute-start | bytes 1572872 | tf_op jit(solution)/shard_map/ppermute | solution.py:911
  416.0 26.4 %collective-permute-start.43 = (bf16[128,2048]{1,0:T(8,128)(2,1)S(1)}, bf16[128,2048]{1,0:T(8,128)(2,1)S(1)}, u32[]{:S(2)}, u32[]{:S(2)}) collective-permute-start(bf16[128,2048]{1,0:T(8,128)(2,1)S(1)} %slice.381), channel_id=1, source_target_pairs={{0,16},{8,24},{16,0},{24,8},{1,17},{9,25},{17,1},{25,9},{2,18},{10... | collective-permute-start | bytes 1572872 | tf_op jit(solution)/shard_map/ppermute | solution.py:914
  436.7 26.1 %all-to-all-start.9 = ((f32[16,1,5632]{2,1,0:T(1,128)}), f32[16,1,5632]{2,1,0:T(1,128)S(1)}, u32[]{:S(2)}, u32[]{:S(2)}) async-start(f32[16,1,5632]{2,1,0:T(1,128)} %broadcast_in_dim.9), calls=%async_computation.9 | async-start | bytes 720896 | tf_op jit(solution)/shard_map/all_to_all | solution.py:1194
  (84 other events, 760.2 us)

commit v4 on v3

--- a/solution.py
+++ b/solution.py
@@ -1062,8 +1062,8 @@
 
     if paired:
         packs = [packed, swap_frames(packed)]
-        full_qkv = gather_frames(w_qkv, full_skip[1])
-        full_down = gather_frames(w_down, full_skip[1])
+        full_qkv = gather_frames(w_qkv, full_skip[1], packs[1])
+        full_down = gather_frames(w_down, full_skip[1], packs[1])
         hidden_z, n1, own_in, other_in = front(
             meta, frames, skips, full_skip, packs, tuple(sizes)
         )
@@ -1142,7 +1142,7 @@
     grad_z, sums1 = rear(
         terms_n1, hidden_z, grad_resid, gain1, after=(down_own, both_flat[-1])
     )
-    up.between()
+    up.between(grad_z)
     up.second()
     down.across()
     left_joined = turned(send_left(inputs, grad_z))
@@ -1157,10 +1157,10 @@
     rest.first()
     qkv_second = qkv.between(*rest_first)
     qkv.second()
-    down_fold = down.along(qkv_second)
+    down_fold = down.along(qkv_second, rest.from_x, rest.from_y)
     rest_second = rest.between(down_fold)
     rest.second()
-    up_fold = up.along(rest_second, rest.from_x, rest.from_y, qkv.then_x, qkv.then_y)
+    up_fold = up.along(rest_second, qkv.then_x, qkv.then_y)
     qkv_own = qkv.own_sum(up_fold)
     down.spread()
     if paired:
@@ -1182,25 +1182,25 @@
     up.spread()
     input_grad, skip_grad = input_grads(meta, grad_z, full_skip, after=(rest_own,))
     down.finish()
-    qkv.along((input_grad,), down.by_x, down.by_y)
-    rest.across(up.by_x, up.by_y)
+    qkv.along((input_grad,), down.by_x, down.by_y, up.by_x, up.by_y)
+    rest.across(down.far_low, down.far_high)
     qkv.spread()
     (grad_w_down,) = down.place()
-    up.finish(grad_w_down)
-    rest.along((mine,), down.far_low, down.far_high)
+    up.finish()
+    rest.along((mine, grad_w_down), qkv.by_x, qkv.by_y)
     copies = jnp.broadcast_to(mine[None], (n_batch * n_seq,) + mine.shape)
 
     def exchange_all(array):
         return lax.all_to_all(array, ("batch", "seq"), split_axis=0, concat_axis=0, tiled=True)
 
     qkv.finish()
-    total = links.send("z", copies, exchange_all, qkv.far_low, qkv.far_high)
+    (grad_w_up,) = up.place()
+    total = exchange_all(tie(copies, qkv.far_low, qkv.far_high))
+    rest.spread(grad_w_up)
+    (grad_w_qkv,) = qkv.place(after=(grad_w_up,))
+    rest.finish(grad_w_qkv)
     total = jnp.sum(total, axis=0).reshape(-1)
     vector_grads = [total[b : b + n] for b, n in zip(starts, sizes)]
-    (grad_w_up,) = up.place()
-    rest.spread(grad_w_up)
-    (grad_w_qkv,) = qkv.place()
-    rest.finish(grad_w_qkv, *vector_grads[:1])
     grad_w_skip, grad_w_out = rest.place(after=(grad_w_qkv,))
 
     def back(array):

time: 495 us -> 474 us (0.958)
  waiting for transfers between devices: 142 us -> 116 us
  matrix products: 66.6 us -> 72.5 us
    ppermute x16, waiting for transfers between devices: 60.4 us -> 17.9 us  [over_x(): return lax.ppermute(array, 'batch', [(i, i ^ 1) for i in range(n_batch)])]
    all_to_all x9, waiting for transfers between devices: 26.1 us -> 39.9 us  [exchange_seq(): return lax.all_to_all(array, 'seq', split_axis=0, concat_axis=0, tiled=True)]
    ppermute x3, waiting for transfers between devices: 13.9 us -> 22.3 us  [from_seq(): lax.ppermute(array, 'seq', [((i + step) % n_seq, i) for i in range(n_seq)])]
    all_to_all x9, starting transfers between devices: 44.6 us -> 38.7 us  [exchange_seq(): return lax.all_to_all(array, 'seq', split_axis=0, concat_axis=0, tiled=True)]
    dot_general x34, matrix products: 56.8 us -> 62.7 us  [contract_rows(): lax.dot_general(left_side, right_side, (((0,), (0,)), ((), ())), preferre...]
    unnamed x114 -> x100, local copies, waits for them, and re-layouts: 15.6 us -> 16.7 us
  transfers between devices with their start and end apart: 62 -> 62, of which waited for: 23 -> 25; matrix products, arithmetic and copies ran while one was open for 20% -> 22% of each run, Pallas kernels for 22% -> 23%
where the time goes in v4:
time: 474 us; the launch traced here: 467 us
  Pallas kernels  134 us (28%)
  waiting for transfers between devices  116 us (24%)
  starting transfers between devices  94.3 us (20%)
  matrix products  72.5 us (15%)
  local copies, waits for them, and re-layouts  28.6 us (6%)
  other arithmetic  19.4 us (4%)
    dot_general x34, matrix products, contract_rows(): lax.dot_general(left_side, right_side, (((0,), (0,)), ((), ())), preferre...  62.7 us
    all_to_all x9, waiting for transfers between devices, exchange_seq(): return lax.all_to_all(array, 'seq', split_axis=0, concat_axis=0, tiled=True)  39.9 us
    all_to_all x9, starting transfers between devices, exchange_seq(): return lax.all_to_all(array, 'seq', split_axis=0, concat_axis=0, tiled=True)  38.7 us
    pallas_call x5, Pallas kernels, place(): pl.pallas_call(kernel, grid_spec=pltpu.PrefetchScalarGridSpec(num_scalar_...  30.3 us
    ppermute x16, waiting for transfers between devices, over_y(): return lax.ppermute(array, 'batch', [(i, i ^ 2) for i in range(n_batch)])  30.2 us
    ppermute x3, waiting for transfers between devices, from_seq(): lax.ppermute(array, 'seq', [((i + step) % n_seq, i) for i in range(n_seq)])  22.3 us
    ppermute x16, starting transfers between devices, over_x(): return lax.ppermute(array, 'batch', [(i, i ^ 1) for i in range(n_batch)])  21.1 us
    ppermute x16, starting transfers between devices, over_y(): return lax.ppermute(array, 'batch', [(i, i ^ 2) for i in range(n_batch)])  19.4 us
  transfers between devices with their start and end apart: 62, of which 25 were waited for; matrix products, arithmetic and copies ran while one was open for 22% of the time, Pallas kernels for 23%

profile of v4, /device:TPU:0, one launch (start us, length us, event | category | flops | bytes accessed | tf_op | source)
XLA Modules:
  0.0 466.8 jit_solution(12118909465249557877)
XLA Ops:
  2.6 4.1 collective-permute-done.1.refs_6_.refs_2_
  8.5 6.4 %front.1 = (f32[192,1024]{1,0:T(8,128)}, bf16[192,1024]{1,0:T(8,128)(2,1)}, bf16[192,1024]{1,0:T(8,128)(2,1)}, bf16[192,1024]{1,0:T(8,128)(2,1)}) custom-call(s32[6]{0:T(128)} %pad_add_fusion.refs_0_, bf16[192,1024]{1,0:T(8,128)(2,1)} %bitcast.62, bf16[192,1024]{1,0:T(8,128)(2,1)} %bitcast.63, bf16[1024,1024]{1,0:T(8,128)(2,1)} %refs_2_.5, ...), custom_call_target="tpu_custom_call" | custom-call | tf_op jit(solution)/shard_map/front/pallas_call | solution.py:263
  15.3 4.7 %collective-permute-start.2 = (bf16[192,1024]{1,0:T(8,128)(2,1)}, bf16[192,1024]{1,0:T(8,128)(2,1)}, u32[]{:S(2)}, u32[]{:S(2)}) collective-permute-start(bf16[192,1024]{1,0:T(8,128)(2,1)} %get-tuple-element.124.refs_3_.refs_1_), channel_id=1, source_target_pairs={{2,0},{4,2},{6,4},{0,6},{3,1},{5,3},{7,5},{1,7},{10,8},{12,10},{14... | collective-permute-start | bytes 1179656 | tf_op jit(solution)/shard_map/ppermute | solution.py:917
  21.1 4.9 %fusion.94.refs_11_.refs_8_ = f32[192,2048]{1,0:T(8,128)} fusion(bf16[192,1024]{1,0:T(8,128)(2,1)S(1)} %bitcast.43, bf16[2048,1024]{1,0:T(8,128)(2,1)} %refs_5_.5), kind=kOutput, calls=%fused_computation.146 | convolution fusion | flops 805306368 | bytes 6160384 | tf_op jit(solution)/shard_map/dot_general | solution.py:40
  27.3 4.9 %fusion.95.refs_12_.refs_9_ = f32[192,2048]{1,0:T(8,128)} fusion(bf16[192,1024]{1,0:T(8,128)(2,1)S(1)} %bitcast.44, bf16[2048,1024]{1,0:T(8,128)(2,1)} %collective-permute-done.6.refs_6_), kind=kOutput, calls=%fused_computation.147 | convolution fusion | flops 805306368 | bytes 6160384 | tf_op jit(solution)/shard_map/dot_general | solution.py:40
  32.2 22.3 %collective-permute-done.3.refs_3_ = bf16[192,1024]{1,0:T(8,128)(2,1)} collective-permute-done((bf16[192,1024]{1,0:T(8,128)(2,1)}, bf16[192,1024]{1,0:T(8,128)(2,1)}, u32[]{:S(2)}, u32[]{:S(2)}) %collective-permute-start.3) | collective-permute-done | bytes 393248 | tf_op jit(solution)/shard_map/ppermute | solution.py:917
  56.1 9.7 %project.1 = (bf16[192,1024]{1,0:T(8,128)(2,1)}, bf16[768,1024]{1,0:T(8,128)(2,1)}, bf16[768,1024]{1,0:T(8,128)(2,1)}, bf16[768,512]{1,0:T(8,128)(2,1)}, bf16[768,512]{1,0:T(8,128)(2,1)}) custom-call(s32[6]{0:T(128)} %pad_add_fusion.refs_0_, bf16[192,1024]{1,0:T(8,128)(2,1)} %get-tuple-element.124.refs_3_.refs_1_, ...), custom_call_target="tpu_custom_call" | custom-call | tf_op jit(solution)/shard_map/project/pallas_call | solution.py:373
  66.5 11.1 %attend_forward.1 = (bf16[192,1024]{1,0:T(8,128)(2,1)}, bf16[8,768,384]{2,1,0:T(8,128)(2,1)}) custom-call(s32[6]{0:T(128)} %pad_add_fusion.refs_0_, bf16[192,1024]{1,0:T(8,128)(2,1)} %get-tuple-element.130.refs_1_.refs_0_, bf16[768,1024]{1,0:T(8,128)(2,1)} %get-tuple-element.131.refs_2_.refs_1_, bf16[768,1024]{1,0:T(8,128)(2,1)} %get-tuple-element.132.refs_3_.refs_2_), custom_call_target="tpu_custom_call" | custom-call | tf_op jit(solution)/shard_map/attend_forward/pallas_call | solution.py:148
  79.9 19.0 %centre.1 = (f32[192,1024]{1,0:T(8,128)}, bf16[192,4096]{1,0:T(8,128)(2,1)}, f32[192,1024]{1,0:T(8,128)}, bf16[192,1024]{1,0:T(8,128)(2,1)}, bf16[192,1024]{1,0:...) custom-call(s32[6]{0:T(128)} %pad_add_fusion.refs_0_, ...), custom_call_target="tpu_custom_call" | custom-call | tf_op jit(solution)/shard_map/centre/pallas_call | solution.py:513
  109.2 11.6 %attend_backward.1.refs_1_ = bf16[3,768,1024]{2,1,0:T(8,128)(2,1)} custom-call(bf16[192,1024]{1,0:T(8,128)(2,1)} %get-tuple-element.130.refs_1_.refs_0_, bf16[768,1024]{1,0:T(8,128)(2,1)} %get-tuple-element.131.refs_2_.refs_1_, bf16[768,1024]{1,0:T(8,128)(2,1)} %get-tuple-element.132.refs_3_.refs_2_, bf16[192,1024]{1,0:T(8,128)(2,1)} %get-tuple-element.150.refs_3_, ...), custom_call_target="tpu_custom_call" | custom-call | tf_op jit(solution)/shard_map/attend_backward/pallas_call | solution.py:180
  120.8 13.6 %unproject.1 = (bf16[4,192,1024]{2,1,0:T(8,128)(2,1)}, bf16[768,3072]{1,0:T(8,128)(2,1)}) custom-call(s32[6]{0:T(128)} %pad_add_fusion.refs_0_, bf16[3,768,1024]{2,1,0:T(8,128)(2,1)} %attend_backward.1.refs_1_, bf16[512,3072]{1,0:T(8,128)(2,1)} %refs_2_.4, bf16[512,3072]{1,0:T(8,128)(2,1)} %copy-done, ...), custom_call_target="tpu_custom_call" | custom-call | tf_op jit(solution)/shard_map/unproject/pallas_call | solution.py:583
  144.5 4.4 all-to-all-start
  158.1 5.8 %collective-permute-done.17 = bf16[512,512]{1,0:T(8,128)(2,1)S(1)} collective-permute-done((bf16[512,512]{1,0:T(8,128)(2,1)}, bf16[512,512]{1,0:T(8,128)(2,1)S(1)}, u32[]{:S(2)}, u32[]{:S(2)}) %collective-permute-start.17) | collective-permute-done | bytes 524320 | tf_op jit(solution)/shard_map/ppermute | solution.py:914
  169.0 18.0 %all-to-all-done.refs_0_ = bf16[4,192,1024]{2,1,0:T(8,128)(2,1)} async-done(((bf16[4,192,1024]{2,1,0:T(8,128)(2,1)}), bf16[4,192,1024]{2,1,0:T(8,128)(2,1)}, u32[]{:S(2)}, u32[]{:S(2)}) %all-to-all-start) | async-done | bytes 1572896 | tf_op jit(solution)/shard_map/all_to_all | solution.py:925
  187.0 4.3 all-to-all-start.1
  220.0 5.4 %collective-permute-done.24 = bf16[128,2048]{1,0:T(8,128)(2,1)S(1)} collective-permute-done((bf16[128,2048]{1,0:T(8,128)(2,1)S(1)}, bf16[128,2048]{1,0:T(8,128)(2,1)S(1)}, u32[]{:S(2)}, u32[]{:S(2)}) %collective-permute-start.24) | collective-permute-done | bytes 524320 | tf_op jit(solution)/shard_map/ppermute | solution.py:911
  230.3 5.4 %all-to-all-start.2 = ((bf16[4,32,4096]{2,1,0:T(8,128)(2,1)}), bf16[4,32,4096]{2,1,0:T(8,128)(2,1)S(1)}, u32[]{:S(2)}, u32[]{:S(2)}) async-start(bf16[4,32,4096]{2,1,0:T(8,128)(2,1)} %bitcast.52), calls=%async_computation.2 | async-start | bytes 2097152 | tf_op jit(solution)/shard_map/all_to_all | solution.py:925
  263.5 4.8 %all-to-all-start.3 = ((bf16[4,128,1024]{2,1,0:T(8,128)(2,1)}), bf16[4,128,1024]{2,1,0:T(8,128)(2,1)}, u32[]{:S(2)}, u32[]{:S(2)}) async-start(bf16[4,128,1024]{2,1,0:T(8,128)(2,1)} %fold.4), calls=%async_computation.3 | async-start | bytes 2097152 | tf_op jit(solution)/shard_map/all_to_all | solution.py:925
  283.0 6.0 %all-to-all-done.3 = bf16[4,128,1024]{2,1,0:T(8,128)(2,1)} async-done(((bf16[4,128,1024]{2,1,0:T(8,128)(2,1)}), bf16[4,128,1024]{2,1,0:T(8,128)(2,1)}, u32[]{:S(2)}, u32[]{:S(2)}) %all-to-all-start.3) | async-done | bytes 1048608 | tf_op jit(solution)/shard_map/all_to_all | solution.py:925
  289.0 4.3 all-to-all-start.4
  301.7 4.1 fusion.2
  306.5 9.1 %all-to-all-done.4 = bf16[4,32,4096]{2,1,0:T(8,128)(2,1)} async-done(((bf16[4,32,4096]{2,1,0:T(8,128)(2,1)}), bf16[4,32,4096]{2,1,0:T(8,128)(2,1)}, u32[]{:S(2)}, u32[]{:S(2)}) %all-to-all-start.4) | async-done | bytes 1048608 | tf_op jit(solution)/shard_map/all_to_all | solution.py:925
  324.2 7.5 %forward.1 = bf16[192,1024]{1,0:T(8,128)(2,1)} custom-call(s32[6]{0:T(128)} %pad_add_fusion.refs_0_, f32[192,1024]{1,0:T(8,128)} %get-tuple-element.144.refs_1_, f32[1,1024]{1,0:T(1,128)} %get-tuple-element.145.refs_2_, bf16[192,2048]{1,0:T(8,128)(2,1)} %get-tuple-element.146.refs_3_, bf16[192,2048]{1,0:T(8,128)(2,1)} %get-tuple-element.147.refs_4_, ...), custom_call_target="tpu_custom_call" | custom-call | tf_op jit(solution)/shard_map/forward/pallas_call | solution.py:659
  335.2 5.8 %input_grads.1 = (f32[192,1024]{1,0:T(8,128)}, f32[192,1024]{1,0:T(8,128)}) custom-call(s32[6]{0:T(128)} %pad_add_fusion.refs_0_, bf16[192,1024]{1,0:T(8,128)(2,1)} %get-tuple-element.180.refs_1_, bf16[1024,1024]{1,0:T(8,128)(2,1)} %refs_2_.5, bf16[1024,1024]{1,0:T(8,128)(2,1)} %collective-permute-done.refs_4_.refs_3_, bf16[4,96,1024]{2,1,0:T(8,128)(2,1)} %fusion.24.refs_4_), custom_call_target="tpu_custom_call" | custom-call | tf_op jit(solution)/shard_map/input_grads/pallas_call | solution.py:730
  345.4 4.6 collective-permute-done.40.refs_3_
  350.7 5.0 %all-to-all-start.6 = ((bf16[4,32,3072]{2,1,0:T(8,128)(2,1)}), bf16[4,32,3072]{2,1,0:T(8,128)(2,1)S(1)}, u32[]{:S(2)}, u32[]{:S(2)}) async-start(bf16[4,32,3072]{2,1,0:T(8,128)(2,1)} %fold.6), calls=%async_computation.6 | async-start | bytes 1572864 | tf_op jit(solution)/shard_map/all_to_all | solution.py:925
  359.7 7.0 %collective-permute-done.38.refs_5_ = bf16[512,512]{1,0:T(8,128)(2,1)S(1)} collective-permute-done((bf16[512,512]{1,0:T(8,128)(2,1)S(1)}, bf16[512,512]{1,0:T(8,128)(2,1)S(1)}, u32[]{:S(2)}, u32[]{:S(2)}) %collective-permute-start.38) | collective-permute-done | bytes 524320 | tf_op jit(solution)/shard_map/ppermute | solution.py:914
  382.4 7.9 %place.5.refs_2_ = f32[2048,1024]{1,0:T(8,128)} custom-call(s32[1]{0:T(128)} %bitcast.2.refs_0_, bf16[512,1024]{1,0:T(8,128)(2,1)} %bitcast.16.refs_1_, bf16[512,1024]{1,0:T(8,128)(2,1)} %collective-permute-done.36.refs_2_, bf16[512,1024]{1,0:T(8,128)(2,1)} %collective-permute-done.35.refs_3_, bf16[512,512]{1,0:T(8,128)(2,1)} %collective-permute-done.37.refs_4_, ...), custom_call_target="tpu_custom_call" | custom-call | tf_op jit(solution)/shard_map/place/pallas_call | solution.py:839
  408.4 7.2 %collective-permute-done.45.refs_5_ = bf16[128,2048]{1,0:T(8,128)(2,1)S(1)} collective-permute-done((bf16[128,2048]{1,0:T(8,128)(2,1)S(1)}, bf16[128,2048]{1,0:T(8,128)(2,1)S(1)}, u32[]{:S(2)}, u32[]{:S(2)}) %collective-permute-start.45) | collective-permute-done | bytes 524320 | tf_op jit(solution)/shard_map/ppermute | solution.py:914
  418.6 7.9 %place.6.refs_6_ = f32[512,4096]{1,0:T(8,128)} custom-call(s32[1]{0:T(128)} %bitcast.2.refs_0_, bf16[128,4096]{1,0:T(8,128)(2,1)} %bitcast.17.refs_1_, bf16[128,4096]{1,0:T(8,128)(2,1)} %collective-permute-done.39.refs_2_, bf16[128,4096]{1,0:T(8,128)(2,1)} %collective-permute-done.40.refs_3_, bf16[128,2048]{1,0:T(8,128)(2,1)} %copy-done.38, ...), custom_call_target="tpu_custom_call" | custom-call | tf_op jit(solution)/shard_map/place/pallas_call | solution.py:839
  431.4 5.2 %all-to-all-start.9 = ((f32[16,1,5632]{2,1,0:T(1,128)}), f32[16,1,5632]{2,1,0:T(1,128)S(1)}, u32[]{:S(2)}, u32[]{:S(2)}) async-start(f32[16,1,5632]{2,1,0:T(1,128)} %broadcast_in_dim.9), calls=%async_computation.9 | async-start | bytes 720896 | tf_op jit(solution)/shard_map/all_to_all | solution.py:1194
  436.6 7.4 %place.7.refs_6_ = f32[512,3072]{1,0:T(8,128)} custom-call(s32[1]{0:T(128)} %bitcast.2.refs_0_, bf16[128,3072]{1,0:T(8,128)(2,1)} %bitcast.57, bf16[128,3072]{1,0:T(8,128)(2,1)} %copy-done.25, bf16[128,3072]{1,0:T(8,128)(2,1)} %copy-done.24, bf16[128,1536]{1,0:T(8,128)(2,1)} %collective-permute-done.48.refs_4_, ...), custom_call_target="tpu_custom_call" | custom-call | tf_op jit(solution)/shard_map/place/pallas_call | solution.py:839
  (285 shorter events, 215.7 us)
Async XLA Ops:
  8.3 46.1 %collective-permute-start.5 = (bf16[512,3072]{1,0:T(8,128)(2,1)}, bf16[512,3072]{1,0:T(8,128)(2,1)S(1)}, u32[]{:S(2)}, u32[]{:S(2)}) collective-permute-start(bf16[512,3072]{1,0:T(8,128)(2,1)} %refs_2_.4), channel_id=1, source_target_pairs={{0,1},{1,0},{2,3},{3,2},{4,5},{5,4},{6,7},{7,6},{8,9},{9,8},{10,11... | collective-permute-start | bytes 9437192 | tf_op jit(solution)/shard_map/ppermute | solution.py:908
  14.9 63.7 %collective-permute-start.8 = (bf16[512,4096]{1,0:T(8,128)(2,1)}, bf16[512,4096]{1,0:T(8,128)(2,1)}, u32[]{:S(2)}, u32[]{:S(2)}) collective-permute-start(bf16[512,4096]{1,0:T(8,128)(2,1)} %refs_6_.5), channel_id=1, source_target_pairs={{0,1},{1,0},{2,3},{3,2},{4,5},{5,4},{6,7},{7,6},{8,9},{9,8},{10,11... | collective-permute-start | bytes 12582920 | tf_op jit(solution)/shard_map/ppermute | solution.py:908
  20.1 34.4 %collective-permute-start.3 = (bf16[192,1024]{1,0:T(8,128)(2,1)}, bf16[192,1024]{1,0:T(8,128)(2,1)}, u32[]{:S(2)}, u32[]{:S(2)}) collective-permute-start(bf16[192,1024]{1,0:T(8,128)(2,1)} %get-tuple-element.124.refs_3_.refs_1_), channel_id=1, source_target_pairs={{4,0},{6,2},{0,4},{2,6},{5,1},{7,3},{1,5},{3,7},{12,8},{14,10},{8,... | collective-permute-start | bytes 1179656 | tf_op jit(solution)/shard_map/ppermute | solution.py:917
  20.1 34.4 %collective-permute-start.4 = (bf16[192,1024]{1,0:T(8,128)(2,1)}, bf16[192,1024]{1,0:T(8,128)(2,1)}, u32[]{:S(2)}, u32[]{:S(2)}) collective-permute-start(bf16[192,1024]{1,0:T(8,128)(2,1)} %get-tuple-element.124.refs_3_.refs_1_), channel_id=1, source_target_pairs={{6,0},{0,2},{2,4},{4,6},{7,1},{1,3},{3,5},{5,7},{14,8},{8,10},{10,... | collective-permute-start | bytes 1179656 | tf_op jit(solution)/shard_map/ppermute | solution.py:917
  99.6 34.8 %collective-permute-start.15 = (bf16[192,4096]{1,0:T(8,128)(2,1)}, bf16[192,4096]{1,0:T(8,128)(2,1)}, u32[]{:S(2)}, u32[]{:S(2)}) collective-permute-start(bf16[192,4096]{1,0:T(8,128)(2,1)} %get-tuple-element.156), channel_id=1, source_target_pairs={{0,1},{1,0},{2,3},{3,2},{4,5},{5,4},{6,7},{7,6},{8,9},{9,8},{10,11... | collective-permute-start | bytes 4718600 | tf_op jit(solution)/shard_map/ppermute | solution.py:908
  103.4 32.7 %collective-permute-start.14 = (bf16[1024,512]{1,0:T(8,128)(2,1)}, bf16[1024,512]{1,0:T(8,128)(2,1)}, u32[]{:S(2)}, u32[]{:S(2)}) collective-permute-start(bf16[1024,512]{1,0:T(8,128)(2,1)} %convolution_convert_fusion.2.refs_5_.refs_4_), channel_id=1, source_target_pairs={{0,8},{8,0},{16,24},{24,16},{1,9},{9,1},{17,25},{25,17},{2,10},{10... | collective-permute-start | bytes 3145736 | tf_op jit(solution)/shard_map/ppermute | solution.py:911
  106.8 29.3 %collective-permute-start.13 = (bf16[1024,512]{1,0:T(8,128)(2,1)}, bf16[1024,512]{1,0:T(8,128)(2,1)}, u32[]{:S(2)}, u32[]{:S(2)}) collective-permute-start(bf16[1024,512]{1,0:T(8,128)(2,1)} %convolution_convert_fusion.3.refs_6_.refs_5_), channel_id=1, source_target_pairs={{0,16},{8,24},{16,0},{24,8},{1,17},{9,25},{17,1},{25,9},{2,18},{10... | collective-permute-start | bytes 3145736 | tf_op jit(solution)/shard_map/ppermute | solution.py:914
  144.5 46.8 %collective-permute-start.19 = (bf16[768,3072]{1,0:T(8,128)(2,1)}, bf16[768,3072]{1,0:T(8,128)(2,1)}, u32[]{:S(2)}, u32[]{:S(2)}) collective-permute-start(bf16[768,3072]{1,0:T(8,128)(2,1)} %get-tuple-element.162), channel_id=1, source_target_pairs={{0,1},{1,0},{2,3},{3,2},{4,5},{5,4},{6,7},{7,6},{8,9},{9,8},{10,11... | collective-permute-start | bytes 14155784 | tf_op jit(solution)/shard_map/ppermute | solution.py:908
  144.5 42.5 %all-to-all-start = ((bf16[4,192,1024]{2,1,0:T(8,128)(2,1)}), bf16[4,192,1024]{2,1,0:T(8,128)(2,1)}, u32[]{:S(2)}, u32[]{:S(2)}) async-start(bf16[4,192,1024]{2,1,0:T(8,128)(2,1)} %get-tuple-element.158), calls=%async_computation | async-start | bytes 3145728 | tf_op jit(solution)/shard_map/all_to_all | solution.py:925
  150.4 44.4 %collective-permute-start.20 = (bf16[256,2048]{1,0:T(8,128)(2,1)}, bf16[256,2048]{1,0:T(8,128)(2,1)}, u32[]{:S(2)}, u32[]{:S(2)}) collective-permute-start(bf16[256,2048]{1,0:T(8,128)(2,1)} %convolution_convert_fusion), channel_id=1, source_target_pairs={{0,8},{8,0},{16,24},{24,16},{1,9},{9,1},{17,25},{25,17},{2,10},{10... | collective-permute-start | bytes 3145736 | tf_op jit(solution)/shard_map/ppermute | solution.py:911
  153.6 43.6 %collective-permute-start.16 = (bf16[256,2048]{1,0:T(8,128)(2,1)}, bf16[256,2048]{1,0:T(8,128)(2,1)}, u32[]{:S(2)}, u32[]{:S(2)}) collective-permute-start(bf16[256,2048]{1,0:T(8,128)(2,1)} %convolution_convert_fusion.1), channel_id=1, source_target_pairs={{0,16},{8,24},{16,0},{24,8},{1,17},{9,25},{17,1},{25,9},{2,18},{10... | collective-permute-start | bytes 3145736 | tf_op jit(solution)/shard_map/ppermute | solution.py:914
  187.0 43.4 %all-to-all-start.1 = ((bf16[4,128,1024]{2,1,0:T(8,128)(2,1)}), bf16[4,128,1024]{2,1,0:T(8,128)(2,1)}, u32[]{:S(2)}, u32[]{:S(2)}) async-start(bf16[4,128,1024]{2,1,0:T(8,128)(2,1)} %bitcast.53), calls=%async_computation.1 | async-start | bytes 2097152 | tf_op jit(solution)/shard_map/all_to_all | solution.py:925
  196.4 23.0 %collective-permute-start.23 = (bf16[128,2048]{1,0:T(8,128)(2,1)S(1)}, bf16[128,2048]{1,0:T(8,128)(2,1)S(1)}, u32[]{:S(2)}, u32[]{:S(2)}) collective-permute-start(bf16[128,2048]{1,0:T(8,128)(2,1)S(1)} %fusion.10), channel_id=1, source_target_pairs={{0,16},{8,24},{16,0},{24,8},{1,17},{9,25},{17,1},{25,9},{2,18},{10... | collective-permute-start | bytes 1572872 | tf_op jit(solution)/shard_map/ppermute | solution.py:914
  211.7 38.7 %collective-permute-start.21 = (bf16[256,1536]{1,0:T(8,128)(2,1)}, bf16[256,1536]{1,0:T(8,128)(2,1)}, u32[]{:S(2)}, u32[]{:S(2)}) collective-permute-start(bf16[256,1536]{1,0:T(8,128)(2,1)} %fusion.3), channel_id=1, source_target_pairs={{0,8},{8,0},{16,24},{24,16},{1,9},{9,1},{17,25},{25,17},{2,10},{10... | collective-permute-start | bytes 2359304 | tf_op jit(solution)/shard_map/ppermute | solution.py:911
  217.9 32.5 %collective-permute-start.28 = (bf16[256,1536]{1,0:T(8,128)(2,1)}, bf16[256,1536]{1,0:T(8,128)(2,1)}, u32[]{:S(2)}, u32[]{:S(2)}) collective-permute-start(bf16[256,1536]{1,0:T(8,128)(2,1)} %fusion.4), channel_id=1, source_target_pairs={{0,16},{8,24},{16,0},{24,8},{1,17},{9,25},{17,1},{25,9},{2,18},{10... | collective-permute-start | bytes 2359304 | tf_op jit(solution)/shard_map/ppermute | solution.py:914
  219.4 22.7 %collective-permute-start.27 = (bf16[192,1024]{1,0:T(8,128)(2,1)}, bf16[192,1024]{1,0:T(8,128)(2,1)}, u32[]{:S(2)}, u32[]{:S(2)}) collective-permute-start(bf16[192,1024]{1,0:T(8,128)(2,1)} %get-tuple-element.182), channel_id=1, source_target_pairs={{0,1},{1,0},{2,3},{3,2},{4,5},{5,4},{6,7},{7,6},{8,9},{9,8},{10,11... | collective-permute-start | bytes 1179656 | tf_op jit(solution)/shard_map/ppermute | solution.py:908
  230.3 32.2 %all-to-all-start.2 = ((bf16[4,32,4096]{2,1,0:T(8,128)(2,1)}), bf16[4,32,4096]{2,1,0:T(8,128)(2,1)S(1)}, u32[]{:S(2)}, u32[]{:S(2)}) async-start(bf16[4,32,4096]{2,1,0:T(8,128)(2,1)} %bitcast.52), calls=%async_computation.2 | async-start | bytes 2097152 | tf_op jit(solution)/shard_map/all_to_all | solution.py:925
  263.5 25.5 %all-to-all-start.3 = ((bf16[4,128,1024]{2,1,0:T(8,128)(2,1)}), bf16[4,128,1024]{2,1,0:T(8,128)(2,1)}, u32[]{:S(2)}, u32[]{:S(2)}) async-start(bf16[4,128,1024]{2,1,0:T(8,128)(2,1)} %fold.4), calls=%async_computation.3 | async-start | bytes 2097152 | tf_op jit(solution)/shard_map/all_to_all | solution.py:925
  289.0 26.6 %all-to-all-start.4 = ((bf16[4,32,4096]{2,1,0:T(8,128)(2,1)}), bf16[4,32,4096]{2,1,0:T(8,128)(2,1)}, u32[]{:S(2)}, u32[]{:S(2)}) async-start(bf16[4,32,4096]{2,1,0:T(8,128)(2,1)} %fold.5), calls=%async_computation.4 | async-start | bytes 2097152 | tf_op jit(solution)/shard_map/all_to_all | solution.py:925
  305.8 39.5 %collective-permute-start.36 = (bf16[512,1024]{1,0:T(8,128)(2,1)}, bf16[512,1024]{1,0:T(8,128)(2,1)}, u32[]{:S(2)}, u32[]{:S(2)}) collective-permute-start(bf16[512,1024]{1,0:T(8,128)(2,1)} %bitcast.16.refs_1_), channel_id=1, source_target_pairs={{0,8},{8,0},{16,24},{24,16},{1,9},{9,1},{17,25},{25,17},{2,10},{10... | collective-permute-start | bytes 3145736 | tf_op jit(solution)/shard_map/ppermute | solution.py:911
  306.5 38.9 %collective-permute-start.35 = (bf16[512,1024]{1,0:T(8,128)(2,1)}, bf16[512,1024]{1,0:T(8,128)(2,1)}, u32[]{:S(2)}, u32[]{:S(2)}) collective-permute-start(bf16[512,1024]{1,0:T(8,128)(2,1)} %bitcast.16.refs_1_), channel_id=1, source_target_pairs={{0,16},{8,24},{16,0},{24,8},{1,17},{9,25},{17,1},{25,9},{2,18},{10... | collective-permute-start | bytes 3145736 | tf_op jit(solution)/shard_map/ppermute | solution.py:914
  315.6 34.4 %collective-permute-start.40 = (bf16[128,4096]{1,0:T(8,128)(2,1)}, bf16[128,4096]{1,0:T(8,128)(2,1)}, u32[]{:S(2)}, u32[]{:S(2)}) collective-permute-start(bf16[128,4096]{1,0:T(8,128)(2,1)} %bitcast.17.refs_1_), channel_id=1, source_target_pairs={{0,16},{8,24},{16,0},{24,8},{1,17},{9,25},{17,1},{25,9},{2,18},{10... | collective-permute-start | bytes 3145736 | tf_op jit(solution)/shard_map/ppermute | solution.py:914
  317.9 32.8 %collective-permute-start.39 = (bf16[128,4096]{1,0:T(8,128)(2,1)}, bf16[128,4096]{1,0:T(8,128)(2,1)}, u32[]{:S(2)}, u32[]{:S(2)}) collective-permute-start(bf16[128,4096]{1,0:T(8,128)(2,1)} %bitcast.17.refs_1_), channel_id=1, source_target_pairs={{0,8},{8,0},{16,24},{24,16},{1,9},{9,1},{17,25},{25,17},{2,10},{10... | collective-permute-start | bytes 3145736 | tf_op jit(solution)/shard_map/ppermute | solution.py:911
  319.3 21.9 %all-to-all-start.5 = ((bf16[4,32,3072]{2,1,0:T(8,128)(2,1)}), bf16[4,32,3072]{2,1,0:T(8,128)(2,1)S(1)}, u32[]{:S(2)}, u32[]{:S(2)}) async-start(bf16[4,32,3072]{2,1,0:T(8,128)(2,1)} %bitcast.9.refs_7_), calls=%async_computation.5 | async-start | bytes 1572864 | tf_op jit(solution)/shard_map/all_to_all | solution.py:925
  350.7 21.5 %all-to-all-start.6 = ((bf16[4,32,3072]{2,1,0:T(8,128)(2,1)}), bf16[4,32,3072]{2,1,0:T(8,128)(2,1)S(1)}, u32[]{:S(2)}, u32[]{:S(2)}) async-start(bf16[4,32,3072]{2,1,0:T(8,128)(2,1)} %fold.6), calls=%async_computation.6 | async-start | bytes 1572864 | tf_op jit(solution)/shard_map/all_to_all | solution.py:925
  372.2 20.9 %all-to-all-start.7 = ((bf16[4,96,1024]{2,1,0:T(8,128)(2,1)}), bf16[4,96,1024]{2,1,0:T(8,128)(2,1)S(1)}, u32[]{:S(2)}, u32[]{:S(2)}) async-start(bf16[4,96,1024]{2,1,0:T(8,128)(2,1)} %fusion.24.refs_4_), calls=%async_computation.7 | async-start | bytes 1572864 | tf_op jit(solution)/shard_map/all_to_all | solution.py:925
  396.1 30.5 %all-to-all-start.8 = ((bf16[4,96,1024]{2,1,0:T(8,128)(2,1)}), bf16[4,96,1024]{2,1,0:T(8,128)(2,1)S(1)}, u32[]{:S(2)}, u32[]{:S(2)}) async-start(bf16[4,96,1024]{2,1,0:T(8,128)(2,1)} %fold.7), calls=%async_computation.8 | async-start | bytes 1572864 | tf_op jit(solution)/shard_map/all_to_all | solution.py:925
  405.9 24.6 %collective-permute-start.49 = (bf16[128,1536]{1,0:T(8,128)(2,1)}, bf16[128,1536]{1,0:T(8,128)(2,1)}, u32[]{:S(2)}, u32[]{:S(2)}) collective-permute-start(bf16[128,1536]{1,0:T(8,128)(2,1)} %slice.382), channel_id=1, source_target_pairs={{0,16},{8,24},{16,0},{24,8},{1,17},{9,25},{17,1},{25,9},{2,18},{10... | collective-permute-start | bytes 1179656 | tf_op jit(solution)/shard_map/ppermute | solution.py:914
  408.4 22.1 %collective-permute-start.48 = (bf16[128,1536]{1,0:T(8,128)(2,1)}, bf16[128,1536]{1,0:T(8,128)(2,1)}, u32[]{:S(2)}, u32[]{:S(2)}) collective-permute-start(bf16[128,1536]{1,0:T(8,128)(2,1)} %slice.381), channel_id=1, source_target_pairs={{0,8},{8,0},{16,24},{24,16},{1,9},{9,1},{17,25},{25,17},{2,10},{10... | collective-permute-start | bytes 1179656 | tf_op jit(solution)/shard_map/ppermute | solution.py:911
  426.6 21.3 %collective-permute-start.46 = (bf16[384,1024]{1,0:T(8,128)(2,1)S(1)}, bf16[384,1024]{1,0:T(8,128)(2,1)S(1)}, u32[]{:S(2)}, u32[]{:S(2)}) collective-permute-start(bf16[384,1024]{1,0:T(8,128)(2,1)S(1)} %bitcast.37), channel_id=1, source_target_pairs={{0,8},{8,0},{16,24},{24,16},{1,9},{9,1},{17,25},{25,17},{2,10},{10... | collective-permute-start | bytes 2359304 | tf_op jit(solution)/shard_map/ppermute | solution.py:911
  428.7 22.0 %collective-permute-start.47 = (bf16[384,1024]{1,0:T(8,128)(2,1)S(1)}, bf16[384,1024]{1,0:T(8,128)(2,1)S(1)}, u32[]{:S(2)}, u32[]{:S(2)}) collective-permute-start(bf16[384,1024]{1,0:T(8,128)(2,1)S(1)} %bitcast.38), channel_id=1, source_target_pairs={{0,16},{8,24},{16,0},{24,8},{1,17},{9,25},{17,1},{25,9},{2,18},{10... | collective-permute-start | bytes 2359304 | tf_op jit(solution)/shard_map/ppermute | solution.py:914
  431.4 20.7 %all-to-all-start.9 = ((f32[16,1,5632]{2,1,0:T(1,128)}), f32[16,1,5632]{2,1,0:T(1,128)S(1)}, u32[]{:S(2)}, u32[]{:S(2)}) async-start(f32[16,1,5632]{2,1,0:T(1,128)} %broadcast_in_dim.9), calls=%async_computation.9 | async-start | bytes 720896 | tf_op jit(solution)/shard_map/all_to_all | solution.py:1194
  (77 other events, 647.6 us)

commit v5 on v4

--- a/solution.py
+++ b/solution.py
@@ -1150,7 +1150,7 @@
     both_branch = right_rows(grad_branch, left_joined)
     rest = Chain([([left_joined], [right_rows(grad_z, left_att)]), ([left_att], [both_branch])])
     qkv_first = qkv.begin(up.next_x, up.next_y)
-    qkv.first()
+    qkv.first(up.then_x, up.then_y)
     up_own = up.own_sum(*qkv_first)
     up.across()
     rest_first = rest.begin(up_own)

time: 474 us -> 479 us (1.011)
    all_to_all x9, waiting for transfers between devices: 39.9 us -> 49.7 us  [exchange_seq(): return lax.all_to_all(array, 'seq', split_axis=0, concat_axis=0, tiled=True)]
    ppermute x3, waiting for transfers between devices: 22.3 us -> 13.9 us  [from_seq(): lax.ppermute(array, 'seq', [((i + step) % n_seq, i) for i in range(n_seq)])]
    all_to_all x9, starting transfers between devices: 38.7 us -> 45.2 us  [exchange_seq(): return lax.all_to_all(array, 'seq', split_axis=0, concat_axis=0, tiled=True)]
    unnamed x100 -> x96, local copies, waits for them, and re-layouts: 16.7 us -> 17 us
  transfers between devices with their start and end apart: 62 -> 62, of which waited for: 25 -> 21; matrix products, arithmetic and copies ran while one was open for 22% -> 22% of each run, Pallas kernels for 23% -> 23%
where the time goes in v5:
time: 479 us; the launch traced here: 471 us
  Pallas kernels  134 us (28%)
  waiting for transfers between devices  119 us (25%)
  starting transfers between devices  95.9 us (20%)
  matrix products  72.4 us (15%)
  local copies, waits for them, and re-layouts  28.8 us (6%)
  other arithmetic  19.4 us (4%)
    dot_general x34, matrix products, contract_rows(): lax.dot_general(left_side, right_side, (((0,), (0,)), ((), ())), preferre...  62.7 us
    all_to_all x9, waiting for transfers between devices, exchange_seq(): return lax.all_to_all(array, 'seq', split_axis=0, concat_axis=0, tiled=True)  49.7 us
    all_to_all x9, starting transfers between devices, exchange_seq(): return lax.all_to_all(array, 'seq', split_axis=0, concat_axis=0, tiled=True)  45.2 us
    pallas_call x5, Pallas kernels, place(): pl.pallas_call(kernel, grid_spec=pltpu.PrefetchScalarGridSpec(num_scalar_...  30.3 us
    ppermute x16, waiting for transfers between devices, over_y(): return lax.ppermute(array, 'batch', [(i, i ^ 2) for i in range(n_batch)])  27.9 us
    ppermute x16, waiting for transfers between devices, over_x(): return lax.ppermute(array, 'batch', [(i, i ^ 1) for i in range(n_batch)])  21.6 us
    pallas_call x1, Pallas kernels, centre(): pl.pallas_call(kernel, grid_spec=pltpu.PrefetchScalarGridSpec(num_scalar_...  19 us
    ppermute x16, starting transfers between devices, over_x(): return lax.ppermute(array, 'batch', [(i, i ^ 1) for i in range(n_batch)])  17.4 us
  transfers between devices with their start and end apart: 62, of which 21 were waited for; matrix products, arithmetic and copies ran while one was open for 22% of the time, Pallas kernels for 23%

profile of v5, /device:TPU:0, one launch (start us, length us, event | category | flops | bytes accessed | tf_op | source)
XLA Modules:
  0.0 471.3 jit_solution(3917693837372811113)
XLA Ops:
  2.6 4.1 collective-permute-done.1.refs_6_.refs_2_
  8.5 6.5 %front.1 = (f32[192,1024]{1,0:T(8,128)}, bf16[192,1024]{1,0:T(8,128)(2,1)}, bf16[192,1024]{1,0:T(8,128)(2,1)}, bf16[192,1024]{1,0:T(8,128)(2,1)}) custom-call(s32[6]{0:T(128)} %pad_add_fusion.refs_0_, bf16[192,1024]{1,0:T(8,128)(2,1)} %bitcast.62, bf16[192,1024]{1,0:T(8,128)(2,1)} %bitcast.63, bf16[1024,1024]{1,0:T(8,128)(2,1)} %refs_2_.5, ...), custom_call_target="tpu_custom_call" | custom-call | tf_op jit(solution)/shard_map/front/pallas_call | solution.py:263
  22.0 4.9 %fusion.94.refs_11_.refs_8_ = f32[192,2048]{1,0:T(8,128)} fusion(bf16[192,1024]{1,0:T(8,128)(2,1)S(1)} %bitcast.43, bf16[2048,1024]{1,0:T(8,128)(2,1)} %refs_5_.5), kind=kOutput, calls=%fused_computation.146 | convolution fusion | flops 805306368 | bytes 6160384 | tf_op jit(solution)/shard_map/dot_general | solution.py:40
  28.3 4.9 %fusion.95.refs_12_.refs_9_ = f32[192,2048]{1,0:T(8,128)} fusion(bf16[192,1024]{1,0:T(8,128)(2,1)S(1)} %bitcast.44, bf16[2048,1024]{1,0:T(8,128)(2,1)} %collective-permute-done.6.refs_6_), kind=kOutput, calls=%fused_computation.147 | convolution fusion | flops 805306368 | bytes 6160384 | tf_op jit(solution)/shard_map/dot_general | solution.py:40
  33.1 13.9 %collective-permute-done.3.refs_3_ = bf16[192,1024]{1,0:T(8,128)(2,1)} collective-permute-done((bf16[192,1024]{1,0:T(8,128)(2,1)}, bf16[192,1024]{1,0:T(8,128)(2,1)}, u32[]{:S(2)}, u32[]{:S(2)}) %collective-permute-start.3) | collective-permute-done | bytes 393248 | tf_op jit(solution)/shard_map/ppermute | solution.py:917
  48.7 9.7 %project.1 = (bf16[192,1024]{1,0:T(8,128)(2,1)}, bf16[768,1024]{1,0:T(8,128)(2,1)}, bf16[768,1024]{1,0:T(8,128)(2,1)}, bf16[768,512]{1,0:T(8,128)(2,1)}, bf16[768,512]{1,0:T(8,128)(2,1)}) custom-call(s32[6]{0:T(128)} %pad_add_fusion.refs_0_, bf16[192,1024]{1,0:T(8,128)(2,1)} %get-tuple-element.124.refs_3_.refs_1_, ...), custom_call_target="tpu_custom_call" | custom-call | tf_op jit(solution)/shard_map/project/pallas_call | solution.py:373
  59.0 11.1 %attend_forward.1 = (bf16[192,1024]{1,0:T(8,128)(2,1)}, bf16[8,768,384]{2,1,0:T(8,128)(2,1)}) custom-call(s32[6]{0:T(128)} %pad_add_fusion.refs_0_, bf16[192,1024]{1,0:T(8,128)(2,1)} %get-tuple-element.130.refs_1_.refs_0_, bf16[768,1024]{1,0:T(8,128)(2,1)} %get-tuple-element.131.refs_2_.refs_1_, bf16[768,1024]{1,0:T(8,128)(2,1)} %get-tuple-element.132.refs_3_.refs_2_), custom_call_target="tpu_custom_call" | custom-call | tf_op jit(solution)/shard_map/attend_forward/pallas_call | solution.py:148
  72.5 19.0 %centre.1 = (f32[192,1024]{1,0:T(8,128)}, bf16[192,4096]{1,0:T(8,128)(2,1)}, f32[192,1024]{1,0:T(8,128)}, bf16[192,1024]{1,0:T(8,128)(2,1)}, bf16[192,1024]{1,0:...) custom-call(s32[6]{0:T(128)} %pad_add_fusion.refs_0_, ...), custom_call_target="tpu_custom_call" | custom-call | tf_op jit(solution)/shard_map/centre/pallas_call | solution.py:513
  101.6 11.6 %attend_backward.1.refs_1_ = bf16[3,768,1024]{2,1,0:T(8,128)(2,1)} custom-call(bf16[192,1024]{1,0:T(8,128)(2,1)} %get-tuple-element.130.refs_1_.refs_0_, bf16[768,1024]{1,0:T(8,128)(2,1)} %get-tuple-element.131.refs_2_.refs_1_, bf16[768,1024]{1,0:T(8,128)(2,1)} %get-tuple-element.132.refs_3_.refs_2_, bf16[192,1024]{1,0:T(8,128)(2,1)} %get-tuple-element.150.refs_3_, ...), custom_call_target="tpu_custom_call" | custom-call | tf_op jit(solution)/shard_map/attend_backward/pallas_call | solution.py:180
  113.3 13.6 %unproject.1 = (bf16[4,192,1024]{2,1,0:T(8,128)(2,1)}, bf16[768,3072]{1,0:T(8,128)(2,1)}) custom-call(s32[6]{0:T(128)} %pad_add_fusion.refs_0_, bf16[3,768,1024]{2,1,0:T(8,128)(2,1)} %attend_backward.1.refs_1_, bf16[512,3072]{1,0:T(8,128)(2,1)} %refs_2_.4, bf16[512,3072]{1,0:T(8,128)(2,1)} %copy-done, ...), custom_call_target="tpu_custom_call" | custom-call | tf_op jit(solution)/shard_map/unproject/pallas_call | solution.py:583
  136.9 11.2 %all-to-all-start = ((bf16[4,192,1024]{2,1,0:T(8,128)(2,1)}), bf16[4,192,1024]{2,1,0:T(8,128)(2,1)}, u32[]{:S(2)}, u32[]{:S(2)}) async-start(bf16[4,192,1024]{2,1,0:T(8,128)(2,1)} %get-tuple-element.158), calls=%async_computation | async-start | bytes 3145728 | tf_op jit(solution)/shard_map/all_to_all | solution.py:925
  157.3 5.8 %collective-permute-done.18 = bf16[512,512]{1,0:T(8,128)(2,1)S(1)} collective-permute-done((bf16[512,512]{1,0:T(8,128)(2,1)}, bf16[512,512]{1,0:T(8,128)(2,1)S(1)}, u32[]{:S(2)}, u32[]{:S(2)}) %collective-permute-start.18) | collective-permute-done | bytes 524320 | tf_op jit(solution)/shard_map/ppermute | solution.py:911
  168.2 17.7 %all-to-all-done.refs_0_ = bf16[4,192,1024]{2,1,0:T(8,128)(2,1)} async-done(((bf16[4,192,1024]{2,1,0:T(8,128)(2,1)}), bf16[4,192,1024]{2,1,0:T(8,128)(2,1)}, u32[]{:S(2)}, u32[]{:S(2)}) %all-to-all-start) | async-done | bytes 1572896 | tf_op jit(solution)/shard_map/all_to_all | solution.py:925
  185.8 4.2 all-to-all-start.1
  223.7 5.4 %all-to-all-start.2 = ((bf16[4,32,4096]{2,1,0:T(8,128)(2,1)}), bf16[4,32,4096]{2,1,0:T(8,128)(2,1)S(1)}, u32[]{:S(2)}, u32[]{:S(2)}) async-start(bf16[4,32,4096]{2,1,0:T(8,128)(2,1)} %bitcast.52), calls=%async_computation.2 | async-start | bytes 2097152 | tf_op jit(solution)/shard_map/all_to_all | solution.py:925
  251.6 7.0 %collective-permute-done.31 = bf16[768,512]{1,0:T(8,128)(2,1)} collective-permute-done((bf16[768,512]{1,0:T(8,128)(2,1)}, bf16[768,512]{1,0:T(8,128)(2,1)}, u32[]{:S(2)}, u32[]{:S(2)}) %collective-permute-start.31) | collective-permute-done | bytes 786464 | tf_op jit(solution)/shard_map/ppermute | solution.py:911
  259.9 4.8 %all-to-all-start.3 = ((bf16[4,128,1024]{2,1,0:T(8,128)(2,1)}), bf16[4,128,1024]{2,1,0:T(8,128)(2,1)}, u32[]{:S(2)}, u32[]{:S(2)}) async-start(bf16[4,128,1024]{2,1,0:T(8,128)(2,1)} %fold.4), calls=%async_computation.3 | async-start | bytes 2097152 | tf_op jit(solution)/shard_map/all_to_all | solution.py:925
  278.9 9.7 %all-to-all-done.3 = bf16[4,128,1024]{2,1,0:T(8,128)(2,1)} async-done(((bf16[4,128,1024]{2,1,0:T(8,128)(2,1)}), bf16[4,128,1024]{2,1,0:T(8,128)(2,1)}, u32[]{:S(2)}, u32[]{:S(2)}) %all-to-all-start.3) | async-done | bytes 1048608 | tf_op jit(solution)/shard_map/all_to_all | solution.py:925
  288.5 4.3 all-to-all-start.4
  306.1 12.1 %all-to-all-done.4 = bf16[4,32,4096]{2,1,0:T(8,128)(2,1)} async-done(((bf16[4,32,4096]{2,1,0:T(8,128)(2,1)}), bf16[4,32,4096]{2,1,0:T(8,128)(2,1)}, u32[]{:S(2)}, u32[]{:S(2)}) %all-to-all-start.4) | async-done | bytes 1048608 | tf_op jit(solution)/shard_map/all_to_all | solution.py:925
  324.9 7.5 %forward.1 = bf16[192,1024]{1,0:T(8,128)(2,1)} custom-call(s32[6]{0:T(128)} %pad_add_fusion.refs_0_, f32[192,1024]{1,0:T(8,128)} %get-tuple-element.144.refs_1_, f32[1,1024]{1,0:T(1,128)} %get-tuple-element.145.refs_2_, bf16[192,2048]{1,0:T(8,128)(2,1)} %get-tuple-element.146.refs_3_, bf16[192,2048]{1,0:T(8,128)(2,1)} %get-tuple-element.147.refs_4_, ...), custom_call_target="tpu_custom_call" | custom-call | tf_op jit(solution)/shard_map/forward/pallas_call | solution.py:659
  336.0 5.8 %input_grads.1 = (f32[192,1024]{1,0:T(8,128)}, f32[192,1024]{1,0:T(8,128)}) custom-call(s32[6]{0:T(128)} %pad_add_fusion.refs_0_, bf16[192,1024]{1,0:T(8,128)(2,1)} %get-tuple-element.180.refs_1_, bf16[1024,1024]{1,0:T(8,128)(2,1)} %refs_2_.5, bf16[1024,1024]{1,0:T(8,128)(2,1)} %collective-permute-done.refs_4_.refs_3_, bf16[4,96,1024]{2,1,0:T(8,128)(2,1)} %fusion.24.refs_4_), custom_call_target="tpu_custom_call" | custom-call | tf_op jit(solution)/shard_map/input_grads/pallas_call | solution.py:730
  345.9 5.7 %collective-permute-done.40.refs_3_ = bf16[128,4096]{1,0:T(8,128)(2,1)} collective-permute-done((bf16[128,4096]{1,0:T(8,128)(2,1)}, bf16[128,4096]{1,0:T(8,128)(2,1)}, u32[]{:S(2)}, u32[]{:S(2)}) %collective-permute-start.40) | collective-permute-done | bytes 1048608 | tf_op jit(solution)/shard_map/ppermute | solution.py:914
  351.7 4.8 %all-to-all-start.6 = ((bf16[4,32,3072]{2,1,0:T(8,128)(2,1)}), bf16[4,32,3072]{2,1,0:T(8,128)(2,1)S(1)}, u32[]{:S(2)}, u32[]{:S(2)}) async-start(bf16[4,32,3072]{2,1,0:T(8,128)(2,1)} %fold.6), calls=%async_computation.6 | async-start | bytes 1572864 | tf_op jit(solution)/shard_map/all_to_all | solution.py:925
  360.0 10.9 %collective-permute-done.38.refs_5_ = bf16[512,512]{1,0:T(8,128)(2,1)S(1)} collective-permute-done((bf16[512,512]{1,0:T(8,128)(2,1)S(1)}, bf16[512,512]{1,0:T(8,128)(2,1)S(1)}, u32[]{:S(2)}, u32[]{:S(2)}) %collective-permute-start.38) | collective-permute-done | bytes 524320 | tf_op jit(solution)/shard_map/ppermute | solution.py:914
  384.0 7.9 %place.5.refs_2_ = f32[2048,1024]{1,0:T(8,128)} custom-call(s32[1]{0:T(128)} %bitcast.2.refs_0_, bf16[512,1024]{1,0:T(8,128)(2,1)} %bitcast.16.refs_1_, bf16[512,1024]{1,0:T(8,128)(2,1)} %collective-permute-done.36.refs_2_, bf16[512,1024]{1,0:T(8,128)(2,1)} %collective-permute-done.35.refs_3_, bf16[512,512]{1,0:T(8,128)(2,1)} %collective-permute-done.37.refs_4_, ...), custom_call_target="tpu_custom_call" | custom-call | tf_op jit(solution)/shard_map/place/pallas_call | solution.py:839
  391.9 6.6 %all-to-all-done.7.refs_0_ = bf16[4,96,1024]{2,1,0:T(8,128)(2,1)S(1)} async-done(((bf16[4,96,1024]{2,1,0:T(8,128)(2,1)}), bf16[4,96,1024]{2,1,0:T(8,128)(2,1)S(1)}, u32[]{:S(2)}, u32[]{:S(2)}) %all-to-all-start.7) | async-done | bytes 786464 | tf_op jit(solution)/shard_map/all_to_all | solution.py:925
  413.0 8.1 %collective-permute-done.45.refs_5_ = bf16[128,2048]{1,0:T(8,128)(2,1)S(1)} collective-permute-done((bf16[128,2048]{1,0:T(8,128)(2,1)S(1)}, bf16[128,2048]{1,0:T(8,128)(2,1)S(1)}, u32[]{:S(2)}, u32[]{:S(2)}) %collective-permute-start.45) | collective-permute-done | bytes 524320 | tf_op jit(solution)/shard_map/ppermute | solution.py:914
  423.0 7.9 %place.6.refs_6_ = f32[512,4096]{1,0:T(8,128)} custom-call(s32[1]{0:T(128)} %bitcast.2.refs_0_, bf16[128,4096]{1,0:T(8,128)(2,1)} %bitcast.17.refs_1_, bf16[128,4096]{1,0:T(8,128)(2,1)} %collective-permute-done.39.refs_2_, bf16[128,4096]{1,0:T(8,128)(2,1)} %collective-permute-done.40.refs_3_, bf16[128,2048]{1,0:T(8,128)(2,1)} %copy-done.38, ...), custom_call_target="tpu_custom_call" | custom-call | tf_op jit(solution)/shard_map/place/pallas_call | solution.py:839
  434.7 5.8 %all-to-all-start.9 = ((f32[16,1,5632]{2,1,0:T(1,128)}), f32[16,1,5632]{2,1,0:T(1,128)S(1)}, u32[]{:S(2)}, u32[]{:S(2)}) async-start(f32[16,1,5632]{2,1,0:T(1,128)} %broadcast_in_dim.9), calls=%async_computation.9 | async-start | bytes 720896 | tf_op jit(solution)/shard_map/all_to_all | solution.py:1194
  440.6 7.4 %place.7.refs_6_ = f32[512,3072]{1,0:T(8,128)} custom-call(s32[1]{0:T(128)} %bitcast.2.refs_0_, bf16[128,3072]{1,0:T(8,128)(2,1)} %bitcast.57, bf16[128,3072]{1,0:T(8,128)(2,1)} %copy-done.24, bf16[128,3072]{1,0:T(8,128)(2,1)} %copy-done.25, bf16[128,1536]{1,0:T(8,128)(2,1)} %collective-permute-done.48.refs_4_, ...), custom_call_target="tpu_custom_call" | custom-call | tf_op jit(solution)/shard_map/place/pallas_call | solution.py:839
  448.0 5.0 %collective-permute-done.46.refs_2_ = bf16[384,1024]{1,0:T(8,128)(2,1)S(1)} collective-permute-done((bf16[384,1024]{1,0:T(8,128)(2,1)S(1)}, bf16[384,1024]{1,0:T(8,128)(2,1)S(1)}, u32[]{:S(2)}, u32[]{:S(2)}) %collective-permute-start.46) | collective-permute-done | bytes 786464 | tf_op jit(solution)/shard_map/ppermute | solution.py:911
  (281 shorter events, 204.5 us)
Async XLA Ops:
  8.3 38.7 %collective-permute-start.5 = (bf16[512,3072]{1,0:T(8,128)(2,1)}, bf16[512,3072]{1,0:T(8,128)(2,1)S(1)}, u32[]{:S(2)}, u32[]{:S(2)}) collective-permute-start(bf16[512,3072]{1,0:T(8,128)(2,1)} %refs_2_.4), channel_id=1, source_target_pairs={{0,1},{1,0},{2,3},{3,2},{4,5},{5,4},{6,7},{7,6},{8,9},{9,8},{10,11... | collective-permute-start | bytes 9437192 | tf_op jit(solution)/shard_map/ppermute | solution.py:908
  14.9 56.3 %collective-permute-start.8 = (bf16[512,4096]{1,0:T(8,128)(2,1)}, bf16[512,4096]{1,0:T(8,128)(2,1)}, u32[]{:S(2)}, u32[]{:S(2)}) collective-permute-start(bf16[512,4096]{1,0:T(8,128)(2,1)} %refs_6_.5), channel_id=1, source_target_pairs={{0,1},{1,0},{2,3},{3,2},{4,5},{5,4},{6,7},{7,6},{8,9},{9,8},{10,11... | collective-permute-start | bytes 12582920 | tf_op jit(solution)/shard_map/ppermute | solution.py:908
  18.1 29.0 %collective-permute-start.3 = (bf16[192,1024]{1,0:T(8,128)(2,1)}, bf16[192,1024]{1,0:T(8,128)(2,1)}, u32[]{:S(2)}, u32[]{:S(2)}) collective-permute-start(bf16[192,1024]{1,0:T(8,128)(2,1)} %get-tuple-element.124.refs_3_.refs_1_), channel_id=1, source_target_pairs={{4,0},{6,2},{0,4},{2,6},{5,1},{7,3},{1,5},{3,7},{12,8},{14,10},{8,... | collective-permute-start | bytes 1179656 | tf_op jit(solution)/shard_map/ppermute | solution.py:917
  20.7 26.4 %collective-permute-start.2 = (bf16[192,1024]{1,0:T(8,128)(2,1)}, bf16[192,1024]{1,0:T(8,128)(2,1)}, u32[]{:S(2)}, u32[]{:S(2)}) collective-permute-start(bf16[192,1024]{1,0:T(8,128)(2,1)} %get-tuple-element.124.refs_3_.refs_1_), channel_id=1, source_target_pairs={{2,0},{4,2},{6,4},{0,6},{3,1},{5,3},{7,5},{1,7},{10,8},{12,10},{14... | collective-permute-start | bytes 1179656 | tf_op jit(solution)/shard_map/ppermute | solution.py:917
  92.1 34.8 %collective-permute-start.15 = (bf16[192,4096]{1,0:T(8,128)(2,1)}, bf16[192,4096]{1,0:T(8,128)(2,1)}, u32[]{:S(2)}, u32[]{:S(2)}) collective-permute-start(bf16[192,4096]{1,0:T(8,128)(2,1)} %get-tuple-element.156), channel_id=1, source_target_pairs={{0,1},{1,0},{2,3},{3,2},{4,5},{5,4},{6,7},{7,6},{8,9},{9,8},{10,11... | collective-permute-start | bytes 4718600 | tf_op jit(solution)/shard_map/ppermute | solution.py:908
  96.0 32.5 %collective-permute-start.13 = (bf16[1024,512]{1,0:T(8,128)(2,1)}, bf16[1024,512]{1,0:T(8,128)(2,1)}, u32[]{:S(2)}, u32[]{:S(2)}) collective-permute-start(bf16[1024,512]{1,0:T(8,128)(2,1)} %convolution_convert_fusion.3.refs_6_.refs_5_), channel_id=1, source_target_pairs={{0,16},{8,24},{16,0},{24,8},{1,17},{9,25},{17,1},{25,9},{2,18},{10... | collective-permute-start | bytes 3145736 | tf_op jit(solution)/shard_map/ppermute | solution.py:914
  99.3 29.3 %collective-permute-start.14 = (bf16[1024,512]{1,0:T(8,128)(2,1)}, bf16[1024,512]{1,0:T(8,128)(2,1)}, u32[]{:S(2)}, u32[]{:S(2)}) collective-permute-start(bf16[1024,512]{1,0:T(8,128)(2,1)} %convolution_convert_fusion.2.refs_5_.refs_4_), channel_id=1, source_target_pairs={{0,8},{8,0},{16,24},{24,16},{1,9},{9,1},{17,25},{25,17},{2,10},{10... | collective-permute-start | bytes 3145736 | tf_op jit(solution)/shard_map/ppermute | solution.py:911
  136.9 53.2 %collective-permute-start.19 = (bf16[768,3072]{1,0:T(8,128)(2,1)}, bf16[768,3072]{1,0:T(8,128)(2,1)}, u32[]{:S(2)}, u32[]{:S(2)}) collective-permute-start(bf16[768,3072]{1,0:T(8,128)(2,1)} %get-tuple-element.162), channel_id=1, source_target_pairs={{0,1},{1,0},{2,3},{3,2},{4,5},{5,4},{6,7},{7,6},{8,9},{9,8},{10,11... | collective-permute-start | bytes 14155784 | tf_op jit(solution)/shard_map/ppermute | solution.py:908
  136.9 48.9 %all-to-all-start = ((bf16[4,192,1024]{2,1,0:T(8,128)(2,1)}), bf16[4,192,1024]{2,1,0:T(8,128)(2,1)}, u32[]{:S(2)}, u32[]{:S(2)}) async-start(bf16[4,192,1024]{2,1,0:T(8,128)(2,1)} %get-tuple-element.158), calls=%async_computation | async-start | bytes 3145728 | tf_op jit(solution)/shard_map/all_to_all | solution.py:925
  149.5 44.1 %collective-permute-start.20 = (bf16[256,2048]{1,0:T(8,128)(2,1)}, bf16[256,2048]{1,0:T(8,128)(2,1)}, u32[]{:S(2)}, u32[]{:S(2)}) collective-permute-start(bf16[256,2048]{1,0:T(8,128)(2,1)} %convolution_convert_fusion), channel_id=1, source_target_pairs={{0,8},{8,0},{16,24},{24,16},{1,9},{9,1},{17,25},{25,17},{2,10},{10... | collective-permute-start | bytes 3145736 | tf_op jit(solution)/shard_map/ppermute | solution.py:911
  150.7 42.9 %collective-permute-start.16 = (bf16[256,2048]{1,0:T(8,128)(2,1)}, bf16[256,2048]{1,0:T(8,128)(2,1)}, u32[]{:S(2)}, u32[]{:S(2)}) collective-permute-start(bf16[256,2048]{1,0:T(8,128)(2,1)} %convolution_convert_fusion.1), channel_id=1, source_target_pairs={{0,16},{8,24},{16,0},{24,8},{1,17},{9,25},{17,1},{25,9},{2,18},{10... | collective-permute-start | bytes 3145736 | tf_op jit(solution)/shard_map/ppermute | solution.py:914
  185.8 37.8 %all-to-all-start.1 = ((bf16[4,128,1024]{2,1,0:T(8,128)(2,1)}), bf16[4,128,1024]{2,1,0:T(8,128)(2,1)}, u32[]{:S(2)}, u32[]{:S(2)}) async-start(bf16[4,128,1024]{2,1,0:T(8,128)(2,1)} %bitcast.53), calls=%async_computation.1 | async-start | bytes 2097152 | tf_op jit(solution)/shard_map/all_to_all | solution.py:925
  193.7 21.6 %collective-permute-start.24 = (bf16[192,1024]{1,0:T(8,128)(2,1)}, bf16[192,1024]{1,0:T(8,128)(2,1)S(1)}, u32[]{:S(2)}, u32[]{:S(2)}) collective-permute-start(bf16[192,1024]{1,0:T(8,128)(2,1)} %get-tuple-element.173), channel_id=1, source_target_pairs={{0,1},{1,0},{2,3},{3,2},{4,5},{5,4},{6,7},{7,6},{8,9},{9,8},{10,11... | collective-permute-start | bytes 1179656 | tf_op jit(solution)/shard_map/ppermute | solution.py:908
  215.9 27.3 %collective-permute-start.28 = (bf16[256,1536]{1,0:T(8,128)(2,1)}, bf16[256,1536]{1,0:T(8,128)(2,1)}, u32[]{:S(2)}, u32[]{:S(2)}) collective-permute-start(bf16[256,1536]{1,0:T(8,128)(2,1)} %fusion.4), channel_id=1, source_target_pairs={{0,16},{8,24},{16,0},{24,8},{1,17},{9,25},{17,1},{25,9},{2,18},{10... | collective-permute-start | bytes 2359304 | tf_op jit(solution)/shard_map/ppermute | solution.py:914
  217.4 25.8 %collective-permute-start.23 = (bf16[256,1536]{1,0:T(8,128)(2,1)}, bf16[256,1536]{1,0:T(8,128)(2,1)}, u32[]{:S(2)}, u32[]{:S(2)}) collective-permute-start(bf16[256,1536]{1,0:T(8,128)(2,1)} %fusion.3), channel_id=1, source_target_pairs={{0,8},{8,0},{16,24},{24,16},{1,9},{9,1},{17,25},{25,17},{2,10},{10... | collective-permute-start | bytes 2359304 | tf_op jit(solution)/shard_map/ppermute | solution.py:911
  223.7 35.2 %all-to-all-start.2 = ((bf16[4,32,4096]{2,1,0:T(8,128)(2,1)}), bf16[4,32,4096]{2,1,0:T(8,128)(2,1)S(1)}, u32[]{:S(2)}, u32[]{:S(2)}) async-start(bf16[4,32,4096]{2,1,0:T(8,128)(2,1)} %bitcast.52), calls=%async_computation.2 | async-start | bytes 2097152 | tf_op jit(solution)/shard_map/all_to_all | solution.py:925
  259.9 28.7 %all-to-all-start.3 = ((bf16[4,128,1024]{2,1,0:T(8,128)(2,1)}), bf16[4,128,1024]{2,1,0:T(8,128)(2,1)}, u32[]{:S(2)}, u32[]{:S(2)}) async-start(bf16[4,128,1024]{2,1,0:T(8,128)(2,1)} %fold.4), calls=%async_computation.3 | async-start | bytes 2097152 | tf_op jit(solution)/shard_map/all_to_all | solution.py:925
  288.5 29.6 %all-to-all-start.4 = ((bf16[4,32,4096]{2,1,0:T(8,128)(2,1)}), bf16[4,32,4096]{2,1,0:T(8,128)(2,1)}, u32[]{:S(2)}, u32[]{:S(2)}) async-start(bf16[4,32,4096]{2,1,0:T(8,128)(2,1)} %fold.5), calls=%async_computation.4 | async-start | bytes 2097152 | tf_op jit(solution)/shard_map/all_to_all | solution.py:925
  303.8 42.1 %collective-permute-start.35 = (bf16[512,1024]{1,0:T(8,128)(2,1)}, bf16[512,1024]{1,0:T(8,128)(2,1)}, u32[]{:S(2)}, u32[]{:S(2)}) collective-permute-start(bf16[512,1024]{1,0:T(8,128)(2,1)} %bitcast.16.refs_1_), channel_id=1, source_target_pairs={{0,16},{8,24},{16,0},{24,8},{1,17},{9,25},{17,1},{25,9},{2,18},{10... | collective-permute-start | bytes 3145736 | tf_op jit(solution)/shard_map/ppermute | solution.py:914
  305.3 40.6 %collective-permute-start.36 = (bf16[512,1024]{1,0:T(8,128)(2,1)}, bf16[512,1024]{1,0:T(8,128)(2,1)}, u32[]{:S(2)}, u32[]{:S(2)}) collective-permute-start(bf16[512,1024]{1,0:T(8,128)(2,1)} %bitcast.16.refs_1_), channel_id=1, source_target_pairs={{0,8},{8,0},{16,24},{24,16},{1,9},{9,1},{17,25},{25,17},{2,10},{10... | collective-permute-start | bytes 3145736 | tf_op jit(solution)/shard_map/ppermute | solution.py:911
  318.2 23.6 %all-to-all-start.5 = ((bf16[4,32,3072]{2,1,0:T(8,128)(2,1)}), bf16[4,32,3072]{2,1,0:T(8,128)(2,1)S(1)}, u32[]{:S(2)}, u32[]{:S(2)}) async-start(bf16[4,32,3072]{2,1,0:T(8,128)(2,1)} %bitcast.9.refs_7_), calls=%async_computation.5 | async-start | bytes 1572864 | tf_op jit(solution)/shard_map/all_to_all | solution.py:925
  321.7 30.0 %collective-permute-start.40 = (bf16[128,4096]{1,0:T(8,128)(2,1)}, bf16[128,4096]{1,0:T(8,128)(2,1)}, u32[]{:S(2)}, u32[]{:S(2)}) collective-permute-start(bf16[128,4096]{1,0:T(8,128)(2,1)} %bitcast.17.refs_1_), channel_id=1, source_target_pairs={{0,16},{8,24},{16,0},{24,8},{1,17},{9,25},{17,1},{25,9},{2,18},{10... | collective-permute-start | bytes 3145736 | tf_op jit(solution)/shard_map/ppermute | solution.py:914
  322.3 29.3 %collective-permute-start.39 = (bf16[128,4096]{1,0:T(8,128)(2,1)}, bf16[128,4096]{1,0:T(8,128)(2,1)}, u32[]{:S(2)}, u32[]{:S(2)}) collective-permute-start(bf16[128,4096]{1,0:T(8,128)(2,1)} %bitcast.17.refs_1_), channel_id=1, source_target_pairs={{0,8},{8,0},{16,24},{24,16},{1,9},{9,1},{17,25},{25,17},{2,10},{10... | collective-permute-start | bytes 3145736 | tf_op jit(solution)/shard_map/ppermute | solution.py:911
  351.7 23.7 %all-to-all-start.6 = ((bf16[4,32,3072]{2,1,0:T(8,128)(2,1)}), bf16[4,32,3072]{2,1,0:T(8,128)(2,1)S(1)}, u32[]{:S(2)}, u32[]{:S(2)}) async-start(bf16[4,32,3072]{2,1,0:T(8,128)(2,1)} %fold.6), calls=%async_computation.6 | async-start | bytes 1572864 | tf_op jit(solution)/shard_map/all_to_all | solution.py:925
  375.4 23.1 %all-to-all-start.7 = ((bf16[4,96,1024]{2,1,0:T(8,128)(2,1)}), bf16[4,96,1024]{2,1,0:T(8,128)(2,1)S(1)}, u32[]{:S(2)}, u32[]{:S(2)}) async-start(bf16[4,96,1024]{2,1,0:T(8,128)(2,1)} %fusion.24.refs_4_), calls=%async_computation.7 | async-start | bytes 1572864 | tf_op jit(solution)/shard_map/all_to_all | solution.py:925
  378.9 22.6 %collective-permute-start.42 = (bf16[128,3072]{1,0:T(8,128)(2,1)S(1)}, bf16[128,3072]{1,0:T(8,128)(2,1)S(1)}, u32[]{:S(2)}, u32[]{:S(2)}) collective-permute-start(bf16[128,3072]{1,0:T(8,128)(2,1)S(1)} %bitcast.55), channel_id=1, source_target_pairs={{0,8},{8,0},{16,24},{24,16},{1,9},{9,1},{17,25},{25,17},{2,10},{10... | collective-permute-start | bytes 2359304 | tf_op jit(solution)/shard_map/ppermute | solution.py:911
  379.8 21.8 %collective-permute-start.43 = (bf16[128,3072]{1,0:T(8,128)(2,1)S(1)}, bf16[128,3072]{1,0:T(8,128)(2,1)S(1)}, u32[]{:S(2)}, u32[]{:S(2)}) collective-permute-start(bf16[128,3072]{1,0:T(8,128)(2,1)S(1)} %bitcast.56), channel_id=1, source_target_pairs={{0,16},{8,24},{16,0},{24,8},{1,17},{9,25},{17,1},{25,9},{2,18},{10... | collective-permute-start | bytes 2359304 | tf_op jit(solution)/shard_map/ppermute | solution.py:914
  401.6 29.4 %all-to-all-start.8 = ((bf16[4,96,1024]{2,1,0:T(8,128)(2,1)}), bf16[4,96,1024]{2,1,0:T(8,128)(2,1)S(1)}, u32[]{:S(2)}, u32[]{:S(2)}) async-start(bf16[4,96,1024]{2,1,0:T(8,128)(2,1)} %fold.7), calls=%async_computation.8 | async-start | bytes 1572864 | tf_op jit(solution)/shard_map/all_to_all | solution.py:925
  409.7 24.1 %collective-permute-start.48 = (bf16[128,1536]{1,0:T(8,128)(2,1)}, bf16[128,1536]{1,0:T(8,128)(2,1)}, u32[]{:S(2)}, u32[]{:S(2)}) collective-permute-start(bf16[128,1536]{1,0:T(8,128)(2,1)} %slice.381), channel_id=1, source_target_pairs={{0,8},{8,0},{16,24},{24,16},{1,9},{9,1},{17,25},{25,17},{2,10},{10... | collective-permute-start | bytes 1179656 | tf_op jit(solution)/shard_map/ppermute | solution.py:911
  410.9 22.9 %collective-permute-start.49 = (bf16[128,1536]{1,0:T(8,128)(2,1)}, bf16[128,1536]{1,0:T(8,128)(2,1)}, u32[]{:S(2)}, u32[]{:S(2)}) collective-permute-start(bf16[128,1536]{1,0:T(8,128)(2,1)} %slice.382), channel_id=1, source_target_pairs={{0,16},{8,24},{16,0},{24,8},{1,17},{9,25},{17,1},{25,9},{2,18},{10... | collective-permute-start | bytes 1179656 | tf_op jit(solution)/shard_map/ppermute | solution.py:914
  430.9 22.1 %collective-permute-start.46 = (bf16[384,1024]{1,0:T(8,128)(2,1)S(1)}, bf16[384,1024]{1,0:T(8,128)(2,1)S(1)}, u32[]{:S(2)}, u32[]{:S(2)}) collective-permute-start(bf16[384,1024]{1,0:T(8,128)(2,1)S(1)} %bitcast.37), channel_id=1, source_target_pairs={{0,8},{8,0},{16,24},{24,16},{1,9},{9,1},{17,25},{25,17},{2,10},{10... | collective-permute-start | bytes 2359304 | tf_op jit(solution)/shard_map/ppermute | solution.py:911
  434.7 22.6 %all-to-all-start.9 = ((f32[16,1,5632]{2,1,0:T(1,128)}), f32[16,1,5632]{2,1,0:T(1,128)S(1)}, u32[]{:S(2)}, u32[]{:S(2)}) async-start(f32[16,1,5632]{2,1,0:T(1,128)} %broadcast_in_dim.9), calls=%async_computation.9 | async-start | bytes 720896 | tf_op jit(solution)/shard_map/all_to_all | solution.py:1194
  (75 other events, 661.1 us)
